TPU v7x, 32 devices: a whole 2x2x4 slice. The times are simulated.
32 devices in a mesh: grp: 2 (over core), shard: 16 (over z, y, x).
Axes of the slice: x: 2, y: 2, z: 4, core: 2. Of those that a mesh axis runs over, the one named last changes fastest.
Arguments:
- tokens: bfloat16 [2, 4, 1024, 1536], P(None, 'grp', 'shard'), may hold values from -6 to 6
- lengths: int32 [2, 2, 2], P(None, 'grp'), may hold values from 1 to 1536, 2048 in all within a row
- piece_order: int32 [2, 2, 2], P(None, 'grp'), may hold values from 0 to 1, as said below
- predecessor: int32 [2, 2, 2], P(None, 'grp'), may hold values from -1 to 1, as said below
- gain_one: bfloat16 [1536], P('shard'), may hold values from 0.099609375 to 1.8984375
- query_weight: bfloat16 [1536, 1536], P('shard'), may hold values from -0.21875 to 0.21875
- keyval_weight: bfloat16 [1536, 256], P('shard'), may hold values from -0.21875 to 0.21875
- outproj_weight: bfloat16 [1536, 1536], P('shard'), may hold values from -0.875 to 0.875
- gain_two: bfloat16 [1536], P('shard'), may hold values from 0.099609375 to 1.8984375
- gate_weight: bfloat16 [1536, 4608], P('shard'), may hold values from -0.15625 to 0.15625
- up_weight: bfloat16 [1536, 4608], P('shard'), may hold values from -0.15625 to 0.15625
- down_weight: bfloat16 [4608, 1536], P('shard'), may hold values from -0.1875 to 0.1875
- cotangent: bfloat16 [2, 4, 1024, 1536], P(None, 'grp', 'shard'), may hold values from -6 to 6
Outputs:
- block_output: bfloat16 [2, 4, 1024, 1536], P(None, 'grp', 'shard')
- input_grad: bfloat16 [2, 4, 1024, 1536], P(None, 'grp', 'shard')
- gain_one_grad: float32 [1536], P('shard')
- query_weight_grad: float32 [1536, 1536], P('shard')
- keyval_weight_grad: float32 [1536, 256], P('shard')
- outproj_weight_grad: float32 [1536, 1536], P('shard')
- gain_two_grad: float32 [1536], P('shard')
- gate_weight_grad: float32 [1536, 4608], P('shard')
- up_weight_grad: float32 [1536, 4608], P('shard')
- down_weight_grad: float32 [4608, 1536], P('shard')
Inputs may be any that keep to these rules, and one draw needn't show every extreme that they name: In each stream the 2 lengths sum to 2048 and the largest is at most 1536. In each stream piece_order is a permutation of the 2 pieces. predecessor[m, g, j] is the slot that holds piece piece_order[m, g, j] - 1, and -1 where piece_order[m, g, j] is 0.
All inputs are finite; a program needn't handle non-finite values.
Results may differ from a plain program's by a relative error of at most 0.018.
Values may be sent and summed in bfloat16 or wider, within the bound.
No kernel may reach another device: no remote copies, remote signals or barrier semaphores. Data moves between devices by JAX's collectives and lax.ppermute only.
A program may use at most 256 MiB of HBM per device.

v0:
```python
import math

import jax
import jax.numpy as jnp
from jax import lax
from jax.sharding import PartitionSpec as P

epsilon = 1e-06
masked_out = -1e30


def as_sent(shard):

    def short(part):
        return part.astype(jnp.bfloat16) if part.dtype == jnp.float32 else part

    return jax.tree.map(short, shard)


def rms_factor(values):
    return lax.rsqrt(jnp.mean(values * values, axis=-1, keepdims=True) + epsilon)


def product(first_op, second_op):
    return jnp.dot(first_op, second_op, preferred_element_type=jnp.float32)


def product_tn(first_op, second_op):
    return lax.dot_general(
        first_op, second_op, (((0,), (0,)), ((), ())), preferred_element_type=jnp.float32
    )


def product_nt(first_op, second_op):
    return lax.dot_general(
        first_op, second_op, (((1,), (1,)), ((), ())), preferred_element_type=jnp.float32
    )


def norm_backward(values, factor, gain, upstream):
    inner_mean = jnp.mean(gain * upstream * values, axis=-1, keepdims=True)
    return factor * gain * upstream - values * factor * factor * factor * inner_mean


def segment_of(positions, seq_ends):
    return jnp.sum((positions[:, None] >= seq_ends[None, :]).astype(jnp.int32), axis=1)


def to_holders(local_rows, slot_piece, pieces, quarters):
    feat_width = local_rows.shape[-1]
    split_rows = local_rows.reshape(pieces, -1, quarters, feat_width)
    picked = jnp.take(split_rows, slot_piece, axis=0)
    return jnp.transpose(picked, (0, 2, 1, 3)).reshape(-1, feat_width)


def from_holders(received, inverse, pieces, quarters):
    feat_width = received.shape[-1]
    split_rows = received.reshape(pieces, quarters, -1, feat_width)
    placed = jnp.transpose(split_rows, (0, 2, 1, 3))
    return jnp.take(placed, inverse, axis=0).reshape(-1, feat_width)


def attend_forward(query_groups, key_part, value_part, allowed, score_scale):

    def one_group(query_block):
        scores = (
            jnp.einsum("grh,uh->gru", query_block, key_part, preferred_element_type=jnp.float32)
            * score_scale
        )
        scores = jnp.where(allowed[None], scores, masked_out)
        top_score = jnp.max(scores, axis=-1, keepdims=True)
        exp_scores = jnp.exp(scores - top_score)
        totals = jnp.sum(exp_scores, axis=-1, keepdims=True)
        attn_prob = (exp_scores / totals).astype(jnp.bfloat16)
        mixed_rows = jnp.einsum(
            "gru,uh->grh", attn_prob, value_part, preferred_element_type=jnp.float32
        )
        return (mixed_rows.astype(jnp.bfloat16), top_score[..., 0] + jnp.log(totals[..., 0]))

    return lax.map(one_group, query_groups)


def attend_backward(query_groups, grad_groups, logsum, key_part, value_part, allowed, score_scale):

    def one_group(running, blocks):
        query_block, grad_block, logsum_block = blocks
        scores = (
            jnp.einsum("grh,uh->gru", query_block, key_part, preferred_element_type=jnp.float32)
            * score_scale
        )
        attn_prob = jnp.where(allowed[None], jnp.exp(scores - logsum_block[..., None]), 0.0)
        grad_prob = jnp.einsum(
            "grh,uh->gru", grad_block, value_part, preferred_element_type=jnp.float32
        )
        row_delta = jnp.sum(attn_prob * grad_prob, axis=-1, keepdims=True)
        grad_scores = (attn_prob * (grad_prob - row_delta)).astype(jnp.bfloat16)
        grad_query = (
            jnp.einsum("gru,uh->grh", grad_scores, key_part, preferred_element_type=jnp.float32)
            * score_scale
        ).astype(jnp.bfloat16)
        grad_keys = (
            running[0]
            + jnp.einsum(
                "gru,grh->uh", grad_scores, query_block, preferred_element_type=jnp.float32
            )
            * score_scale
        )
        grad_values = running[1] + jnp.einsum(
            "gru,grh->uh",
            attn_prob.astype(jnp.bfloat16),
            grad_block,
            preferred_element_type=jnp.float32,
        )
        return ((grad_keys, grad_values), grad_query)

    initial = (jnp.zeros(key_part.shape, jnp.float32), jnp.zeros(value_part.shape, jnp.float32))
    return lax.scan(one_group, initial, (query_groups, grad_groups, logsum))


def on_device(
    tokens,
    lengths,
    piece_order,
    predecessor,
    gain_one,
    query_weight,
    keyval_weight,
    outproj_weight,
    gain_two,
    gate_weight,
    up_weight,
    down_weight,
    cotangent,
):
    shard_count = lax.axis_size("shard")
    micro_count, piece_count, sub_rows, feat_width = tokens.shape
    window = sub_rows * shard_count
    local_rows = piece_count * sub_rows
    quarters = window // local_rows
    head_size = keyval_weight.shape[1] // 2
    head_count = query_weight.shape[1] // head_size
    group_heads = max(
        (
            divisor
            for divisor in range(1, head_count + 1)
            if head_count % divisor == 0 and divisor * local_rows <= max(512, local_rows)
        )
    )
    group_count = head_count // group_heads
    score_scale = 1.0 / math.sqrt(head_size)
    my_index = lax.axis_index("shard")
    my_slot = my_index // quarters
    my_quarter = my_index % quarters
    piece_index = jnp.arange(piece_count, dtype=jnp.int32)
    offsets = jnp.arange(window, dtype=jnp.int32)
    shards = (
        gain_one,
        query_weight,
        keyval_weight,
        outproj_weight,
        gain_two,
        gate_weight,
        up_weight,
        down_weight,
    )
    outputs = []
    in_grads = []
    grad_totals = None
    for micro_step in range(micro_count):
        gathered = (
            lax.all_gather(shards[0], "shard", axis=0, tiled=True),
            lax.all_gather(shards[1], "shard", axis=0, tiled=True),
            lax.all_gather(shards[2], "shard", axis=0, tiled=True),
            lax.all_gather(shards[3], "shard", axis=0, tiled=True),
            lax.all_gather(shards[4], "shard", axis=0, tiled=True),
            lax.all_gather(shards[5], "shard", axis=0, tiled=True),
            lax.all_gather(shards[6], "shard", axis=0, tiled=True),
            lax.all_gather(shards[7], "shard", axis=0, tiled=True),
        )
        (
            full_gain_one,
            full_query,
            full_keyval,
            full_outproj,
            full_gain_two,
            full_gate,
            full_up,
            full_down,
        ) = gathered
        slot_piece = piece_order[micro_step, 0]
        before = predecessor[micro_step, 0]
        seq_ends = jnp.cumsum(lengths[micro_step, 0])
        inverse = jnp.sum(
            jnp.where(slot_piece[None, :] == piece_index[:, None], piece_index[None, :], 0), axis=1
        )
        dest_slot = jnp.arange(shard_count, dtype=jnp.int32) // quarters
        dest_own = slot_piece[dest_slot]
        dest_has = before[dest_slot] >= 0
        dest_prev = slot_piece[jnp.maximum(before[dest_slot], 0)]
        stream = tokens[micro_step].reshape(local_rows, feat_width).astype(jnp.float32)
        factor_one = rms_factor(stream)
        normed_one = (stream * factor_one * full_gain_one).astype(jnp.bfloat16)
        queries = product(normed_one, full_query).astype(jnp.bfloat16)
        keyvals = (
            product(normed_one, full_keyval).astype(jnp.bfloat16).reshape(piece_count, sub_rows, -1)
        )
        query_send = to_holders(queries, slot_piece, piece_count, quarters)[None]
        keyval_send = jnp.stack(
            [jnp.take(keyvals, dest_own, axis=0), jnp.take(keyvals, dest_prev, axis=0)]
        ).reshape(2, window, -1)
        query_recv, keyval_recv = (
            lax.all_to_all(query_send, "shard", split_axis=1, concat_axis=1, tiled=True),
            lax.all_to_all(keyval_send, "shard", split_axis=1, concat_axis=1, tiled=True),
        )
        own_piece = slot_piece[my_slot]
        has_before = before[my_slot] >= 0
        prev_piece = slot_piece[jnp.maximum(before[my_slot], 0)]
        key_rows = keyval_recv.reshape(2 * window, -1)
        key_part = key_rows[:, :head_size]
        value_part = key_rows[:, head_size:]
        query_pos = (
            own_piece * window + quarters * jnp.arange(local_rows, dtype=jnp.int32) + my_quarter
        )
        key_pos = jnp.concatenate([own_piece * window + offsets, prev_piece * window + offsets])
        key_live = jnp.concatenate(
            [jnp.ones((window,), dtype=bool), jnp.broadcast_to(has_before, (window,))]
        )
        distance = query_pos[:, None] - key_pos[None, :]
        same_seq = (
            segment_of(query_pos, seq_ends)[:, None] == segment_of(key_pos, seq_ends)[None, :]
        )
        allowed = same_seq & (distance >= 0) & (distance < window) & key_live[None, :]
        query_groups = jnp.transpose(
            query_recv[0].reshape(local_rows, group_count, group_heads, head_size), (1, 2, 0, 3)
        )
        mixed_groups, logsum = attend_forward(
            query_groups, key_part, value_part, allowed, score_scale
        )
        mixed_send = jnp.transpose(mixed_groups, (2, 0, 1, 3)).reshape(local_rows, -1)
        mixed_back = lax.all_to_all(mixed_send, "shard", split_axis=0, concat_axis=0, tiled=True)
        mixed_rows = from_holders(mixed_back, inverse, piece_count, quarters)
        residual = stream + product(mixed_rows, full_outproj)
        factor_two = rms_factor(residual)
        normed_two = (residual * factor_two * full_gain_two).astype(jnp.bfloat16)
        gate_pre = product(normed_two, full_gate)
        upward = product(normed_two, full_up)
        active, gelu_pull = jax.vjp(jax.nn.gelu, gate_pre)
        hidden = (active * upward).astype(jnp.bfloat16)
        result = residual + product(hidden, full_down)
        outputs.append(result.astype(jnp.bfloat16).reshape(piece_count, sub_rows, feat_width))
        upstream = cotangent[micro_step].reshape(local_rows, feat_width)
        grad_down = product_tn(hidden, upstream)
        grad_hidden = product_nt(upstream, full_down)
        grad_gate_in = gelu_pull(grad_hidden * upward)[0].astype(jnp.bfloat16)
        grad_up_in = (grad_hidden * active).astype(jnp.bfloat16)
        grad_gate = product_tn(normed_two, grad_gate_in)
        grad_up = product_tn(normed_two, grad_up_in)
        grad_normed_two = product_nt(grad_gate_in, full_gate) + product_nt(grad_up_in, full_up)
        grad_gain_two = jnp.sum(grad_normed_two * residual * factor_two, axis=0)
        grad_resid = upstream.astype(jnp.float32) + norm_backward(
            residual, factor_two, full_gain_two, grad_normed_two
        )
        grad_attn = grad_resid.astype(jnp.bfloat16)
        grad_outproj = product_tn(mixed_rows, grad_attn)
        grad_mixed = product_nt(grad_attn, full_outproj).astype(jnp.bfloat16)
        grad_send = to_holders(grad_mixed, slot_piece, piece_count, quarters)
        grad_recv = lax.all_to_all(grad_send, "shard", split_axis=0, concat_axis=0, tiled=True)
        grad_groups = jnp.transpose(
            grad_recv.reshape(local_rows, group_count, group_heads, head_size), (1, 2, 0, 3)
        )
        key_val_grads, grad_query_groups = attend_backward(
            query_groups, grad_groups, logsum, key_part, value_part, allowed, score_scale
        )
        grad_query_send = jnp.transpose(grad_query_groups, (2, 0, 1, 3)).reshape(local_rows, -1)
        query_back = lax.all_to_all(
            grad_query_send, "shard", split_axis=0, concat_axis=0, tiled=True
        )
        grad_queries = from_holders(query_back, inverse, piece_count, quarters)
        keyval_partial = jnp.concatenate([key_val_grads[0], key_val_grads[1]], axis=1).reshape(
            2, window, -1
        )
        keyval_back = (
            lax.all_to_all(
                keyval_partial.astype(jnp.bfloat16),
                "shard",
                split_axis=1,
                concat_axis=1,
                tiled=True,
            )
            .astype(keyval_partial.dtype)
            .reshape(2, shard_count, -1)
        )
        own_hits = (dest_own[None, :] == piece_index[:, None]).astype(jnp.float32)
        prev_hits = ((dest_prev[None, :] == piece_index[:, None]) & dest_has[None, :]).astype(
            jnp.float32
        )
        summed = jnp.dot(own_hits, keyval_back[0], precision=lax.Precision.HIGHEST) + jnp.dot(
            prev_hits, keyval_back[1], precision=lax.Precision.HIGHEST
        )
        grad_keyvals = summed.reshape(local_rows, -1).astype(jnp.bfloat16)
        grad_query_w = product_tn(normed_one, grad_queries)
        grad_keyval_w = product_tn(normed_one, grad_keyvals)
        grad_normed_one = product_nt(grad_queries, full_query) + product_nt(
            grad_keyvals, full_keyval
        )
        grad_gain_one = jnp.sum(grad_normed_one * stream * factor_one, axis=0)
        grad_stream = grad_resid + norm_backward(stream, factor_one, full_gain_one, grad_normed_one)
        in_grads.append(grad_stream.astype(jnp.bfloat16).reshape(piece_count, sub_rows, feat_width))
        micro_grads = (
            grad_gain_one,
            grad_query_w,
            grad_keyval_w,
            grad_outproj,
            grad_gain_two,
            grad_gate,
            grad_up,
            grad_down,
        )
        shares = (
            lax.psum_scatter(micro_grads[0], "shard", scatter_dimension=0, tiled=True),
            lax.psum_scatter(micro_grads[1], "shard", scatter_dimension=0, tiled=True),
            lax.psum_scatter(micro_grads[2], "shard", scatter_dimension=0, tiled=True),
            lax.psum_scatter(micro_grads[3], "shard", scatter_dimension=0, tiled=True),
            lax.psum_scatter(micro_grads[4], "shard", scatter_dimension=0, tiled=True),
            lax.psum_scatter(micro_grads[5], "shard", scatter_dimension=0, tiled=True),
            lax.psum_scatter(micro_grads[6], "shard", scatter_dimension=0, tiled=True),
            lax.psum_scatter(micro_grads[7], "shard", scatter_dimension=0, tiled=True),
        )
        grad_totals = shares if grad_totals is None else jax.tree.map(jnp.add, grad_totals, shares)
    finals = jax.tree.map(
        lambda part: part.astype(jnp.float32), lax.psum(as_sent(grad_totals), "grp")
    )
    return (
        jnp.stack(outputs),
        jnp.stack(in_grads),
        finals[0],
        finals[1],
        finals[2],
        finals[3],
        finals[4],
        finals[5],
        finals[6],
        finals[7],
    )


def solution(mesh):
    in_specs = (
        P(None, "grp", "shard", None),
        P(None, "grp", None),
        P(None, "grp", None),
        P(None, "grp", None),
        P("shard"),
        P("shard", None),
        P("shard", None),
        P("shard", None),
        P("shard"),
        P("shard", None),
        P("shard", None),
        P("shard", None),
        P(None, "grp", "shard", None),
    )
    out_specs = (
        P(None, "grp", "shard", None),
        P(None, "grp", "shard", None),
        P("shard"),
        P("shard", None),
        P("shard", None),
        P("shard", None),
        P("shard"),
        P("shard", None),
        P("shard", None),
        P("shard", None),
    )
    return jax.shard_map(
        on_device, mesh=mesh, in_specs=in_specs, out_specs=out_specs, check_vma=False
    )
```

profile of v0, /device:TPU:0, one launch (start us, length us, event | category | flops | bytes accessed | tf_op | source)
XLA Modules:
  0.0 2619.2 jit_solution(17179378077230914266)
XLA Ops:
  14.3 44.6 %all-reduce.7 = (bf16[1536]{0:T(1024)(128)(2,1)S(1)}, bf16[1536]{0:T(1024)(128)(2,1)S(1)}) all-reduce(bf16[1536]{0:T(1024)(128)(2,1)S(1)} %dynamic-update-slice, bf16[1536]{0:T(1024)(128)(2,1)S(1)} %dynamic-update-slice.1), channel_id=1, replica_groups=mesh['grp'=2,'shard'=16] {'shard'}, use_global_device_ids=true, to_apply=%add.2 | all-reduce | flops 3072 | bytes 12288
  60.5 46.3 %all_gather.34 = bf16[1536,256]{1,0:T(8,128)(2,1)S(1)} all-gather(bf16[96,256]{1,0:T(8,128)(2,1)} %param.31), channel_id=1, replica_groups=mesh['grp'=2,'shard'=16] {'shard'}, dimensions={0}, use_global_device_ids=true | all-gather | bytes 835584 | tf_op jit(solution)/shard_map/all_gather | solution.py:173
  135.5 15.9 all-to-all-done.4
  151.4 15.1 all-to-all-start.1
  178.2 22.2 all-to-all-done.1
  217.2 14.7 all-to-all-start.3
  260.5 19.9 while.57
  296.2 15.8 while.56
  347.5 50.3 %all-gather.10.cloned.1.call-done = bf16[1536,4608]{1,0:T(8,128)(2,1)} async-done(((bf16[96,4608]{1,0:T(8,128)(2,1)}), bf16[1536,4608]{1,0:T(8,128)(2,1)}) %all-gather.10.cloned.1.call-update) | async-done | bytes 14155792 | tf_op jit(solution)/shard_map/all_gather | solution.py:176
  406.3 159.8 %all-gather.12.cloned.1.call-done = bf16[1536,4608]{1,0:T(8,128)(2,1)} async-done(((bf16[96,4608]{1,0:T(8,128)(2,1)}), bf16[1536,4608]{1,0:T(8,128)(2,1)}) %all-gather.12.cloned.1.call-update) | async-done | bytes 14155792 | tf_op jit(solution)/shard_map/all_gather | solution.py:177
  574.5 159.3 %all-gather.14.cloned.1.call-done = bf16[4608,1536]{1,0:T(8,128)(2,1)} async-done(((bf16[288,1536]{1,0:T(8,128)(2,1)}), bf16[4608,1536]{1,0:T(8,128)(2,1)}) %all-gather.14.cloned.1.call-update) | async-done | bytes 14155792 | tf_op jit(solution)/shard_map/all_gather | solution.py:178
  860.4 46.1 %while.59 = (s32[]{:T(128)}, f32[2048,128]{1,0:T(8,128)}, f32[2048,128]{1,0:T(8,128)}, bf16[3,4,128,128]{3,2,1,0:T(8,128)(2,1)}, bf16[3,4,128,128]{3,2,1,0:T(8,1...) while((s32[]{:T(128)}, f32[2048,128]{1,0:T(8,128)}, ...), condition=%wide.region_28.31_spmd.clone, body=%wide.region_26.30_spmd.clone.sunk | while | flops 1354890752 | bytes 72250616 | solution.py:117
  918.4 46.3 %while.58 = (s32[]{:T(128)}, f32[2048,128]{1,0:T(8,128)}, f32[2048,128]{1,0:T(8,128)}, bf16[3,4,128,128]{3,2,1,0:T(8,128)(2,1)}, bf16[3,4,128,128]{3,2,1,0:T(8,1...) while((s32[]{:T(128)}, f32[2048,128]{1,0:T(8,128)}, ...), condition=%wide.region_23.26_spmd.clone, body=%wide.region_21.25_spmd.clone.sunk | while | flops 1354890752 | bytes 72295784 | solution.py:117
  1012.7 18.9 convolution_add_fusion.1
  1044.4 18.7 convolution_add_fusion
  1076.1 19.3 convolution_add_fusion.2
  1110.9 21.5 all-to-all-done.11
  1188.3 49.3 %reduce-scatter.7.cloned.1.call-done = f32[96,1536]{1,0:T(8,128)} async-done(((f32[1536,1536]{1,0:T(8,128)}), f32[96,1536]{1,0:T(8,128)}) %reduce-scatter.7.cloned.1.call-update) | async-done | bytes 589840 | tf_op jit(solution)/shard_map/reduce_scatter | solution.py:321
  1239.4 401.4 %reduce-scatter.13.cloned.1.call-done = f32[96,4608]{1,0:T(8,128)} async-done(((f32[1536,4608]{1,0:T(8,128)}), f32[96,4608]{1,0:T(8,128)}) %reduce-scatter.13.cloned.1.call-update) | async-done | bytes 1769488 | tf_op jit(solution)/shard_map/reduce_scatter | solution.py:325
  1643.2 401.1 %reduce-scatter.15.cloned.1.call-done = f32[96,4608]{1,0:T(8,128)} async-done(((f32[1536,4608]{1,0:T(8,128)}), f32[96,4608]{1,0:T(8,128)}) %reduce-scatter.15.cloned.1.call-update) | async-done | bytes 1769488 | tf_op jit(solution)/shard_map/reduce_scatter | solution.py:326
  2046.7 400.9 %reduce-scatter.17.cloned.1.call-done = f32[288,1536]{1,0:T(8,128)} async-done(((f32[4608,1536]{1,0:T(8,128)}), f32[288,1536]{1,0:T(8,128)}) %reduce-scatter.17.cloned.1.call-update) | async-done | bytes 1769488 | tf_op jit(solution)/shard_map/reduce_scatter | solution.py:327
  2463.9 75.0 %all-reduce.6 = (bf16[1536]{0:T(1024)(128)(2,1)S(1)}, bf16[1536]{0:T(1024)(128)(2,1)S(1)}) all-reduce(f32[1536]{0:T(1024)S(1)} %add.386, f32[1536]{0:T(1024)S(1)} %add.390), channel_id=10, replica_groups=mesh['grp'=2,'shard'=16] {'shard'}, use_global_device_ids=true, to_apply=%region_31.34.clone | all-reduce | flops 3072 | bytes 18432
  2541.9 34.7 %reduce-scatter.9.cloned.1.call-done = f32[96,256]{1,0:T(8,128)} async-done(((f32[1536,256]{1,0:T(8,128)}), f32[96,256]{1,0:T(8,128)}) %reduce-scatter.9.cloned.1.call-update) | async-done | bytes 98320 | tf_op jit(solution)/shard_map/reduce_scatter | solution.py:322
  2582.8 20.2 all-reduce.12.cloned.1.call-done
  (594 shorter events, 608.3 us)
Async XLA Ops:
  7.2 196.8 %all-gather.6.cloned.1.call-start = ((), (), s32[]{:S(2)}) async-start(), calls=%async_computation.18 | async-start | bytes 5013504 | tf_op jit(solution)/shard_map/all_gather | solution.py:172
  7.9 333.1 %all-gather.8.cloned.1.call-start = ((), (), s32[]{:S(2)}) async-start(), calls=%async_computation.19 | async-start | bytes 5013504 | tf_op jit(solution)/shard_map/all_gather | solution.py:174
  8.7 389.1 %all-gather.10.cloned.1.call-start = ((), (), s32[]{:S(2)}) async-start(), calls=%async_computation.20 | async-start | bytes 15040512 | tf_op jit(solution)/shard_map/all_gather | solution.py:176
  9.4 556.6 %all-gather.12.cloned.1.call-start = ((), (), s32[]{:S(2)}) async-start(), calls=%async_computation.21 | async-start | bytes 15040512 | tf_op jit(solution)/shard_map/all_gather | solution.py:177
  10.0 723.8 %all-gather.14.cloned.1.call-start = ((), (), s32[]{:S(2)}) async-start(), calls=%async_computation.22 | async-start | bytes 15040512 | tf_op jit(solution)/shard_map/all_gather | solution.py:178
  116.4 34.9 %all-to-all-start.4 = ((bf16[2,1024,256]{2,0,1:T(2,128)(2,1)}), bf16[2,1024,256]{2,0,1:T(2,128)(2,1)S(1)}, u32[]{:S(2)}, u32[]{:S(2)}) async-start(bf16[2,1024,256]{2,0,1:T(2,128)(2,1)} %copy.140), calls=%async_computation.4 | async-start | bytes 2097152 | tf_op jit(solution)/shard_map/all_to_all | solution.py:213
  151.4 49.1 %all-to-all-start.1 = ((bf16[2,1024,256]{2,0,1:T(2,128)(2,1)}), bf16[2,1024,256]{2,0,1:T(2,128)(2,1)}, u32[]{:S(2)}, u32[]{:S(2)}) async-start(bf16[2,1024,256]{2,0,1:T(2,128)(2,1)} %copy.132), calls=%async_computation.1 | async-start | bytes 2097152 | tf_op jit(solution)/shard_map/all_to_all | solution.py:213
  217.2 30.5 %all-to-all-start.3 = ((bf16[16,2,6144]{2,1,0:T(2,128)(2,1)}), bf16[16,2,6144]{2,1,0:T(2,128)(2,1)}, u32[]{:S(2)}, u32[]{:S(2)}) async-start(bf16[16,2,6144]{2,1,0:T(2,128)(2,1)} %reshape.791), calls=%async_computation.3 | async-start | bytes 786432 | tf_op jit(solution)/shard_map/all_to_all | solution.py:212
  247.8 34.5 %all-to-all-start = ((bf16[16,2,6144]{2,1,0:T(2,128)(2,1)}), bf16[16,2,6144]{2,1,0:T(2,128)(2,1)S(1)}, u32[]{:S(2)}, u32[]{:S(2)}) async-start(bf16[16,2,6144]{2,1,0:T(2,128)(2,1)} %reshape.793), calls=%async_computation | async-start | bytes 786432 | tf_op jit(solution)/shard_map/all_to_all | solution.py:212
  283.0 32.1 %all-to-all-start.5 = ((bf16[16,8,1536]{2,1,0:T(8,128)(2,1)}), bf16[16,8,1536]{2,1,0:T(8,128)(2,1)S(1)}, u32[]{:S(2)}, u32[]{:S(2)}) async-start(bf16[16,8,1536]{2,1,0:T(8,128)(2,1)} %all_to_all.60), calls=%async_computation.5 | async-start | bytes 786432 | tf_op jit(solution)/shard_map/all_to_all | solution.py:240
  315.1 22.8 all-to-all-start.2
  826.9 23.7 all-to-all-start.9
  831.1 355.4 %reduce-scatter.11.cloned.1.call-start = ((), (), s32[]{:S(2)}) async-start(), calls=%async_computation.25 | async-start | bytes 10027008 | tf_op jit(solution)/shard_map/reduce_scatter | solution.py:323
  850.6 58.0 %all-to-all-start.6 = ((bf16[16,8,1536]{2,1,0:T(8,128)(2,1)}), bf16[16,8,1536]{2,1,0:T(8,128)(2,1)}, u32[]{:S(2)}, u32[]{:S(2)}) async-start(bf16[16,8,1536]{2,1,0:T(8,128)(2,1)} %bitcast.61), calls=%async_computation.6 | async-start | bytes 786432 | tf_op jit(solution)/shard_map/all_to_all | solution.py:267
  908.7 58.3 %all-to-all-start.10 = ((bf16[16,8,1536]{2,1,0:T(8,128)(2,1)}), bf16[16,8,1536]{2,1,0:T(8,128)(2,1)}, u32[]{:S(2)}, u32[]{:S(2)}) async-start(bf16[16,8,1536]{2,1,0:T(8,128)(2,1)} %all_to_all.69), calls=%async_computation.10 | async-start | bytes 786432 | tf_op jit(solution)/shard_map/all_to_all | solution.py:275
  967.0 24.9 all-to-all-start.7
  973.9 263.6 %reduce-scatter.7.cloned.1.call-start = ((), (), s32[]{:S(2)}) async-start(), calls=%async_computation.23 | async-start | bytes 10027008 | tf_op jit(solution)/shard_map/reduce_scatter | solution.py:321
  999.5 641.2 %reduce-scatter.13.cloned.1.call-start = ((), (), s32[]{:S(2)}) async-start(), calls=%async_computation.26 | async-start | bytes 30081024 | tf_op jit(solution)/shard_map/reduce_scatter | solution.py:325
  1031.6 1012.6 %reduce-scatter.15.cloned.1.call-start = ((), (), s32[]{:S(2)}) async-start(), calls=%async_computation.27 | async-start | bytes 30081024 | tf_op jit(solution)/shard_map/reduce_scatter | solution.py:326
  1063.1 1384.6 %reduce-scatter.17.cloned.1.call-start = ((), (), s32[]{:S(2)}) async-start(), calls=%async_computation.28 | async-start | bytes 30081024 | tf_op jit(solution)/shard_map/reduce_scatter | solution.py:327
  1099.3 33.1 %all-to-all-start.11 = ((bf16[2,1024,256]{2,0,1:T(2,128)(2,1)}), bf16[2,1024,256]{2,0,1:T(2,128)(2,1)}, u32[]{:S(2)}, u32[]{:S(2)}) async-start(bf16[2,1024,256]{2,0,1:T(2,128)(2,1)} %copy.156), calls=%async_computation.11 | async-start | bytes 2097152 | tf_op jit(solution)/shard_map/all_to_all | solution.py:283
  1132.4 29.7 %all-to-all-start.8 = ((bf16[2,1024,256]{2,0,1:T(2,128)(2,1)}), bf16[2,1024,256]{2,0,1:T(2,128)(2,1)S(1)}, u32[]{:S(2)}, u32[]{:S(2)}) async-start(bf16[2,1024,256]{2,0,1:T(2,128)(2,1)} %copy.150), calls=%async_computation.8 | async-start | bytes 2097152 | tf_op jit(solution)/shard_map/all_to_all | solution.py:283
  1139.4 1437.3 %reduce-scatter.9.cloned.1.call-start = ((), (), s32[]{:S(2)}) async-start(), calls=%async_computation.24 | async-start | bytes 1671168 | tf_op jit(solution)/shard_map/reduce_scatter | solution.py:322
  1177.8 1425.2 %all-reduce.12.cloned.1.call-start = ((), (), s32[]{:S(2)}) async-start(), calls=%async_computation.29 | async-start | bytes 6488064 | tf_op jit(solution)/shard_map/psum | solution.py:331
  (123 other events, 4522.7 us)
Sparse Core Ops, SparseCore 0:
  10.8 92.8 all-gather.5
  106.6 105.2 all-gather.7
  214.7 183.1 all-gather.9
  400.5 165.4 all-gather.11
  568.7 165.0 all-gather.13
  850.7 192.6 reduce-scatter.10
  1050.1 187.3 reduce-scatter.6
  1243.3 397.3 reduce-scatter.12
  1646.5 397.7 reduce-scatter.14
  2049.9 397.7 reduce-scatter.16
  2453.0 123.6 reduce-scatter.8
  2580.4 22.5 all-reduce.11
where the time goes:
time: 2630 us; the launch traced here: 2620 us
  waiting for transfers between devices  1780 us (68%)
  matrix products  344 us (13%)
  blocking collectives  169 us (6%)
  local copies, waits for them, and re-layouts  122 us (5%)
  starting transfers between devices  96.7 us (4%)
  other arithmetic  86.7 us (3%)
    reduce_scatter x1, waiting for transfers between devices, on_device(): lax.psum_scatter(micro_grads[5], 'shard', scatter_dimension=0, tiled=True)  401 us
    reduce_scatter x1, waiting for transfers between devices, on_device(): lax.psum_scatter(micro_grads[6], 'shard', scatter_dimension=0, tiled=True)  401 us
    reduce_scatter x1, waiting for transfers between devices, on_device(): lax.psum_scatter(micro_grads[7], 'shard', scatter_dimension=0, tiled=True)  401 us
    all_gather x1, waiting for transfers between devices, on_device(): lax.all_gather(shards[6], 'shard', axis=0, tiled=True)  160 us
    all_gather x1, waiting for transfers between devices, on_device(): lax.all_gather(shards[7], 'shard', axis=0, tiled=True)  159 us
    unnamed x2, blocking collectives  120 us
    dot_general x12, matrix products, product_tn(): lax.dot_general(first_op, second_op, (((0,), (0,)), ((), ())), preferred_...  114 us
    dot_general x12, matrix products, product_nt(): lax.dot_general(first_op, second_op, (((1,), (1,)), ((), ())), preferred_...  82 us
  transfers between devices with their start and end apart: 24, of which 16 were waited for; matrix products, arithmetic and copies ran while one was open for 16% of the time, Pallas kernels for 0%

commit v1 on v0

v1 whole, which is shorter than its diff:
```python
import functools
import math

import jax
import jax.numpy as jnp
from jax import lax
from jax.experimental import pallas as pl
from jax.experimental.pallas import tpu as pltpu
from jax.sharding import PartitionSpec as P

epsilon = 1e-06
masked_out = -1e30
bf16 = jnp.bfloat16
f32 = jnp.float32
plane = 4
ring_order = (0, 1, 3, 2)


def rms_factor(values):
    return lax.rsqrt(jnp.mean(values * values, axis=-1, keepdims=True) + epsilon)


def product(first_op, second_op):
    return jnp.dot(first_op, second_op, preferred_element_type=f32)


def product_tn(first_op, second_op):
    return lax.dot_general(
        first_op, second_op, (((0,), (0,)), ((), ())), preferred_element_type=f32
    )


def product_nt(first_op, second_op):
    return lax.dot_general(
        first_op, second_op, (((1,), (1,)), ((), ())), preferred_element_type=f32
    )


def norm_backward(values, factor, gain, upstream):
    inner_mean = jnp.mean(gain * upstream * values, axis=-1, keepdims=True)
    return factor * gain * upstream - values * factor * factor * factor * inner_mean


def across(value, mask):
    count = lax.axis_size("shard")
    return lax.ppermute(value, "shard", [(i, i ^ mask) for i in range(count)])


def peer(value):
    count = lax.axis_size("grp")
    return lax.ppermute(value, "grp", [(i, i ^ 1) for i in range(count)])


def column_groups():
    count = lax.axis_size("shard")
    return [[a * plane + b for a in range(count // plane)] for b in range(plane)]


def gather_column(value):
    return lax.all_gather(
        value, "shard", axis=0, tiled=True, axis_index_groups=column_groups()
    )


def scatter_column(value):
    return lax.psum_scatter(
        value, "shard", scatter_dimension=0, tiled=True, axis_index_groups=column_groups()
    )


def gather_plane(value):
    half = value.shape[0] // 2
    first = across(value, 1)
    second = across(value, 2)
    far_top = across(first[:half], 2)
    far_bottom = across(second[half:], 1)
    return value, first, second, far_top, far_bottom


def place_plane(blocks, my_place):
    own, first, second, far_top, far_bottom = blocks
    lead, rows, width = own.shape
    out = jnp.zeros((lead, plane, rows, width), own.dtype)
    far = jnp.concatenate([far_top, far_bottom], axis=0)
    for mask, block in enumerate((own, first, second, far)):
        out = lax.dynamic_update_slice_in_dim(out, block[:, None], my_place ^ mask, axis=1)
    return out


def reduce_plane(x_send, x_keep, y_send, y_keep):
    x_got = across(x_send.astype(bf16), 1).astype(f32)
    y_got = across(y_send.astype(bf16), 2).astype(f32)
    x_last = across((x_keep[1].astype(f32) + x_got[1]).astype(bf16), 2).astype(f32)
    y_last = across((y_keep[1].astype(f32) + y_got[1]).astype(bf16), 1).astype(f32)
    return (
        x_keep[0].astype(f32) + x_got[0] + x_last,
        y_keep[0].astype(f32) + y_got[0] + y_last,
    )


def pick(stack, index):
    return lax.dynamic_index_in_dim(stack, index, axis=1, keepdims=False)


def reduce_rows(grad, my_place):
    count = lax.axis_size("shard")
    rows = grad.shape[0] // count
    lead = count // plane
    blocks = grad.reshape(lead, plane, rows, -1)
    parts = [pick(blocks, my_place ^ mask) for mask in range(plane)]
    half = lead // 2
    top = [part[:half] for part in parts]
    low = [part[half:] for part in parts]
    x_sum, y_sum = reduce_plane(
        jnp.stack([top[1], top[3]]),
        jnp.stack([top[0], top[2]]),
        jnp.stack([low[2], low[3]]),
        jnp.stack([low[0], low[1]]),
    )
    summed = jnp.concatenate([x_sum, y_sum], axis=0).astype(bf16)
    return scatter_column(summed.reshape(lead * rows, -1))


def window_mask(info, dims, micro, piece):
    sub, window, keys, pad, seqs = dims
    base = piece * window + info[1] * sub
    query = base + lax.broadcasted_iota(jnp.int32, (sub, 1), 0)
    start = jnp.zeros((sub, 1), jnp.int32)
    end = jnp.int32(0)
    for k in range(seqs - 1):
        end = end + info[2 + micro * seqs + k]
        start = jnp.where(query >= end, end, start)
    lowest = jnp.maximum(start, query - (window - 1))
    key = base - pad + lax.broadcasted_iota(jnp.int32, (sub, keys), 1)
    return jnp.where((key >= lowest) & (key <= query), 0.0, masked_out).astype(f32)


def fill_window(info, dims, micro_count, pieces, blocks, key_all, value_all):
    sub, window, keys, pad, seqs = dims
    head_size = key_all.shape[-1]
    key_all[:, :pad, :] = jnp.zeros((micro_count, pad, head_size), bf16)
    value_all[:, :pad, :] = jnp.zeros((micro_count, pad, head_size), bf16)
    slots = micro_count * pieces
    offset = {0: 0, 1: 0, 2: 0, 3: 0}
    for mask, block in zip((0, 1, 2, 3, 3), blocks):
        member = info[0] ^ mask
        first = offset[mask]
        amount = block.shape[0] // sub

        def copy(step, carry, block=block, member=member, first=first):
            index = step + first
            row = pl.multiple_of(
                pad + (index % pieces) * window + ((index // slots) * plane + member) * sub, 16
            )
            micro = (index // pieces) % micro_count
            rows = block[pl.ds(pl.multiple_of(step * sub, 16), sub), :]
            key_all[micro, pl.ds(row, sub), :] = rows[:, :head_size]
            value_all[micro, pl.ds(row, sub), :] = rows[:, head_size:]
            return carry

        lax.fori_loop(0, amount, copy, 0)
        offset[mask] = first + amount


def stack_heads(ref, rows, heads, head_size):
    block = ref[rows, :]
    return jnp.concatenate(
        [block[:, h * head_size : (h + 1) * head_size] for h in heads], axis=0
    )


def attend_forward_kernel(
    dims, micro_count, pieces, group, info, q_ref, k0, k1, k2, k3, k4, o_ref, lse_ref, key_all, value_all
):
    sub, window, keys, pad, seqs = dims
    head_size = key_all.shape[-1]
    head_count = q_ref.shape[1] // head_size
    fill_window(info, dims, micro_count, pieces, (k0, k1, k2, k3, k4), key_all, value_all)
    scale = 1.0 / math.sqrt(head_size) / math.log(2.0)

    def slot(index, carry):
        micro = index // pieces
        piece = index % pieces
        bias = window_mask(info, dims, micro, piece)
        start = pl.multiple_of(piece * window + info[1] * sub, 16)
        key_part = key_all[micro, pl.ds(start, keys), :]
        value_part = value_all[micro, pl.ds(start, keys), :]
        rows = pl.ds(pl.multiple_of(index * sub, 16), sub)
        for first in range(0, head_count, group):
            heads = range(first, first + group)
            queries = stack_heads(q_ref, rows, heads, head_size)
            scores = product_nt(queries, key_part) * scale
            scores = scores.reshape(group, sub, keys) + bias[None]
            scores = scores.reshape(group * sub, keys)
            top = jnp.max(scores, axis=-1, keepdims=True)
            weights = jnp.exp2(scores - top)
            total = jnp.sum(weights, axis=-1, keepdims=True)
            mixed = (product(weights.astype(bf16), value_part) / total).astype(bf16)
            for at, h in enumerate(heads):
                o_ref[rows, h * head_size : (h + 1) * head_size] = mixed[at * sub : (at + 1) * sub]
            lse_ref[index, first * sub : (first + group) * sub, :] = top + jnp.log2(total)
        return carry

    lax.fori_loop(0, micro_count * pieces, slot, 0)


def attend_backward_kernel(
    dims,
    micro_count,
    pieces,
    group,
    info,
    q_ref,
    g_ref,
    lse_ref,
    k0,
    k1,
    k2,
    k3,
    k4,
    dq_ref,
    kx_send,
    kx_keep,
    vy_send,
    vy_keep,
    key_all,
    value_all,
    dkey_all,
    dvalue_all,
):
    sub, window, keys, pad, seqs = dims
    head_size = key_all.shape[-1]
    head_count = q_ref.shape[1] // head_size
    fill_window(info, dims, micro_count, pieces, (k0, k1, k2, k3, k4), key_all, value_all)
    dkey_all[...] = jnp.zeros(dkey_all.shape, f32)
    dvalue_all[...] = jnp.zeros(dvalue_all.shape, f32)
    plain = 1.0 / math.sqrt(head_size)
    scale = plain / math.log(2.0)

    def slot(index, carry):
        micro = index // pieces
        piece = index % pieces
        bias = window_mask(info, dims, micro, piece)
        start = pl.multiple_of(piece * window + info[1] * sub, 16)
        key_part = key_all[micro, pl.ds(start, keys), :]
        value_part = value_all[micro, pl.ds(start, keys), :]
        rows = pl.ds(pl.multiple_of(index * sub, 16), sub)
        dkey = jnp.zeros((keys, head_size), f32)
        dvalue = jnp.zeros((keys, head_size), f32)
        for first in range(0, head_count, group):
            heads = range(first, first + group)
            queries = stack_heads(q_ref, rows, heads, head_size)
            grads = stack_heads(g_ref, rows, heads, head_size)
            lse = lse_ref[index, first * sub : (first + group) * sub, :]
            scores = product_nt(queries, key_part) * scale
            scores = scores.reshape(group, sub, keys) + bias[None]
            prob = jnp.exp2(scores.reshape(group * sub, keys) - lse)
            dprob = product_nt(grads, value_part)
            delta = jnp.sum(prob * dprob, axis=-1, keepdims=True)
            dscore = (prob * (dprob - delta)).astype(bf16)
            dquery = (product(dscore, key_part) * plain).astype(bf16)
            for at, h in enumerate(heads):
                dq_ref[rows, h * head_size : (h + 1) * head_size] = dquery[
                    at * sub : (at + 1) * sub
                ]
            dkey = dkey + product_tn(dscore, queries)
            dvalue = dvalue + product_tn(prob.astype(bf16), grads)
        dkey_all[micro, pl.ds(start, keys), :] += dkey * plain
        dvalue_all[micro, pl.ds(start, keys), :] += dvalue
        return carry

    lax.fori_loop(0, micro_count * pieces, slot, 0)
    slots = micro_count * pieces
    for mask, k_out, k_at, v_out, v_at in (
        (0, kx_keep, 0, vy_keep, 0),
        (1, kx_send, 0, vy_keep, 1),
        (2, kx_keep, 1, vy_send, 0),
        (3, kx_send, 1, vy_send, 1),
    ):
        member = info[0] ^ mask

        def copy(index, carry, member=member, k_out=k_out, k_at=k_at, v_out=v_out, v_at=v_at):
            row = pl.multiple_of(
                pad + (index % pieces) * window + ((index // slots) * plane + member) * sub, 16
            )
            micro = (index // pieces) % micro_count
            to = pl.ds(pl.multiple_of(index * sub, 16), sub)
            k_out[k_at, to, :] = dkey_all[micro, pl.ds(row, sub), :].astype(bf16)
            v_out[v_at, to, :] = dvalue_all[micro, pl.ds(row, sub), :].astype(bf16)
            return carry

        lax.fori_loop(0, kx_keep.shape[1] // sub, copy, 0)


def attention_calls(micro_count, pieces, sub, window, head_size, head_count, seqs, kv_rows):
    keys = -(-(window + sub) // 128) * 128
    pad = keys - sub
    dims = (sub, window, keys, pad, seqs)
    group = max(g for g in range(1, head_count + 1) if head_count % g == 0 and g * sub <= max(384, sub))
    token_count = micro_count * pieces * sub
    width = head_count * head_size
    smem = pl.BlockSpec(memory_space=pltpu.SMEM)
    vmem = pl.BlockSpec(memory_space=pltpu.VMEM)
    shape = jax.ShapeDtypeStruct
    span = pad + pieces * window
    work = token_count * head_count * keys
    lse_shape = shape((micro_count * pieces, head_count * sub, 1), f32)
    params = pltpu.CompilerParams(vmem_limit_bytes=56 * 2**20)
    forward = pl.pallas_call(
        functools.partial(attend_forward_kernel, dims, micro_count, pieces, group),
        out_shape=(shape((token_count, width), bf16), lse_shape),
        in_specs=[smem] + [vmem] * 6,
        out_specs=(vmem, vmem),
        scratch_shapes=[pltpu.VMEM((micro_count, span, head_size), bf16)] * 2,
        cost_estimate=pl.CostEstimate(
            flops=4 * work * head_size, transcendentals=work, bytes_accessed=4 * 2**20
        ),
        compiler_params=params,
        name="attend_forward",
    )
    block = shape((2, kv_rows, head_size), bf16)
    backward = pl.pallas_call(
        functools.partial(attend_backward_kernel, dims, micro_count, pieces, group),
        out_shape=(shape((token_count, width), bf16), block, block, block, block),
        in_specs=[smem] + [vmem] * 8,
        out_specs=(vmem,) * 5,
        scratch_shapes=[pltpu.VMEM((micro_count, span, head_size), bf16)] * 2
        + [pltpu.VMEM((micro_count, span, head_size), f32)] * 2,
        cost_estimate=pl.CostEstimate(
            flops=10 * work * head_size, transcendentals=work, bytes_accessed=8 * 2**20
        ),
        compiler_params=params,
        name="attend_backward",
    )
    return forward, backward


def on_device(
    tokens,
    lengths,
    piece_order,
    predecessor,
    gain_one,
    query_weight,
    keyval_weight,
    outproj_weight,
    gain_two,
    gate_weight,
    up_weight,
    down_weight,
    cotangent,
):
    shard_count = lax.axis_size("shard")
    grp_count = lax.axis_size("grp")
    lead = shard_count // plane
    micro_count, piece_count, sub_rows, feat = tokens.shape
    window = sub_rows * shard_count
    token_count = micro_count * piece_count * sub_rows
    head_size = keyval_weight.shape[1] // 2
    width = query_weight.shape[1]
    head_count = width // head_size
    hidden_width = gate_weight.shape[1]
    my_rows = query_weight.shape[0]
    my_hidden = down_weight.shape[0]
    part = hidden_width // plane
    half_w = width // 2
    half_d = feat // 2
    my_index = lax.axis_index("shard")
    my_place = my_index % plane
    core = lax.axis_index("grp") % 2
    first_core = core == 0

    def in_order(own, other):
        return jnp.where(
            first_core,
            jnp.concatenate([own, other], axis=1),
            jnp.concatenate([other, own], axis=1),
        )

    def halves(value):
        size = value.shape[1] // 2
        return (
            lax.dynamic_slice_in_dim(value, core * size, size, 1),
            lax.dynamic_slice_in_dim(value, (1 - core) * size, size, 1),
        )

    gain_cols = jnp.pad(jnp.stack([gain_one, gain_two], axis=1), ((0, 0), (0, 126)))
    qkv_mine = jnp.concatenate(
        [halves(query_weight)[0], halves(keyval_weight)[0], gain_cols], axis=1
    )
    out_mine = halves(outproj_weight)[0]
    attn_w = gather_column(jnp.concatenate([qkv_mine, out_mine], axis=1))
    attn_blocks = gather_plane(attn_w.reshape(lead, my_rows, -1))
    attn_own = place_plane(attn_blocks, my_place).reshape(feat, -1)
    attn_other = peer(attn_own)
    cut = half_w + head_size
    qkv_own, qkv_other = attn_own[:, :cut], attn_other[:, :cut]
    out_own, out_other = attn_own[:, cut + 128 :], attn_other[:, cut + 128 :]
    gains = attn_own[:, cut : cut + 2].T
    full_gain_one = gains[0].astype(f32)
    full_gain_two = gains[1].astype(f32)

    gate_or_up = jnp.where(first_core, gate_weight, up_weight)
    pieces_out = jnp.transpose(
        gate_or_up.reshape(my_rows, lead, plane, my_hidden), (2, 0, 1, 3)
    ).reshape(plane, my_rows, part)
    wide_in = jnp.zeros((plane, my_rows, part), bf16)
    for mask in range(plane):
        block = lax.dynamic_index_in_dim(pieces_out, my_place ^ mask, axis=0, keepdims=True)
        block = block if mask == 0 else across(block, mask)
        wide_in = lax.dynamic_update_slice_in_dim(wide_in, block, my_place ^ mask, axis=0)
    wide_own = gather_column(wide_in.reshape(plane * my_rows, part))
    down_own = gather_column(halves(down_weight)[0])
    wide_other = peer(wide_own)
    down_other = peer(down_own)

    stream = tokens.reshape(token_count, feat).astype(f32)
    factor_one = rms_factor(stream)
    normed_one = (stream * factor_one * full_gain_one).astype(bf16)
    mixed_own = product(normed_one, qkv_own).astype(bf16)
    mixed_other = product(normed_one, qkv_other).astype(bf16)
    queries = in_order(mixed_own[:, :half_w], mixed_other[:, :half_w])
    keyvals = in_order(mixed_own[:, half_w:], mixed_other[:, half_w:])
    kv_blocks = gather_plane(gather_column(keyvals))
    forward, backward = attention_calls(
        micro_count,
        piece_count,
        sub_rows,
        window,
        head_size,
        head_count,
        lengths.shape[-1],
        lead * token_count,
    )
    info = jnp.concatenate(
        [
            jnp.stack([my_place, my_index]).astype(jnp.int32),
            lengths.reshape(-1).astype(jnp.int32),
        ]
    )
    attended, logsum = forward(info, queries, *kv_blocks)
    residual = stream + in_order(product(attended, out_own), product(attended, out_other))
    factor_two = rms_factor(residual)
    normed_two = (residual * factor_two * full_gain_two).astype(bf16)

    def plane_tokens(value):
        own, first, second, far_top, far_bottom = gather_plane(value)
        return jnp.concatenate([own, first, far_top, far_bottom, second], axis=0)

    upstream = cotangent.reshape(token_count, feat)
    all_up = plane_tokens(upstream)
    all_normed = plane_tokens(normed_two)
    pre_own = product(all_normed, wide_own)
    pre_other = product(all_normed, wide_other)
    gate_pre = jnp.where(first_core, pre_own, pre_other)
    upward = jnp.where(first_core, pre_other, pre_own)
    root = math.sqrt(2.0 / math.pi)
    curve = jnp.tanh(root * (gate_pre + 0.044715 * gate_pre * gate_pre * gate_pre))
    active = 0.5 * gate_pre * (1.0 + curve)
    slope = 0.5 * (1.0 + curve) + 0.5 * gate_pre * (1.0 - curve * curve) * root * (
        1.0 + 3 * 0.044715 * gate_pre * gate_pre
    )
    hidden = (active * upward).astype(bf16)
    up_own, up_other = halves(all_up)
    grad_hidden = product_nt(up_own, down_own) + product_nt(up_other, down_other)
    grad_gate_in = (grad_hidden * upward * slope).astype(bf16)
    grad_up_in = (grad_hidden * active).astype(bf16)
    grad_own_in = jnp.where(first_core, grad_gate_in, grad_up_in)
    grad_other_in = jnp.where(first_core, grad_up_in, grad_gate_in)

    def token_sum(first_half, second_half):
        one = first_half.astype(bf16).reshape(plane, token_count, -1)
        two = second_half.astype(bf16).reshape(plane, token_count, -1)
        return reduce_plane(
            one[1:3], (one[0], one[3]), jnp.stack([two[3], two[2]]), (two[0], two[1])
        )

    out_sum = token_sum(product(hidden, down_own), product(hidden, down_other))
    block_output = (residual + in_order(*out_sum)).astype(bf16).reshape(tokens.shape)
    grad_wide = product_nt(grad_own_in, wide_own) + product_nt(grad_other_in, wide_other)
    grad_normed_two = jnp.concatenate(
        token_sum(grad_wide[:, :half_d], grad_wide[:, half_d:]), axis=1
    )

    def chip_sum(own, other):
        return (own + peer(other.astype(bf16)).astype(f32)).astype(bf16)

    down_grad = scatter_column(
        chip_sum(product_tn(hidden, up_own), product_tn(hidden, up_other))
    )
    wide_grad = scatter_column(
        chip_sum(product_tn(all_normed, grad_own_in), product_tn(all_normed, grad_other_in))
    ).reshape(plane, my_rows, part)
    wide_back = jnp.zeros((plane, my_rows, part), bf16)
    for mask in range(plane):
        block = lax.dynamic_index_in_dim(wide_grad, my_place ^ mask, axis=0, keepdims=True)
        block = block if mask == 0 else across(block, mask)
        wide_back = lax.dynamic_update_slice_in_dim(wide_back, block, my_place ^ mask, axis=0)
    wide_share = jnp.transpose(
        wide_back.reshape(plane, my_rows, lead, my_hidden), (1, 2, 0, 3)
    ).reshape(my_rows, hidden_width)

    grad_gain_two = jnp.sum(grad_normed_two * residual * factor_two, axis=0)
    grad_resid = upstream.astype(f32) + norm_backward(
        residual, factor_two, full_gain_two, grad_normed_two
    )
    grad_attn = grad_resid.astype(bf16)
    attn_own_half, attn_other_half = halves(grad_attn)
    outproj_share = reduce_rows(
        chip_sum(product_tn(attended, attn_own_half), product_tn(attended, attn_other_half)),
        my_place,
    )
    grad_mixed = (
        product_nt(attn_own_half, out_own) + product_nt(attn_other_half, out_other)
    ).astype(bf16)
    grad_queries, kx_send, kx_keep, vy_send, vy_keep = backward(
        info, queries, grad_mixed, logsum, *kv_blocks
    )
    grad_kv = jnp.concatenate(reduce_plane(kx_send, kx_keep, vy_send, vy_keep), axis=1)
    grad_keyvals = scatter_column(grad_kv.astype(bf16))
    dq_own, dq_other = halves(grad_queries)
    dkv_own, dkv_other = halves(grad_keyvals)
    query_share = reduce_rows(
        chip_sum(product_tn(normed_one, dq_own), product_tn(normed_one, dq_other)), my_place
    )
    dqkv_own = jnp.concatenate([dq_own, dkv_own], axis=1)
    dqkv_other = jnp.concatenate([dq_other, dkv_other], axis=1)
    grad_normed_one = product_nt(dqkv_own, qkv_own) + product_nt(dqkv_other, qkv_other)
    grad_gain_one = jnp.sum(grad_normed_one * stream * factor_one, axis=0)
    grad_stream = grad_resid + norm_backward(stream, factor_one, full_gain_one, grad_normed_one)
    input_grad = grad_stream.astype(bf16).reshape(tokens.shape)

    def as_column(value):
        return jnp.broadcast_to(value[:, None], (feat, 128))

    gain_own = as_column(jnp.where(first_core, grad_gain_one, grad_gain_two))
    gain_other = as_column(jnp.where(first_core, grad_gain_two, grad_gain_one))
    last_share = reduce_rows(
        chip_sum(
            jnp.concatenate([product_tn(normed_one, dkv_own), gain_own], axis=1),
            jnp.concatenate([product_tn(normed_one, dkv_other), gain_other], axis=1),
        ),
        my_place,
    )

    def whole(share):
        total = share
        for step in range(1, grp_count // 2):
            moved = lax.ppermute(
                share, "grp", [(i, (i + 2 * step) % grp_count) for i in range(grp_count)]
            )
            total = total.astype(f32) + moved.astype(f32)
        total = total.astype(bf16)
        return total.astype(f32), peer(total).astype(f32)

    wide_one, wide_two = whole(wide_share)
    down_pair = whole(down_grad)
    out_pair = whole(outproj_share)
    query_pair = whole(query_share)
    last_one, last_two = whole(last_share)
    return (
        block_output,
        input_grad,
        jnp.where(first_core, last_one[:, head_size], last_two[:, head_size]),
        in_order(*query_pair),
        in_order(last_one[:, :head_size], last_two[:, :head_size]),
        in_order(*out_pair),
        jnp.where(first_core, last_two[:, head_size], last_one[:, head_size]),
        jnp.where(first_core, wide_one, wide_two),
        jnp.where(first_core, wide_two, wide_one),
        in_order(*down_pair),
    )


def solution(mesh):
    in_specs = (
        P(None, "grp", "shard", None),
        P(None, "grp", None),
        P(None, "grp", None),
        P(None, "grp", None),
        P("shard"),
        P("shard", None),
        P("shard", None),
        P("shard", None),
        P("shard"),
        P("shard", None),
        P("shard", None),
        P("shard", None),
        P(None, "grp", "shard", None),
    )
    out_specs = (
        P(None, "grp", "shard", None),
        P(None, "grp", "shard", None),
        P("shard"),
        P("shard", None),
        P("shard", None),
        P("shard", None),
        P("shard"),
        P("shard", None),
        P("shard", None),
        P("shard", None),
    )
    return jax.shard_map(
        on_device, mesh=mesh, in_specs=in_specs, out_specs=out_specs, check_vma=False
    )
```

time: 2630 us -> 648 us (0.25)
  waiting for transfers between devices: 1780 us -> 316 us
  matrix products: 344 us -> 109 us
  blocking collectives: 169 us -> 22.9 us
  local copies, waits for them, and re-layouts: 122 us -> 44.9 us
  other arithmetic: 86.7 us -> 40.7 us
  starting transfers between devices: 96.7 us -> 57.5 us
  Pallas kernels: 0 us -> 32.3 us
    reduce_scatter x6, waiting for transfers between devices: 1290 us -> 70 us  [scatter_column(): lax.psum_scatter(value, 'shard', scatter_dimension=0, tiled=True, axis_in...]
    all_gather x5 -> x3, waiting for transfers between devices: 369 us -> 58.4 us  [gather_column(): lax.all_gather(value, 'shard', axis=0, tiled=True, axis_index_groups=colu...]
    ppermute x0 -> x59, waiting for transfers between devices: none -> 188 us  [the longest x46 187 us: across(): return lax.ppermute(value, 'shard', [(i, i ^ mask) for i in range(count)])]
    unnamed x2 -> x0, blocking collectives: 120 us -> none
    dot_general x58 -> x8, matrix products: 148 us -> 28.8 us  [product(): return jnp.dot(first_op, second_op, preferred_element_type=f32)]
    all_to_all x12 -> x0, waiting for transfers between devices: 98.8 us -> none  [the longest x2 38.1 us: on_device(): lax.all_to_all(keyval_send, 'shard', split_axis=1, concat_axis=1, tiled=T...]
    all_to_all x12 -> x0, starting transfers between devices: 95.2 us -> none  [the longest x2 20.9 us: on_device(): lax.all_to_all(query_send, 'shard', split_axis=1, concat_axis=1, tiled=True)]
    dot_general x12 -> x10, matrix products: 114 us -> 37.9 us  [product_tn(): lax.dot_general(first_op, second_op, (((0,), (0,)), ((), ())), preferred_...]
  transfers between devices with their start and end apart: 24 -> 68, of which waited for: 16 -> 34; matrix products, arithmetic and copies ran while one was open for 16% -> 23% of each run, Pallas kernels for 0% -> 2%
where the time goes in v1:
time: 648 us; the launch traced here: 640 us
  waiting for transfers between devices  316 us (49%)
  matrix products  109 us (17%)
  starting transfers between devices  57.5 us (9%)
  local copies, waits for them, and re-layouts  44.9 us (7%)
  other arithmetic  40.7 us (6%)
  Pallas kernels  32.3 us (5%)
  blocking collectives  22.9 us (4%)
  between operations  15.6 us (2%)
    ppermute x46, waiting for transfers between devices, across(): return lax.ppermute(value, 'shard', [(i, i ^ mask) for i in range(count)])  187 us
    reduce_scatter x6, waiting for transfers between devices, scatter_column(): lax.psum_scatter(value, 'shard', scatter_dimension=0, tiled=True, axis_in...  70 us
    all_gather x3, waiting for transfers between devices, gather_column(): lax.all_gather(value, 'shard', axis=0, tiled=True, axis_index_groups=colu...  58.4 us
    ppermute x46, starting transfers between devices, across(): return lax.ppermute(value, 'shard', [(i, i ^ mask) for i in range(count)])  55.8 us
    dot_general x8, matrix products, product_nt(): lax.dot_general(first_op, second_op, (((1,), (1,)), ((), ())), preferred_...  42.8 us
    dot_general x10, matrix products, product_tn(): lax.dot_general(first_op, second_op, (((0,), (0,)), ((), ())), preferred_...  37.9 us
    dot_general x8, matrix products, product(): return jnp.dot(first_op, second_op, preferred_element_type=f32)  28.8 us
    all_gather x1, blocking collectives, gather_column(): lax.all_gather(value, 'shard', axis=0, tiled=True, axis_index_groups=colu...  22.9 us
  transfers between devices with their start and end apart: 68, of which 34 were waited for; matrix products, arithmetic and copies ran while one was open for 23% of the time, Pallas kernels for 2%

profile of v1, /device:TPU:0, one launch (start us, length us, event | category | flops | bytes accessed | tf_op | source)
XLA Modules:
  0.0 639.8 jit_solution(15816905528528498983)
XLA Ops:
  10.7 36.6 %all-gather.4.cloned.1.call-done = bf16[384,1792]{1,0:T(8,128)(2,1)} async-done(((bf16[96,1792]{1,0:T(8,128)(2,1)}), bf16[384,1792]{1,0:T(8,128)(2,1)}) %all-gather.4.cloned.1.call-update) | async-done | bytes 1376272 | tf_op jit(solution)/shard_map/all_gather | solution.py:60
  55.3 23.4 %collective-permute-done = bf16[4,96,1792]{2,1,0:T(8,128)(2,1)S(1)} collective-permute-done((bf16[4,96,1792]{2,1,0:T(8,128)(2,1)}, bf16[4,96,1792]{2,1,0:T(8,128)(2,1)S(1)}, u32[]{:S(2)}, u32[]{:S(2)}) %collective-permute-start) | collective-permute-done | bytes 1376288 | tf_op jit(solution)/shard_map/ppermute | solution.py:46
  86.9 7.8 %collective-permute-done.2 = bf16[2,96,1792]{2,1,0:T(8,128)(2,1)S(1)} collective-permute-done((bf16[2,96,1792]{2,1,0:T(8,128)(2,1)S(1)}, bf16[2,96,1792]{2,1,0:T(8,128)(2,1)S(1)}, u32[]{:S(2)}, u32[]{:S(2)}) %collective-permute-start.2) | collective-permute-done | bytes 688160 | tf_op jit(solution)/shard_map/ppermute | solution.py:46
  126.2 22.9 %all_gather.13.k0 = bf16[1024,256]{1,0:T(8,128)(2,1)} all-gather(bf16[256,256]{1,0:T(8,128)(2,1)S(1)} %maximum_select_fusion.7), channel_id=1, replica_groups={{0,4,8,12},{1,5,9,13},{2,6,10,14},{3,7,11,15},{16,20,24,28},{17,21,25,2..., dimensions={0}, use_global_device_ids=true | all-gather | bytes 655360 | tf_op jit(solution)/shard_map/all_gather | solution.py:60
  172.4 21.8 %all-gather.6.cloned.1.call-done = bf16[1536,1152]{1,0:T(8,128)(2,1)} async-done(((bf16[384,1152]{1,0:T(8,128)(2,1)}), bf16[1536,1152]{1,0:T(8,128)(2,1)}) %all-gather.6.cloned.1.call-update) | async-done | bytes 3538960 | tf_op jit(solution)/shard_map/all_gather | solution.py:60
  194.2 12.7 %attend_forward.1 = (bf16[256,1536]{1,0:T(8,128)(2,1)}, f32[4,768,1]{2,1,0:T(8,128)}) custom-call(s32[6]{0:T(128)} %pad_add_fusion.info, bf16[256,1536]{1,0:T(8,128)(2,1)} %maximum_select_fusion.4.q_ref, bf16[1024,256]{1,0:T(8,128)(2,1)} %all_gather.13.k0, bf16[1024,256]{1,0:T(8,128)(2,1)} %collective-permute-done.5.k1, ...), custom_call_target="tpu_custom_call" | custom-call | flops 1811939328 | bytes 4194304 | tf_op jit(solution)/shard_map/attend_forward/pallas_call | solution.py:441
  218.5 14.4 %collective-permute-done.9 = bf16[256,1536]{1,0:T(8,128)(2,1)S(1)} collective-permute-done((bf16[256,1536]{1,0:T(8,128)(2,1)S(1)}, bf16[256,1536]{1,0:T(8,128)(2,1)S(1)}, u32[]{:S(2)}, u32[]{:S(2)}) %collective-permute-start.9) | collective-permute-done | bytes 786464 | tf_op jit(solution)/shard_map/ppermute | solution.py:46
  244.3 6.7 %collective-permute-done.12 = bf16[128,1536]{1,0:T(8,128)(2,1)S(1)} collective-permute-done((bf16[128,1536]{1,0:T(8,128)(2,1)S(1)}, bf16[128,1536]{1,0:T(8,128)(2,1)S(1)}, u32[]{:S(2)}, u32[]{:S(2)}) %collective-permute-start.12) | collective-permute-done | bytes 393248 | tf_op jit(solution)/shard_map/ppermute | solution.py:46
  261.6 8.2 %fusion.7 = (bf16[1024,1152]{1,0:T(8,128)(2,1)}, f32[1024,1152]{1,0:T(8,128)S(1)}, f32[1024,1152]{1,0:T(8,128)S(1)}) fusion(f32[1024,1152]{1,0:T(8,128)S(1)} %fusion.140, f32[1024,1152]{1,0:T(8,128)S(1)} %fusion.139, pred[]{:T(512)S(6)} %eq.6, f32[1024,1152]{1,0:T(8,128)} %fusion.45, bf16[1152,768]{1,0:T(8,128)(2,1)} %all-gather.8.cloned.1.call-done, ...), kind=kOutput, calls=%fused_computation.12 | convolution fusion | flops 1839071232 | bytes 29294596 | tf_op jit(solution)/shard_map/dot_general | solution.py:34
  278.7 8.3 %fusion.56 = f32[1024,1536]{1,0:T(8,128)} fusion(bf16[1536,1152]{1,0:T(8,128)(2,1)} %collective-permute-done.16, bf16[1024,1152]{1,0:T(8,128)(2,1)S(1)} %get-tuple-element.36, bf16[1024,1152]{1,0:T(8,128)(2,1)S(1)} %copy-done.52, pred[]{:T(512)S(6)} %eq.6), kind=kOutput, calls=%fused_computation.99 | convolution fusion | flops 3625058304 | bytes 14548993 | tf_op jit(solution)/shard_map/dot_general | solution.py:34
  287.0 6.7 %add_convert_fusion = bf16[1024,1536]{1,0:T(8,128)(2,1)S(1)} fusion(f32[1024,1536]{1,0:T(8,128)} %fusion.56, bf16[1536,1152]{1,0:T(8,128)(2,1)S(1)} %copy-done.50, bf16[1024,1152]{1,0:T(8,128)(2,1)S(1)} %copy-done.52, bf16[1024,1152]{1,0:T(8,128)(2,1)} %copy-done.16, pred[]{:T(512)S(6)} %eq.6), kind=kOutput, calls=%fused_computation.5 | convolution fusion | flops 3628204032 | bytes 17694720 | tf_op jit(solution)/shard_map/dot_general | solution.py:34
  299.0 15.3 %collective-permute-done.26 = bf16[2,256,768]{2,1,0:T(8,128)(2,1)S(1)} collective-permute-done((bf16[2,256,768]{2,1,0:T(8,128)(2,1)S(1)}, bf16[2,256,768]{2,1,0:T(8,128)(2,1)S(1)}, u32[]{:S(2)}, u32[]{:S(2)}) %collective-permute-start.26) | collective-permute-done | bytes 786464 | tf_op jit(solution)/shard_map/ppermute | solution.py:46
  316.9 14.3 %collective-permute-done.17 = bf16[2,256,768]{2,1,0:T(8,128)(2,1)S(1)} collective-permute-done((bf16[2,256,768]{2,1,0:T(8,128)(2,1)S(1)}, bf16[2,256,768]{2,1,0:T(8,128)(2,1)S(1)}, u32[]{:S(2)}, u32[]{:S(2)}) %collective-permute-start.17) | collective-permute-done | bytes 786464 | tf_op jit(solution)/shard_map/ppermute | solution.py:46
  339.9 6.4 collective-permute-done.29
  358.6 19.6 %attend_backward.1 = (bf16[256,1536]{1,0:T(8,128)(2,1)}, bf16[2,1024,128]{2,1,0:T(8,128)(2,1)}, bf16[2,1024,128]{2,1,0:T(8,128)(2,1)}, bf16[2,1024,128]{2,1,0:T(8,128)(2,1)}, bf16[2,1024,128]{2,1,0:T(8,128)(2,1)}) custom-call(s32[6]{0:T(128)} %pad_add_fusion.info, bf16[256,1536]{1,0:T(8,128)(2,1)} %maximum_select_fusion.4.q_ref, ...), custom_call_target="tpu_custom_call" | custom-call | flops 4529848320 | bytes 8388608 | tf_op jit(solution)/shard_map/attend_backward/pallas_call | solution.py:516
  380.2 10.3 %collective-permute-done.30 = bf16[2,1024,128]{2,1,0:T(8,128)(2,1)S(1)} collective-permute-done((bf16[2,1024,128]{2,1,0:T(8,128)(2,1)}, bf16[2,1024,128]{2,1,0:T(8,128)(2,1)S(1)}, u32[]{:S(2)}, u32[]{:S(2)}) %collective-permute-start.30) | collective-permute-done | bytes 524320 | tf_op jit(solution)/shard_map/ppermute | solution.py:46
  399.9 8.8 %convolution_convert_fusion = bf16[1536,1152]{1,0:T(8,128)(2,1)} fusion(bf16[1024,1536]{1,0:T(8,128)(2,1)} %copy-done.38, bf16[1024,1152]{1,0:T(8,128)(2,1)} %copy-done.16, bf16[1024,1152]{1,0:T(8,128)(2,1)} %get-tuple-element.34, pred[]{:T(512)S(6)} %eq.6), kind=kOutput, calls=%fused_computation.1 | convolution fusion | flops 3626827776 | bytes 11403265 | tf_op jit(solution)/shard_map/dot_general | solution.py:28
  408.8 11.4 %reduce-scatter.7.cloned.1.call-done = bf16[256,256]{1,0:T(8,128)(2,1)} async-done(((bf16[1024,256]{1,0:T(8,128)(2,1)}), bf16[256,256]{1,0:T(8,128)(2,1)}) %reduce-scatter.7.cloned.1.call-update) | async-done | bytes 131088 | tf_op jit(solution)/shard_map/reduce_scatter | solution.py:66
  451.9 9.8 %fusion = bf16[1536,1152]{1,0:T(8,128)(2,1)} fusion(bf16[1024,1536]{1,0:T(8,128)(2,1)} %copy-done.38, bf16[1536,1152]{1,0:T(8,128)(2,1)} %collective-permute-done.52, bf16[1024,1152]{1,0:T(8,128)(2,1)} %get-tuple-element.34, bf16[1024,1152]{1,0:T(8,128)(2,1)} %copy-done.16, pred[]{:T(512)S(6)} %eq.6), kind=kOutput, calls=%fused_computation.2 | convolution fusion | flops 3630366720 | bytes 14942209 | tf_op jit(solution)/shard_map/dot_general | solution.py:28
  483.7 10.2 %collective-permute-done.47 = bf16[2,2,96,768]{3,2,1,0:T(8,128)(2,1)S(1)} collective-permute-done((bf16[2,2,96,768]{3,2,1,0:T(8,128)(2,1)S(1)}, bf16[2,2,96,768]{3,2,1,0:T(8,128)(2,1)S(1)}, u32[]{:S(2)}, u32[]{:S(2)}) %collective-permute-start.47) | collective-permute-done | bytes 589856 | tf_op jit(solution)/shard_map/ppermute | solution.py:46
  528.0 6.5 %collective-permute-done.44 = bf16[2,96,768]{2,1,0:T(8,128)(2,1)S(1)} collective-permute-done((bf16[2,96,768]{2,1,0:T(8,128)(2,1)S(1)}, bf16[2,96,768]{2,1,0:T(8,128)(2,1)S(1)}, u32[]{:S(2)}, u32[]{:S(2)}) %collective-permute-start.44) | collective-permute-done | bytes 294944 | tf_op jit(solution)/shard_map/ppermute | solution.py:46
  543.1 34.9 %reduce-scatter.17.cloned.1.call-done = bf16[288,768]{1,0:T(8,128)(2,1)} async-done(((bf16[1152,768]{1,0:T(8,128)(2,1)}), bf16[288,768]{1,0:T(8,128)(2,1)}) %reduce-scatter.17.cloned.1.call-update) | async-done | bytes 442384 | tf_op jit(solution)/shard_map/reduce_scatter | solution.py:66
  581.6 9.1 %collective-permute-done.54 = bf16[1,96,1152]{2,1,0:T(8,128)(2,1)S(1)} collective-permute-done((bf16[1,96,1152]{2,1,0:T(8,128)(2,1)}, bf16[1,96,1152]{2,1,0:T(8,128)(2,1)S(1)}, u32[]{:S(2)}, u32[]{:S(2)}) %collective-permute-start.54) | collective-permute-done | bytes 221216 | tf_op jit(solution)/shard_map/ppermute | solution.py:46
  602.1 23.2 %reduce-scatter.11.cloned.1.call-done = bf16[96,768]{1,0:T(8,128)(2,1)} async-done(((bf16[384,768]{1,0:T(8,128)(2,1)}), bf16[96,768]{1,0:T(8,128)(2,1)}) %reduce-scatter.11.cloned.1.call-update) | async-done | bytes 147472 | tf_op jit(solution)/shard_map/reduce_scatter | solution.py:66
  (407 shorter events, 274.7 us)
Async XLA Ops:
  7.2 40.1 %all-gather.4.cloned.1.call-start = ((), (), s32[]{:S(2)}) async-start(), calls=%async_computation.6 | async-start | bytes 1720320 | tf_op jit(solution)/shard_map/all_gather | solution.py:60
  10.7 159.6 %all-gather.8.cloned.1.call-start = ((), (), s32[]{:S(2)}) async-start(), calls=%async_computation.8 | async-start | bytes 2211840 | tf_op jit(solution)/shard_map/all_gather | solution.py:60
  47.3 31.4 %collective-permute-start = (bf16[4,96,1792]{2,1,0:T(8,128)(2,1)}, bf16[4,96,1792]{2,1,0:T(8,128)(2,1)S(1)}, u32[]{:S(2)}, u32[]{:S(2)}) collective-permute-start(bf16[4,96,1792]{2,1,0:T(8,128)(2,1)} %bitcast.421), channel_id=1, source_target_pairs={{0,1},{1,0},{2,3},{3,2},{4,5},{5,4},{6,7},{7,6},{8,9},{9,8},{10,11... | collective-permute-start | bytes 4128776 | tf_op jit(solution)/shard_map/ppermute | solution.py:46
  48.8 31.6 %collective-permute-start.1 = (bf16[4,96,1792]{2,1,0:T(8,128)(2,1)}, bf16[4,96,1792]{2,1,0:T(8,128)(2,1)}, u32[]{:S(2)}, u32[]{:S(2)}) collective-permute-start(bf16[4,96,1792]{2,1,0:T(8,128)(2,1)} %bitcast.422), channel_id=1, source_target_pairs={{0,2},{1,3},{2,0},{3,1},{4,6},{5,7},{6,4},{7,5},{8,10},{9,11},{10,... | collective-permute-start | bytes 4128776 | tf_op jit(solution)/shard_map/ppermute | solution.py:46
  51.1 143.1 %all-gather.6.cloned.1.call-start = ((), (), s32[]{:S(2)}) async-start(), calls=%async_computation.7 | async-start | bytes 4423680 | tf_op jit(solution)/shard_map/all_gather | solution.py:60
  116.3 303.9 %reduce-scatter.7.cloned.1.call-start = ((), (), s32[]{:S(2)}) async-start(), calls=%async_computation.9 | async-start | bytes 655360 | tf_op jit(solution)/shard_map/reduce_scatter | solution.py:66
  116.4 49.8 %collective-permute-start.22 = (bf16[256,1536]{1,0:T(8,128)(2,1)}, bf16[256,1536]{1,0:T(8,128)(2,1)S(1)}, u32[]{:S(2)}, u32[]{:S(2)}) collective-permute-start(bf16[256,1536]{1,0:T(8,128)(2,1)} %bitcast.27), channel_id=1, source_target_pairs={{0,1},{1,0},{2,3},{3,2},{4,5},{5,4},{6,7},{7,6},{8,9},{9,8},{10,11... | collective-permute-start | bytes 2359304 | tf_op jit(solution)/shard_map/ppermute | solution.py:46
  116.9 51.0 %collective-permute-start.24 = (bf16[256,1536]{1,0:T(8,128)(2,1)}, bf16[256,1536]{1,0:T(8,128)(2,1)S(1)}, u32[]{:S(2)}, u32[]{:S(2)}) collective-permute-start(bf16[256,1536]{1,0:T(8,128)(2,1)} %bitcast.27), channel_id=1, source_target_pairs={{0,2},{1,3},{2,0},{3,1},{4,6},{5,7},{6,4},{7,5},{8,10},{9,11},{10,... | collective-permute-start | bytes 2359304 | tf_op jit(solution)/shard_map/ppermute | solution.py:46
  162.3 31.9 %collective-permute-start.7 = (bf16[512,256]{1,0:T(8,128)(2,1)}, bf16[512,256]{1,0:T(8,128)(2,1)}, u32[]{:S(2)}, u32[]{:S(2)}) collective-permute-start(bf16[512,256]{1,0:T(8,128)(2,1)} %slice.435), channel_id=1, source_target_pairs={{0,2},{1,3},{2,0},{3,1},{4,6},{5,7},{6,4},{7,5},{8,10},{9,11},{10,... | collective-permute-start | bytes 786440 | tf_op jit(solution)/shard_map/ppermute | solution.py:46
  167.0 47.8 %collective-permute-start.23 = (bf16[128,1536]{1,0:T(8,128)(2,1)}, bf16[128,1536]{1,0:T(8,128)(2,1)}, u32[]{:S(2)}, u32[]{:S(2)}) collective-permute-start(bf16[128,1536]{1,0:T(8,128)(2,1)} %slice.453), channel_id=1, source_target_pairs={{0,2},{1,3},{2,0},{3,1},{4,6},{5,7},{6,4},{7,5},{8,10},{9,11},{10,... | collective-permute-start | bytes 1179656 | tf_op jit(solution)/shard_map/ppermute | solution.py:46
  168.8 48.6 %collective-permute-start.25 = (bf16[128,1536]{1,0:T(8,128)(2,1)}, bf16[128,1536]{1,0:T(8,128)(2,1)}, u32[]{:S(2)}, u32[]{:S(2)}) collective-permute-start(bf16[128,1536]{1,0:T(8,128)(2,1)} %slice.454), channel_id=1, source_target_pairs={{0,1},{1,0},{2,3},{3,2},{4,5},{5,4},{6,7},{7,6},{8,9},{9,8},{10,11... | collective-permute-start | bytes 1179656 | tf_op jit(solution)/shard_map/ppermute | solution.py:46
  170.3 64.2 %collective-permute-start.19 = (bf16[1152,768]{1,0:T(8,128)(2,1)}, bf16[1152,768]{1,0:T(8,128)(2,1)}, u32[]{:S(2)}, u32[]{:S(2)}) collective-permute-start(bf16[1152,768]{1,0:T(8,128)(2,1)} %all-gather.8.cloned.1.call-done), channel_id=1, source_target_pairs={{0,16},{16,0},{1,17},{17,1},{2,18},{18,2},{3,19},{19,3},{4,20},{20... | collective-permute-start | bytes 5308424 | tf_op jit(solution)/shard_map/ppermute | solution.py:51
  194.2 61.1 %collective-permute-start.16 = (bf16[1536,1152]{1,0:T(8,128)(2,1)}, bf16[1536,1152]{1,0:T(8,128)(2,1)}, u32[]{:S(2)}, u32[]{:S(2)}) collective-permute-start(bf16[1536,1152]{1,0:T(8,128)(2,1)} %all-gather.6.cloned.1.call-done), channel_id=1, source_target_pairs={{0,16},{16,0},{1,17},{17,1},{2,18},{18,2},{3,19},{19,3},{4,20},{20... | collective-permute-start | bytes 10616840 | tf_op jit(solution)/shard_map/ppermute | solution.py:51
  277.2 38.0 %collective-permute-start.20 = (bf16[2,256,768]{2,1,0:T(8,128)(2,1)S(1)}, bf16[2,256,768]{2,1,0:T(8,128)(2,1)S(1)}, u32[]{:S(2)}, u32[]{:S(2)}) collective-permute-start(bf16[2,256,768]{2,1,0:T(8,128)(2,1)S(1)} %pad_maximum_fusion.1), channel_id=1, source_target_pairs={{0,2},{1,3},{2,0},{3,1},{4,6},{5,7},{6,4},{7,5},{8,10},{9,11},{10,... | collective-permute-start | bytes 2359304 | tf_op jit(solution)/shard_map/ppermute | solution.py:46
  297.6 33.6 %collective-permute-start.17 = (bf16[2,256,768]{2,1,0:T(8,128)(2,1)S(1)}, bf16[2,256,768]{2,1,0:T(8,128)(2,1)S(1)}, u32[]{:S(2)}, u32[]{:S(2)}) collective-permute-start(bf16[2,256,768]{2,1,0:T(8,128)(2,1)S(1)} %bitcast.425), channel_id=1, source_target_pairs={{0,1},{1,0},{2,3},{3,2},{4,5},{5,4},{6,7},{7,6},{8,9},{9,8},{10,11... | collective-permute-start | bytes 2359304 | tf_op jit(solution)/shard_map/ppermute | solution.py:46
  298.4 33.7 %collective-permute-start.28 = (bf16[2,256,768]{2,1,0:T(8,128)(2,1)S(1)}, bf16[2,256,768]{2,1,0:T(8,128)(2,1)S(1)}, u32[]{:S(2)}, u32[]{:S(2)}) collective-permute-start(bf16[2,256,768]{2,1,0:T(8,128)(2,1)S(1)} %pad_maximum_fusion.2), channel_id=1, source_target_pairs={{0,2},{1,3},{2,0},{3,1},{4,6},{5,7},{6,4},{7,5},{8,10},{9,11},{10,... | collective-permute-start | bytes 2359304 | tf_op jit(solution)/shard_map/ppermute | solution.py:46
  399.7 128.3 %reduce-scatter.9.cloned.1.call-start = ((), (), s32[]{:S(2)}) async-start(), calls=%async_computation.10 | async-start | bytes 245760 | tf_op jit(solution)/shard_map/reduce_scatter | solution.py:66
  408.8 43.1 %collective-permute-start.52 = (bf16[1536,1152]{1,0:T(8,128)(2,1)}, bf16[1536,1152]{1,0:T(8,128)(2,1)}, u32[]{:S(2)}, u32[]{:S(2)}) collective-permute-start(bf16[1536,1152]{1,0:T(8,128)(2,1)} %convolution_convert_fusion), channel_id=1, source_target_pairs={{0,16},{16,0},{1,17},{17,1},{2,18},{18,2},{3,19},{19,3},{4,20},{20... | collective-permute-start | bytes 10616840 | tf_op jit(solution)/shard_map/ppermute | solution.py:51
  451.6 85.1 %reduce-scatter.15.cloned.1.call-start = ((), (), s32[]{:S(2)}) async-start(), calls=%async_computation.13 | async-start | bytes 4423680 | tf_op jit(solution)/shard_map/reduce_scatter | solution.py:66
  461.8 116.2 %reduce-scatter.17.cloned.1.call-start = ((), (), s32[]{:S(2)}) async-start(), calls=%async_computation.14 | async-start | bytes 2211840 | tf_op jit(solution)/shard_map/reduce_scatter | solution.py:66
  474.7 127.3 %reduce-scatter.13.cloned.1.call-start = ((), (), s32[]{:S(2)}) async-start(), calls=%async_computation.12 | async-start | bytes 737280 | tf_op jit(solution)/shard_map/reduce_scatter | solution.py:66
  517.9 107.3 %reduce-scatter.11.cloned.1.call-start = ((), (), s32[]{:S(2)}) async-start(), calls=%async_computation.11 | async-start | bytes 737280 | tf_op jit(solution)/shard_map/reduce_scatter | solution.py:66
  539.8 41.1 %collective-permute-start.53 = (bf16[1,96,1152]{2,1,0:T(8,128)(2,1)}, bf16[1,96,1152]{2,1,0:T(8,128)(2,1)S(1)}, u32[]{:S(2)}, u32[]{:S(2)}) collective-permute-start(bf16[1,96,1152]{2,1,0:T(8,128)(2,1)} %get-tuple-element.61), channel_id=1, source_target_pairs={{0,1},{1,0},{2,3},{3,2},{4,5},{5,4},{6,7},{7,6},{8,9},{9,8},{10,11... | collective-permute-start | bytes 663560 | tf_op jit(solution)/shard_map/ppermute | solution.py:46
  598.6 30.8 %collective-permute-start.56 = (bf16[96,4608]{1,0:T(8,128)(2,1)}, bf16[96,4608]{1,0:T(8,128)(2,1)S(1)}, u32[]{:S(2)}, u32[]{:S(2)}) collective-permute-start(bf16[96,4608]{1,0:T(8,128)(2,1)} %reshape.280), channel_id=1, source_target_pairs={{0,16},{16,0},{1,17},{17,1},{2,18},{18,2},{3,19},{19,3},{4,20},{20... | collective-permute-start | bytes 2654216 | tf_op jit(solution)/shard_map/ppermute | solution.py:51
  (98 other events, 1072.7 us)
Sparse Core Ops, SparseCore 0:
  10.8 36.5 all-gather.3
  51.2 37.4 all-gather.7
  116.5 77.7 all-gather.5
  399.8 20.3 reduce-scatter.6
  451.8 17.5 reduce-scatter.8
  471.7 64.5 reduce-scatter.14
  539.3 38.6 reduce-scatter.16
  580.8 21.1 reduce-scatter.12
  604.9 20.3 reduce-scatter.10

commit v2 on v1

--- a/solution.py
+++ b/solution.py
@@ -41,6 +41,10 @@
     return factor * gain * upstream - values * factor * factor * factor * inner_mean
 
 
+def tie(*values):
+    return lax.optimization_barrier(values)
+
+
 def across(value, mask):
     count = lax.axis_size("shard")
     return lax.ppermute(value, "shard", [(i, i ^ mask) for i in range(count)])
@@ -68,57 +72,151 @@
     )
 
 
-def gather_plane(value):
+def halve_column(value, line_place, during=()):
+    during = list(during)
+    lead = lax.axis_size("shard") // plane
+    held = value.reshape(lead, -1, value.shape[1])
+    size = lead // 2
+    done = 0
+    while size >= 1:
+        pair = held.reshape(2, size, *held.shape[1:])
+        mine = (line_place // size) % 2
+        kept = lax.dynamic_index_in_dim(pair, mine, axis=0, keepdims=False)
+        got = across(
+            lax.dynamic_index_in_dim(pair, 1 - mine, axis=0, keepdims=False), size * plane
+        )
+        if done < len(during):
+            got, *during[done] = tie(got, *during[done])
+            done += 1
+        held = (kept.astype(f32) + got.astype(f32)).astype(bf16)
+        size //= 2
+    return held[0], during
+
+
+def start_plane(value):
+    return across(value, 1), across(value, 2)
+
+
+def finish_plane(value, first, second):
     half = value.shape[0] // 2
-    first = across(value, 1)
-    second = across(value, 2)
     far_top = across(first[:half], 2)
     far_bottom = across(second[half:], 1)
     return value, first, second, far_top, far_bottom
 
 
-def place_plane(blocks, my_place):
-    own, first, second, far_top, far_bottom = blocks
-    lead, rows, width = own.shape
-    out = jnp.zeros((lead, plane, rows, width), own.dtype)
-    far = jnp.concatenate([far_top, far_bottom], axis=0)
-    for mask, block in enumerate((own, first, second, far)):
-        out = lax.dynamic_update_slice_in_dim(out, block[:, None], my_place ^ mask, axis=1)
-    return out
-
-
-def reduce_plane(x_send, x_keep, y_send, y_keep):
-    x_got = across(x_send.astype(bf16), 1).astype(f32)
-    y_got = across(y_send.astype(bf16), 2).astype(f32)
-    x_last = across((x_keep[1].astype(f32) + x_got[1]).astype(bf16), 2).astype(f32)
-    y_last = across((y_keep[1].astype(f32) + y_got[1]).astype(bf16), 1).astype(f32)
-    return (
-        x_keep[0].astype(f32) + x_got[0] + x_last,
-        y_keep[0].astype(f32) + y_got[0] + y_last,
-    )
-
-
-def pick(stack, index):
-    return lax.dynamic_index_in_dim(stack, index, axis=1, keepdims=False)
-
-
-def reduce_rows(grad, my_place):
-    count = lax.axis_size("shard")
-    rows = grad.shape[0] // count
-    lead = count // plane
-    blocks = grad.reshape(lead, plane, rows, -1)
-    parts = [pick(blocks, my_place ^ mask) for mask in range(plane)]
-    half = lead // 2
-    top = [part[:half] for part in parts]
-    low = [part[half:] for part in parts]
-    x_sum, y_sum = reduce_plane(
-        jnp.stack([top[1], top[3]]),
-        jnp.stack([top[0], top[2]]),
-        jnp.stack([low[2], low[3]]),
-        jnp.stack([low[0], low[1]]),
-    )
-    summed = jnp.concatenate([x_sum, y_sum], axis=0).astype(bf16)
-    return scatter_column(summed.reshape(lead * rows, -1))
+def gather_plane(value):
+    return finish_plane(value, *tie(*start_plane(value)))
+
+
+def place_kernel(place, own, first, second, far_top, far_bottom, out):
+    half = far_top.shape[0]
+    me = place[0]
+    out[:, pl.ds(me, 1)] = own[...][:, None]
+    out[:, pl.ds(me ^ 1, 1)] = first[...][:, None]
+    out[:, pl.ds(me ^ 2, 1)] = second[...][:, None]
+    out[:half, pl.ds(me ^ 3, 1)] = far_top[...][:, None]
+    out[half:, pl.ds(me ^ 3, 1)] = far_bottom[...][:, None]
+
+
+def place_plane(blocks, place):
+    lead, rows, width = blocks[0].shape
+    vmem = pl.BlockSpec(memory_space=pltpu.VMEM)
+    return pl.pallas_call(
+        place_kernel,
+        out_shape=jax.ShapeDtypeStruct((lead, plane, rows, width), blocks[0].dtype),
+        in_specs=[pl.BlockSpec(memory_space=pltpu.SMEM)] + [vmem] * 5,
+        out_specs=vmem,
+        cost_estimate=pl.CostEstimate(
+            flops=0, transcendentals=0, bytes_accessed=4 * plane * lead * rows * width
+        ),
+        name="place_plane",
+    )(place, *blocks)
+
+
+def unshuffle(pieces, place, unit):
+    rows, part = pieces[0].shape
+    lead = part // unit
+    vmem = pl.BlockSpec(memory_space=pltpu.VMEM)
+
+    def kernel(place, p0, p1, p2, p3, out, natural):
+        for mask, piece in enumerate((p0, p1, p2, p3)):
+            natural[pl.ds(place[0] ^ mask, 1)] = piece[...].astype(f32)[None]
+        columns = [
+            natural[member][:, a * unit : (a + 1) * unit]
+            for a in range(lead)
+            for member in range(plane)
+        ]
+        out[...] = jnp.concatenate(columns, axis=1).astype(bf16)
+
+    return pl.pallas_call(
+        kernel,
+        out_shape=jax.ShapeDtypeStruct((rows, plane * part), bf16),
+        in_specs=[pl.BlockSpec(memory_space=pltpu.SMEM)] + [vmem] * 4,
+        out_specs=vmem,
+        scratch_shapes=[pltpu.VMEM((plane, rows, part), f32)],
+        cost_estimate=pl.CostEstimate(
+            flops=0, transcendentals=0, bytes_accessed=4 * plane * rows * part
+        ),
+        name="unshuffle",
+    )(place, *pieces)
+
+
+def exchange_plane(x_send, x_keep, y_send, y_keep, during_first=(), during_second=()):
+    x_got = across(x_send.astype(bf16), 1)
+    y_got = across(y_send.astype(bf16), 2)
+    x_got, y_got, *during_first = tie(x_got, y_got, *during_first)
+    x_pass, y_pass = tie(
+        (x_keep[1].astype(f32) + x_got[1].astype(f32)).astype(bf16),
+        (y_keep[1].astype(f32) + y_got[0].astype(f32)).astype(bf16),
+    )
+    x_last = across(x_pass, 2)
+    y_last = across(y_pass, 1)
+    x_last, y_last, *during_second = tie(x_last, y_last, *during_second)
+    return x_got, x_last, y_got, y_last, during_first, during_second
+
+
+def split_kernel(place, own, got, x_send, x_keep, y_send, y_keep):
+    half = own.shape[0] // 2
+    for out, slot, mask, first in (
+        (x_send, 0, 1, 0),
+        (x_send, 1, 3, 0),
+        (x_keep, 0, 0, 0),
+        (x_keep, 1, 2, 0),
+        (y_send, 0, 3, half),
+        (y_send, 1, 2, half),
+        (y_keep, 0, 0, half),
+        (y_keep, 1, 1, half),
+    ):
+        at = (slice(first, first + half), pl.ds(place[0] ^ mask, 1))
+        out[slot] = (own[at].astype(f32) + got[at].astype(f32))[:, 0].astype(bf16)
+
+
+def split_rows(place, own, got, rows):
+    lead = own.shape[0] // (plane * rows)
+    shape = (lead, plane, rows, own.shape[1])
+    vmem = pl.BlockSpec(memory_space=pltpu.VMEM)
+    sent = jax.ShapeDtypeStruct((2, lead // 2, rows, own.shape[1]), bf16)
+    return pl.pallas_call(
+        split_kernel,
+        out_shape=(sent,) * 4,
+        in_specs=[pl.BlockSpec(memory_space=pltpu.SMEM), vmem, vmem],
+        out_specs=(vmem,) * 4,
+        cost_estimate=pl.CostEstimate(
+            flops=own.size, transcendentals=0, bytes_accessed=6 * own.size
+        ),
+        compiler_params=pltpu.CompilerParams(vmem_limit_bytes=56 * 2**20),
+        name="split_rows",
+    )(place, own.reshape(shape), got.reshape(shape))
+
+
+def joined(x_keep, x_got, x_last, y_keep, y_got, y_last, axis):
+    return jnp.concatenate(
+        [
+            x_keep[0].astype(f32) + x_got[0].astype(f32) + x_last.astype(f32),
+            y_keep[0].astype(f32) + y_got[1].astype(f32) + y_last.astype(f32),
+        ],
+        axis=axis,
+    ).astype(bf16)
 
 
 def window_mask(info, dims, micro, piece):
@@ -274,8 +372,8 @@
     for mask, k_out, k_at, v_out, v_at in (
         (0, kx_keep, 0, vy_keep, 0),
         (1, kx_send, 0, vy_keep, 1),
-        (2, kx_keep, 1, vy_send, 0),
-        (3, kx_send, 1, vy_send, 1),
+        (2, kx_keep, 1, vy_send, 1),
+        (3, kx_send, 1, vy_send, 0),
     ):
         member = info[0] ^ mask
 
@@ -333,6 +431,221 @@
         name="attend_backward",
     )
     return forward, backward
+
+
+def outproj_kernel(core, att, own, other, tokens, gain, residual, normed):
+    half = own.shape[1]
+    columns = (pl.ds(pl.multiple_of(core[0] * half, 128), half), pl.ds(pl.multiple_of((1 - core[0]) * half, 128), half))
+    rows = att[...]
+    for weight, cols in zip((own, other), columns):
+        residual[:, cols] = product(rows, weight[...])
+    total = residual[...] + tokens[...].astype(f32)
+    residual[...] = total
+    normed[...] = (total * rms_factor(total) * gain[...]).astype(bf16)
+
+
+def outproj_norm(core, attended, own, other, tokens, gain):
+    rows, width = tokens.shape
+    vmem = pl.BlockSpec(memory_space=pltpu.VMEM)
+    shape = jax.ShapeDtypeStruct
+    return pl.pallas_call(
+        outproj_kernel,
+        out_shape=(shape((rows, width), f32), shape((rows, width), bf16)),
+        in_specs=[pl.BlockSpec(memory_space=pltpu.SMEM)] + [vmem] * 5,
+        out_specs=(vmem, vmem),
+        cost_estimate=pl.CostEstimate(
+            flops=2 * rows * width * attended.shape[1],
+            transcendentals=0,
+            bytes_accessed=2 * width * attended.shape[1] + 10 * rows * width,
+        ),
+        compiler_params=pltpu.CompilerParams(vmem_limit_bytes=56 * 2**20),
+        name="outproj_norm",
+    )(core, attended, own, other, tokens, gain)
+
+
+def feed_kernel(
+    core, h0, h1, h2, h3, h4, c0, c1, c2, c3, c4, w_own, w_other, d_own, d_other,
+    h_all, c_all, hidden, g_own, g_other, x_send, x_keep, y_send, y_keep, total,
+):
+    rows = h0.shape[0]
+    cut = rows // 2
+    for out, blocks in ((h_all, (h0, h1, h3, h4, h2)), (c_all, (c0, c1, c3, c4, c2))):
+        at = 0
+        for block in blocks:
+            out[at : at + block.shape[0], :] = block[...]
+            at += block.shape[0]
+    half = d_own.shape[1]
+    part = hidden.shape[1]
+    step = 384 if part % 384 == 0 else part
+    is_first = core[0] == 0
+    mine = pl.ds(pl.multiple_of(core[0] * half, 128), half)
+    theirs = pl.ds(pl.multiple_of((1 - core[0]) * half, 128), half)
+    root = math.sqrt(2.0 / math.pi)
+
+    def block(index, carry):
+        at = pl.ds(pl.multiple_of(index * rows, 16), rows)
+        tokens = h_all[at, :]
+        up_mine = c_all[at, mine]
+        up_theirs = c_all[at, theirs]
+        for first in range(0, part, step):
+            cols = slice(first, first + step)
+            pre_own = product(tokens, w_own[:, cols])
+            pre_other = product(tokens, w_other[:, cols])
+            gate = jnp.where(is_first, pre_own, pre_other)
+            upward = jnp.where(is_first, pre_other, pre_own)
+            grad = product_nt(up_mine, d_own[cols, :]) + product_nt(up_theirs, d_other[cols, :])
+            square = gate * gate
+            curve = jnp.tanh(root * gate * (1.0 + 0.044715 * square))
+            lift = 0.5 * (1.0 + curve)
+            active = gate * lift
+            slope = lift + (0.5 * root) * gate * (1.0 - curve * curve) * (
+                1.0 + (3 * 0.044715) * square
+            )
+            hidden[at, cols] = (active * upward).astype(bf16)
+            grad_gate = grad * upward * slope
+            grad_up = grad * active
+            mine_in = jnp.where(is_first, grad_gate, grad_up).astype(bf16)
+            theirs_in = jnp.where(is_first, grad_up, grad_gate).astype(bf16)
+            g_own[at, cols] = mine_in
+            g_other[at, cols] = theirs_in
+            back = product_nt(mine_in, w_own[:, cols]) + product_nt(theirs_in, w_other[:, cols])
+            if first == 0:
+                total[at, :] = back
+            else:
+                total[at, :] += back
+        return carry
+
+    lax.fori_loop(0, plane, block, 0)
+    width = total.shape[1] // 2
+    for out, slot, member in (
+        (x_keep, 0, 0), (x_send, 0, 1), (x_send, 1, 2), (x_keep, 1, 3),
+    ):
+        out[slot] = total[member * rows : (member + 1) * rows, :width].astype(bf16)
+    for out, slot, member in (
+        (y_keep, 0, 0), (y_keep, 1, 1), (y_send, 0, 2), (y_send, 1, 3),
+    ):
+        out[slot] = total[member * rows : (member + 1) * rows, width:].astype(bf16)
+
+
+def feed_forward(core, h_blocks, c_blocks, w_own, w_other, d_own, d_other):
+    rows, width = h_blocks[0].shape
+    part = w_own.shape[1]
+    count = plane * rows
+    vmem = pl.BlockSpec(memory_space=pltpu.VMEM)
+    shape = jax.ShapeDtypeStruct
+    wide = shape((count, part), bf16)
+    sent = shape((2, rows, width // 2), bf16)
+    return pl.pallas_call(
+        feed_kernel,
+        out_shape=(shape((count, width), bf16),) * 2 + (wide,) * 3 + (sent,) * 4,
+        in_specs=[pl.BlockSpec(memory_space=pltpu.SMEM)] + [vmem] * 14,
+        out_specs=(vmem,) * 9,
+        scratch_shapes=[pltpu.VMEM((count, width), f32)],
+        cost_estimate=pl.CostEstimate(
+            flops=10 * count * width * part,
+            transcendentals=count * part,
+            bytes_accessed=8 * width * part + 12 * count * part,
+        ),
+        compiler_params=pltpu.CompilerParams(vmem_limit_bytes=58 * 2**20),
+        name="feed_forward",
+    )(core, *h_blocks, *c_blocks, w_own, w_other, d_own, d_other)
+
+
+def norm_two_kernel(
+    core, x_keep, x_got, x_last, y_keep, y_got, y_last, residual, up, gain, own, other,
+    grad_out, attn, mixed, grad_gain,
+):
+    width = x_last.shape[1]
+    half = own.shape[1]
+    mine = pl.ds(pl.multiple_of(core[0] * half, 128), half)
+    theirs = pl.ds(pl.multiple_of((1 - core[0]) * half, 128), half)
+    upstream = jnp.concatenate(
+        [
+            x_keep[0].astype(f32) + x_got[0].astype(f32) + x_last[...].astype(f32),
+            y_keep[0].astype(f32) + y_got[1].astype(f32) + y_last[...].astype(f32),
+        ],
+        axis=1,
+    )
+    values = residual[...]
+    factor = rms_factor(values)
+    grad_gain[...] = jnp.sum(upstream * values * factor, axis=0, keepdims=True)
+    total = up[...].astype(f32) + norm_backward(values, factor, gain[...], upstream)
+    grad_out[...] = total
+    attn[...] = total.astype(bf16)
+    mixed[...] = (
+        product_nt(attn[:, mine], own[...]) + product_nt(attn[:, theirs], other[...])
+    ).astype(bf16)
+
+
+def norm_two_backward(core, sums, residual, up, gain, own, other):
+    rows, width = residual.shape
+    vmem = pl.BlockSpec(memory_space=pltpu.VMEM)
+    shape = jax.ShapeDtypeStruct
+    return pl.pallas_call(
+        norm_two_kernel,
+        out_shape=(
+            shape((rows, width), f32),
+            shape((rows, width), bf16),
+            shape((rows, own.shape[0]), bf16),
+            shape((1, width), f32),
+        ),
+        in_specs=[pl.BlockSpec(memory_space=pltpu.SMEM)] + [vmem] * 11,
+        out_specs=(vmem,) * 4,
+        cost_estimate=pl.CostEstimate(
+            flops=2 * rows * width * own.shape[0],
+            transcendentals=0,
+            bytes_accessed=2 * width * own.shape[0] + 20 * rows * width,
+        ),
+        compiler_params=pltpu.CompilerParams(vmem_limit_bytes=56 * 2**20),
+        name="norm_two_backward",
+    )(core, *sums, residual, up, gain, own, other)
+
+
+def input_kernel(
+    core, partial, dkv, kv_own, kv_other, normed, tokens, gain, other_gain, grad_resid,
+    grad_input, last_own, last_other,
+):
+    head = kv_own.shape[1]
+    mine = pl.ds(pl.multiple_of(core[0] * head, 128), head)
+    theirs = pl.ds(pl.multiple_of((1 - core[0]) * head, 128), head)
+    is_first = core[0] == 0
+    upstream = (
+        partial[...]
+        + product_nt(dkv[:, mine], kv_own[...])
+        + product_nt(dkv[:, theirs], kv_other[...])
+    )
+    values = tokens[...].astype(f32)
+    factor = rms_factor(values)
+    grad_gain = jnp.sum(upstream * values * factor, axis=0, keepdims=True)
+    grad_input[...] = (
+        grad_resid[...] + norm_backward(values, factor, gain[...], upstream)
+    ).astype(bf16)
+    kept = jnp.where(is_first, grad_gain, other_gain[...])
+    given = jnp.where(is_first, other_gain[...], grad_gain)
+    width = kept.shape[1]
+    for out, cols, row in ((last_own, mine, kept), (last_other, theirs, given)):
+        out[:, :head] = product_tn(normed[...], dkv[:, cols]).astype(bf16)
+        out[:, head:] = jnp.broadcast_to(row, (128, width)).T.astype(bf16)
+
+
+def input_backward(core, partial, dkv, kv_own, kv_other, normed, tokens, gain, other_gain, grad_resid):
+    rows, width = tokens.shape
+    vmem = pl.BlockSpec(memory_space=pltpu.VMEM)
+    shape = jax.ShapeDtypeStruct
+    last = shape((width, kv_own.shape[1] + 128), bf16)
+    return pl.pallas_call(
+        input_kernel,
+        out_shape=(shape((rows, width), bf16), last, last),
+        in_specs=[pl.BlockSpec(memory_space=pltpu.SMEM)] + [vmem] * 9,
+        out_specs=(vmem,) * 3,
+        cost_estimate=pl.CostEstimate(
+            flops=8 * rows * width * kv_own.shape[1],
+            transcendentals=0,
+            bytes_accessed=16 * rows * width,
+        ),
+        compiler_params=pltpu.CompilerParams(vmem_limit_bytes=56 * 2**20),
+        name="input_backward",
+    )(core, partial, dkv, kv_own, kv_other, normed, tokens, gain, other_gain, grad_resid)
 
 
 def on_device(
@@ -384,23 +697,25 @@
             lax.dynamic_slice_in_dim(value, (1 - core) * size, size, 1),
         )
 
+    place = jnp.stack([my_place, my_index]).astype(jnp.int32)
+
+    def by_lead(value):
+        return value.reshape(lead, my_rows, -1)
+
+    def plane_weight(blocks):
+        return place_plane(blocks, place).reshape(feat, -1)
+
+    qo_line = gather_column(
+        jnp.concatenate([halves(query_weight)[0], halves(outproj_weight)[0]], axis=1)
+    )
     gain_cols = jnp.pad(jnp.stack([gain_one, gain_two], axis=1), ((0, 0), (0, 126)))
-    qkv_mine = jnp.concatenate(
-        [halves(query_weight)[0], halves(keyval_weight)[0], gain_cols], axis=1
-    )
-    out_mine = halves(outproj_weight)[0]
-    attn_w = gather_column(jnp.concatenate([qkv_mine, out_mine], axis=1))
-    attn_blocks = gather_plane(attn_w.reshape(lead, my_rows, -1))
-    attn_own = place_plane(attn_blocks, my_place).reshape(feat, -1)
-    attn_other = peer(attn_own)
-    cut = half_w + head_size
-    qkv_own, qkv_other = attn_own[:, :cut], attn_other[:, :cut]
-    out_own, out_other = attn_own[:, cut + 128 :], attn_other[:, cut + 128 :]
-    gains = attn_own[:, cut : cut + 2].T
-    full_gain_one = gains[0].astype(f32)
-    full_gain_two = gains[1].astype(f32)
-
+    kv_mine = jnp.concatenate([halves(keyval_weight)[0], gain_cols], axis=1)
+    kv_line = gather_column(kv_mine)
+    upstream = cotangent.reshape(token_count, feat)
     gate_or_up = jnp.where(first_core, gate_weight, up_weight)
+    up_first, up_second, kv_line, gate_or_up = tie(
+        *start_plane(upstream), by_lead(kv_line), gate_or_up
+    )
     pieces_out = jnp.transpose(
         gate_or_up.reshape(my_rows, lead, plane, my_hidden), (2, 0, 1, 3)
     ).reshape(plane, my_rows, part)
@@ -409,19 +724,38 @@
         block = lax.dynamic_index_in_dim(pieces_out, my_place ^ mask, axis=0, keepdims=True)
         block = block if mask == 0 else across(block, mask)
         wide_in = lax.dynamic_update_slice_in_dim(wide_in, block, my_place ^ mask, axis=0)
-    wide_own = gather_column(wide_in.reshape(plane * my_rows, part))
-    down_own = gather_column(halves(down_weight)[0])
-    wide_other = peer(wide_own)
-    down_other = peer(down_own)
+    kv_own = plane_weight(gather_plane(kv_line))
+    kv_own, qo_line = tie(kv_own, qo_line)
+    query_line, out_line = by_lead(qo_line[:, :half_w]), by_lead(qo_line[:, half_w:])
+    query_first, query_second = start_plane(query_line)
+    out_first, out_second = start_plane(out_line)
+    kv_other = peer(kv_own)
+    gains = kv_own[:, head_size : head_size + 2].T
+    kv_own, kv_other = kv_own[:, :head_size], kv_other[:, :head_size]
+    full_gain_one = gains[0].astype(f32)
+    full_gain_two = gains[1].astype(f32)
 
     stream = tokens.reshape(token_count, feat).astype(f32)
     factor_one = rms_factor(stream)
     normed_one = (stream * factor_one * full_gain_one).astype(bf16)
-    mixed_own = product(normed_one, qkv_own).astype(bf16)
-    mixed_other = product(normed_one, qkv_other).astype(bf16)
-    queries = in_order(mixed_own[:, :half_w], mixed_other[:, :half_w])
-    keyvals = in_order(mixed_own[:, half_w:], mixed_other[:, half_w:])
-    kv_blocks = gather_plane(gather_column(keyvals))
+    keyvals = in_order(product(normed_one, kv_own), product(normed_one, kv_other)).astype(bf16)
+    keyvals, wide_in = tie(keyvals, wide_in)
+    wide_own = gather_column(wide_in.reshape(plane * my_rows, part))
+    down_own = gather_column(halves(down_weight)[0])
+    keyvals_line, query_first, query_second, out_first, out_second = tie(
+        gather_column(keyvals), query_first, query_second, out_first, out_second
+    )
+    query_blocks = finish_plane(query_line, query_first, query_second)
+    key_first, key_second, *query_blocks = tie(*start_plane(keyvals_line), *query_blocks)
+    query_own = plane_weight(query_blocks)
+    kv_blocks = finish_plane(keyvals_line, key_first, key_second)
+    out_blocks = finish_plane(out_line, out_first, out_second)
+    *blocks, query_own = tie(*kv_blocks, *out_blocks, query_own)
+    kv_blocks, out_blocks = blocks[:5], blocks[5:]
+    out_own = plane_weight(out_blocks)
+    query_other = peer(query_own)
+    out_other = peer(out_own)
+    queries = in_order(product(normed_one, query_own), product(normed_one, query_other)).astype(bf16)
     forward, backward = attention_calls(
         micro_count,
         piece_count,
@@ -432,116 +766,139 @@
         lengths.shape[-1],
         lead * token_count,
     )
-    info = jnp.concatenate(
-        [
-            jnp.stack([my_place, my_index]).astype(jnp.int32),
-            lengths.reshape(-1).astype(jnp.int32),
-        ]
-    )
+    info = jnp.concatenate([place, lengths.reshape(-1).astype(jnp.int32)])
     attended, logsum = forward(info, queries, *kv_blocks)
-    residual = stream + in_order(product(attended, out_own), product(attended, out_other))
-    factor_two = rms_factor(residual)
-    normed_two = (residual * factor_two * full_gain_two).astype(bf16)
-
-    def plane_tokens(value):
-        own, first, second, far_top, far_bottom = gather_plane(value)
-        return jnp.concatenate([own, first, far_top, far_bottom, second], axis=0)
-
-    upstream = cotangent.reshape(token_count, feat)
-    all_up = plane_tokens(upstream)
-    all_normed = plane_tokens(normed_two)
-    pre_own = product(all_normed, wide_own)
-    pre_other = product(all_normed, wide_other)
-    gate_pre = jnp.where(first_core, pre_own, pre_other)
-    upward = jnp.where(first_core, pre_other, pre_own)
-    root = math.sqrt(2.0 / math.pi)
-    curve = jnp.tanh(root * (gate_pre + 0.044715 * gate_pre * gate_pre * gate_pre))
-    active = 0.5 * gate_pre * (1.0 + curve)
-    slope = 0.5 * (1.0 + curve) + 0.5 * gate_pre * (1.0 - curve * curve) * root * (
-        1.0 + 3 * 0.044715 * gate_pre * gate_pre
-    )
-    hidden = (active * upward).astype(bf16)
+    attended, *up_blocks = tie(attended, *finish_plane(upstream, up_first, up_second))
+    core_info = core.astype(jnp.int32).reshape(1)
+    gain_two_row = full_gain_two.reshape(1, feat)
+    residual, normed_two = outproj_norm(
+        core_info,
+        attended,
+        out_own,
+        out_other,
+        tokens.reshape(token_count, feat),
+        gain_two_row,
+    )
+
+    normed_first, normed_second, wide_own, down_own = tie(
+        *start_plane(normed_two), wide_own, down_own
+    )
+    normed_blocks = finish_plane(normed_two, normed_first, normed_second)
+    wide_other = peer(wide_own)
+    down_other = peer(down_own)
+    all_normed, all_up, hidden, grad_own_in, grad_other_in, *sums = feed_forward(
+        core_info, normed_blocks, up_blocks, wide_own, wide_other, down_own, down_other
+    )
     up_own, up_other = halves(all_up)
-    grad_hidden = product_nt(up_own, down_own) + product_nt(up_other, down_other)
-    grad_gate_in = (grad_hidden * upward * slope).astype(bf16)
-    grad_up_in = (grad_hidden * active).astype(bf16)
-    grad_own_in = jnp.where(first_core, grad_gate_in, grad_up_in)
-    grad_other_in = jnp.where(first_core, grad_up_in, grad_gate_in)
-
-    def token_sum(first_half, second_half):
-        one = first_half.astype(bf16).reshape(plane, token_count, -1)
-        two = second_half.astype(bf16).reshape(plane, token_count, -1)
-        return reduce_plane(
-            one[1:3], (one[0], one[3]), jnp.stack([two[3], two[2]]), (two[0], two[1])
-        )
-
-    out_sum = token_sum(product(hidden, down_own), product(hidden, down_other))
-    block_output = (residual + in_order(*out_sum)).astype(bf16).reshape(tokens.shape)
-    grad_wide = product_nt(grad_own_in, wide_own) + product_nt(grad_other_in, wide_other)
-    grad_normed_two = jnp.concatenate(
-        token_sum(grad_wide[:, :half_d], grad_wide[:, half_d:]), axis=1
-    )
 
     def chip_sum(own, other):
-        return (own + peer(other.astype(bf16)).astype(f32)).astype(bf16)
-
-    down_grad = scatter_column(
-        chip_sum(product_tn(hidden, up_own), product_tn(hidden, up_other))
-    )
-    wide_grad = scatter_column(
-        chip_sum(product_tn(all_normed, grad_own_in), product_tn(all_normed, grad_other_in))
-    ).reshape(plane, my_rows, part)
-    wide_back = jnp.zeros((plane, my_rows, part), bf16)
-    for mask in range(plane):
-        block = lax.dynamic_index_in_dim(wide_grad, my_place ^ mask, axis=0, keepdims=True)
-        block = block if mask == 0 else across(block, mask)
-        wide_back = lax.dynamic_update_slice_in_dim(wide_back, block, my_place ^ mask, axis=0)
-    wide_share = jnp.transpose(
-        wide_back.reshape(plane, my_rows, lead, my_hidden), (1, 2, 0, 3)
-    ).reshape(my_rows, hidden_width)
-
-    grad_gain_two = jnp.sum(grad_normed_two * residual * factor_two, axis=0)
-    grad_resid = upstream.astype(f32) + norm_backward(
-        residual, factor_two, full_gain_two, grad_normed_two
-    )
-    grad_attn = grad_resid.astype(bf16)
-    attn_own_half, attn_other_half = halves(grad_attn)
-    outproj_share = reduce_rows(
-        chip_sum(product_tn(attended, attn_own_half), product_tn(attended, attn_other_half)),
-        my_place,
-    )
-    grad_mixed = (
-        product_nt(attn_own_half, out_own) + product_nt(attn_other_half, out_other)
-    ).astype(bf16)
+        return (own.astype(f32) + peer(other.astype(bf16)).astype(f32)).astype(bf16)
+
+    wide_peer = product_tn(all_normed, grad_other_in).astype(bf16)
+    wide_mine = product_tn(all_normed, grad_own_in).astype(bf16)
+    out_mine = product(hidden, down_own).astype(bf16)
+    out_peer = product(hidden, down_other).astype(bf16)
+    x_send, x_keep, y_send, y_keep = sums
+    x_got, x_last, y_got, y_last, during_first, during_second = exchange_plane(
+        x_send,
+        x_keep,
+        y_send,
+        y_keep,
+        (wide_mine, wide_peer),
+        (
+            out_mine,
+            out_peer,
+            product_tn(hidden, up_own).astype(bf16),
+            product_tn(hidden, up_other).astype(bf16),
+        ),
+    )
+    out_mine, out_peer, *down_parts = during_second
+    wide_grad = scatter_column(chip_sum(*during_first))
+    down_grad = scatter_column(chip_sum(*down_parts))
+    grad_resid, grad_attn, grad_mixed, grad_gain_two = norm_two_backward(
+        core_info,
+        (x_keep, x_got, x_last, y_keep, y_got, y_last),
+        residual,
+        upstream,
+        gain_two_row,
+        out_own,
+        out_other,
+    )
+
+    one = out_mine.reshape(plane, token_count, -1)
+    two = out_peer.reshape(plane, token_count, -1)
+    out_parts = (one[1:3], (one[0], one[3]), two[2:4], (two[0], two[1]))
     grad_queries, kx_send, kx_keep, vy_send, vy_keep = backward(
         info, queries, grad_mixed, logsum, *kv_blocks
     )
-    grad_kv = jnp.concatenate(reduce_plane(kx_send, kx_keep, vy_send, vy_keep), axis=1)
-    grad_keyvals = scatter_column(grad_kv.astype(bf16))
+    out_x, out_x_last, out_y, out_y_last, kernel_out, _ = exchange_plane(
+        *out_parts, (grad_queries, kx_send, kx_keep, vy_send, vy_keep, grad_attn)
+    )
+    grad_queries, kx_send, kx_keep, vy_send, vy_keep, grad_attn = kernel_out
+    out_sum = (
+        one[0].astype(f32) + out_x[0].astype(f32) + out_x_last.astype(f32),
+        two[0].astype(f32) + out_y[1].astype(f32) + out_y_last.astype(f32),
+    )
+    block_output = (residual + in_order(*out_sum)).astype(bf16).reshape(tokens.shape)
+
     dq_own, dq_other = halves(grad_queries)
-    dkv_own, dkv_other = halves(grad_keyvals)
-    query_share = reduce_rows(
-        chip_sum(product_tn(normed_one, dq_own), product_tn(normed_one, dq_other)), my_place
-    )
-    dqkv_own = jnp.concatenate([dq_own, dkv_own], axis=1)
-    dqkv_other = jnp.concatenate([dq_other, dkv_other], axis=1)
-    grad_normed_one = product_nt(dqkv_own, qkv_own) + product_nt(dqkv_other, qkv_other)
-    grad_gain_one = jnp.sum(grad_normed_one * stream * factor_one, axis=0)
-    grad_stream = grad_resid + norm_backward(stream, factor_one, full_gain_one, grad_normed_one)
-    input_grad = grad_stream.astype(bf16).reshape(tokens.shape)
-
-    def as_column(value):
-        return jnp.broadcast_to(value[:, None], (feat, 128))
-
-    gain_own = as_column(jnp.where(first_core, grad_gain_one, grad_gain_two))
-    gain_other = as_column(jnp.where(first_core, grad_gain_two, grad_gain_one))
-    last_share = reduce_rows(
-        chip_sum(
-            jnp.concatenate([product_tn(normed_one, dkv_own), gain_own], axis=1),
-            jnp.concatenate([product_tn(normed_one, dkv_other), gain_other], axis=1),
-        ),
-        my_place,
-    )
+    da_own, da_other = halves(grad_attn)
+    attn_mine = product_tn(attended, da_own).astype(bf16)
+    attn_peer = peer(product_tn(attended, da_other).astype(bf16))
+    kx_got, kx_last, vy_got, vy_last, attn_parts, query_parts = exchange_plane(
+        kx_send,
+        kx_keep,
+        vy_send,
+        vy_keep,
+        (attn_mine, attn_peer),
+        (
+            product_tn(normed_one, dq_own).astype(bf16),
+            product_tn(normed_one, dq_other).astype(bf16),
+        ),
+    )
+    grad_kv, wide_grad = tie(
+        joined(kx_keep, kx_got, kx_last, vy_keep, vy_got, vy_last, 1), wide_grad
+    )
+    attn_split = split_rows(place, *attn_parts, my_rows)
+    query_split = split_rows(place, query_parts[0], peer(query_parts[1]), my_rows)
+    partial = product_nt(dq_own, query_own) + product_nt(dq_other, query_other)
+    grad_keyvals, (attn_split, query_split) = halve_column(
+        grad_kv, my_index // plane, (attn_split, (*query_split, partial))
+    )
+    *query_split, partial = query_split
+    wide_grad = wide_grad.reshape(plane, my_rows, part)
+
+    def plane_rows(x_send, x_keep, y_send, y_keep):
+        x_got, x_last, y_got, y_last, _, _ = exchange_plane(x_send, x_keep, y_send, y_keep)
+        total = joined(x_keep, x_got, x_last, y_keep, y_got, y_last, 0)
+        return total.reshape(lead * my_rows, -1)
+
+    attn_plane = plane_rows(*attn_split)
+    query_plane = plane_rows(*query_split)
+    input_grad, last_own, last_other = input_backward(
+        core_info,
+        partial,
+        grad_keyvals,
+        kv_own,
+        kv_other,
+        normed_one,
+        tokens.reshape(token_count, feat),
+        full_gain_one.reshape(1, feat),
+        grad_gain_two,
+        grad_resid,
+    )
+    input_grad = input_grad.reshape(tokens.shape)
+    last_plane = plane_rows(*split_rows(place, last_own, peer(last_other), my_rows))
+    last_plane, down_grad = tie(last_plane, down_grad)
+    last_share = scatter_column(
+        jnp.concatenate([query_plane, attn_plane, last_plane], axis=1)
+    )
+
+    wide_back = []
+    for mask in range(plane):
+        block = lax.dynamic_index_in_dim(wide_grad, my_place ^ mask, axis=0, keepdims=False)
+        wide_back.append(block if mask == 0 else across(block, mask))
+    wide_share = unshuffle(wide_back, place, my_hidden)
 
     def whole(share):
         total = share
@@ -555,9 +912,10 @@
 
     wide_one, wide_two = whole(wide_share)
     down_pair = whole(down_grad)
-    out_pair = whole(outproj_share)
-    query_pair = whole(query_share)
-    last_one, last_two = whole(last_share)
+    last_pair = whole(last_share)
+    query_pair = [share[:, :half_w] for share in last_pair]
+    out_pair = [share[:, half_w : half_w + half_d] for share in last_pair]
+    last_one, last_two = [share[:, half_w + half_d :] for share in last_pair]
     return (
         block_output,
         input_grad,

time: 648 us -> 467 us (0.72)
  waiting for transfers between devices: 316 us -> 122 us
  Pallas kernels: 32.3 us -> 113 us
  matrix products: 109 us -> 47.9 us
  blocking collectives: 22.9 us -> 38.5 us
  local copies, waits for them, and re-layouts: 44.9 us -> 30.3 us
  other arithmetic: 40.7 us -> 29.6 us
    pallas_call x0 -> x11, Pallas kernels: none -> 80 us  [the longest x1 37.8 us: feed_forward(): pl.pallas_call(feed_kernel, out_shape=(shape((count, width), bf16),) * 2...]
    ppermute x46 -> x56, waiting for transfers between devices: 187 us -> 109 us  [across(): return lax.ppermute(value, 'shard', [(i, i ^ mask) for i in range(count)])]
    reduce_scatter x6 -> x3, waiting for transfers between devices: 70 us -> 5.38 us  [scatter_column(): lax.psum_scatter(value, 'shard', scatter_dimension=0, tiled=True, axis_in...]
    all_gather x3, waiting for transfers between devices: 58.4 us -> 0.01 us  [gather_column(): lax.all_gather(value, 'shard', axis=0, tiled=True, axis_index_groups=colu...]
    dot_general x8 -> x2, matrix products: 42.8 us -> 7.06 us  [product_nt(): lax.dot_general(first_op, second_op, (((1,), (1,)), ((), ())), preferred_...]
    dot_general x8 -> x6, matrix products: 28.8 us -> 8.32 us  [product(): return jnp.dot(first_op, second_op, preferred_element_type=f32)]
    all_gather x1 -> x2, blocking collectives: 22.9 us -> 38.5 us  [gather_column(): lax.all_gather(value, 'shard', axis=0, tiled=True, axis_index_groups=colu...]
    ppermute x13, waiting for transfers between devices: 0.44 us -> 7.78 us  [peer(): return lax.ppermute(value, 'grp', [(i, i ^ 1) for i in range(count)])]
  transfers between devices with their start and end apart: 68 -> 75, of which waited for: 34 -> 36; matrix products, arithmetic and copies ran while one was open for 23% -> 20% of each run, Pallas kernels for 2% -> 16%
where the time goes in v2:
time: 467 us; the launch traced here: 459 us
  waiting for transfers between devices  122 us (26%)
  Pallas kernels  113 us (24%)
  starting transfers between devices  61.7 us (13%)
  matrix products  47.9 us (10%)
  blocking collectives  38.5 us (8%)
  local copies, waits for them, and re-layouts  30.3 us (6%)
  other arithmetic  29.6 us (6%)
  between operations  15.8 us (3%)
    ppermute x56, waiting for transfers between devices, across(): return lax.ppermute(value, 'shard', [(i, i ^ mask) for i in range(count)])  109 us
    ppermute x56, starting transfers between devices, across(): return lax.ppermute(value, 'shard', [(i, i ^ mask) for i in range(count)])  59.4 us
    all_gather x2, blocking collectives, gather_column(): lax.all_gather(value, 'shard', axis=0, tiled=True, axis_index_groups=colu...  38.5 us
    pallas_call x1, Pallas kernels, feed_forward(): pl.pallas_call(feed_kernel, out_shape=(shape((count, width), bf16),) * 2...  37.8 us
    dot_general x8, matrix products, product_tn(): lax.dot_general(first_op, second_op, (((0,), (0,)), ((), ())), preferred_...  32.5 us
    pallas_call x1, Pallas kernels, on_device(): backward(info, queries, grad_mixed, logsum, *kv_blocks)  19.9 us
    pallas_call x1, Pallas kernels, on_device(): attended, logsum = forward(info, queries, *kv_blocks)  12.7 us
    pallas_call x3, Pallas kernels, split_rows(): pl.pallas_call(split_kernel, out_shape=(sent,) * 4, in_specs=[pl.BlockSpe...  11.1 us
  transfers between devices with their start and end apart: 75, of which 36 were waited for; matrix products, arithmetic and copies ran while one was open for 20% of the time, Pallas kernels for 16%

profile of v2, /device:TPU:0, one launch (start us, length us, event | category | flops | bytes accessed | tf_op | source)
XLA Modules:
  0.0 458.9 jit_solution(9652190187357823014)
XLA Ops:
  16.2 15.7 %all_gather.15 = bf16[384,256]{1,0:T(8,128)(2,1)} all-gather(bf16[96,256]{1,0:T(8,128)(2,1)S(1)} %copy.39), channel_id=1, replica_groups={{0,4,8,12},{1,5,9,13},{2,6,10,14},{3,7,11,15},{16,20,24,28},{17,21,25,2..., dimensions={0}, use_global_device_ids=true | all-gather | bytes 245760 | tf_op jit(solution)/shard_map/all_gather | solution.py:64
  49.3 5.8 %collective-permute-done.8 = bf16[1,96,1152]{2,1,0:T(8,128)(2,1)S(1)} collective-permute-done((bf16[1,96,1152]{2,1,0:T(8,128)(2,1)S(1)}, bf16[1,96,1152]{2,1,0:T(8,128)(2,1)S(1)}, u32[]{:S(2)}, u32[]{:S(2)}) %collective-permute-start.8) | collective-permute-done | bytes 221216 | tf_op jit(solution)/shard_map/ppermute | solution.py:50
  69.7 22.8 %all_gather.17.k0 = bf16[1024,256]{1,0:T(8,128)(2,1)S(1)} all-gather(bf16[256,256]{1,0:T(8,128)(2,1)S(1)} %fusion.31), channel_id=1, replica_groups={{0,4,8,12},{1,5,9,13},{2,6,10,14},{3,7,11,15},{16,20,24,28},{17,21,25,2..., dimensions={0}, use_global_device_ids=true | all-gather | bytes 655360 | tf_op jit(solution)/shard_map/all_gather | solution.py:64
  101.3 13.1 %collective-permute-done.17.far_bottom = bf16[2,96,768]{2,1,0:T(8,128)(2,1)S(1)} collective-permute-done((bf16[2,96,768]{2,1,0:T(8,128)(2,1)S(1)}, bf16[2,96,768]{2,1,0:T(8,128)(2,1)S(1)}, u32[]{:S(2)}, u32[]{:S(2)}) %collective-permute-start.17) | collective-permute-done | bytes 294944 | tf_op jit(solution)/shard_map/ppermute | solution.py:50
  139.2 12.7 %attend_forward.1 = (bf16[256,1536]{1,0:T(8,128)(2,1)}, f32[4,768,1]{2,1,0:T(8,128)}) custom-call(s32[6]{0:T(128)} %pad_add_fusion.info, bf16[256,1536]{1,0:T(8,128)(2,1)} %fusion.q_ref, bf16[1024,256]{1,0:T(8,128)(2,1)} %copy-done.37, bf16[1024,256]{1,0:T(8,128)(2,1)} %copy-done.58, bf16[1024,256]{1,0:T(8,128)(2,1)} %copy-done.57, ...), custom_call_target="tpu_custom_call" | custom-call | flops 1811939328 | bytes 4194304 | tf_op jit(solution)/shard_map/attend_forward/pallas_call | solution.py:770
  151.9 6.1 %outproj_norm.1 = (f32[256,1536]{1,0:T(8,128)}, bf16[256,1536]{1,0:T(8,128)(2,1)}) custom-call(s32[1]{0:T(128)} %bitcast.core, bf16[256,1536]{1,0:T(8,128)(2,1)} %get-tuple-element.185.att, bf16[1536,768]{1,0:T(8,128)(2,1)} %bitcast.137, bf16[1536,768]{1,0:T(8,128)(2,1)} %collective-permute-done.25.other, bf16[256,1536]{1,0:T(8,128)(2,1)} %bitcast.141, ...), custom_call_target="tpu_custom_call" | custom-call | flops 1207959552 | bytes 8650752 | tf_op jit(solution)/shard_map/outproj_norm/pallas_call | solution.py:451
  160.2 17.1 %collective-permute-done.27.h2 = bf16[256,1536]{1,0:T(8,128)(2,1)S(1)} collective-permute-done((bf16[256,1536]{1,0:T(8,128)(2,1)}, bf16[256,1536]{1,0:T(8,128)(2,1)S(1)}, u32[]{:S(2)}, u32[]{:S(2)}) %collective-permute-start.27) | collective-permute-done | bytes 786464 | tf_op jit(solution)/shard_map/ppermute | solution.py:50
  180.8 9.1 %collective-permute-done.29.h4 = bf16[128,1536]{1,0:T(8,128)(2,1)S(1)} collective-permute-done((bf16[128,1536]{1,0:T(8,128)(2,1)S(1)}, bf16[128,1536]{1,0:T(8,128)(2,1)S(1)}, u32[]{:S(2)}, u32[]{:S(2)}) %collective-permute-start.29) | collective-permute-done | bytes 393248 | tf_op jit(solution)/shard_map/ppermute | solution.py:50
  191.9 37.8 %feed_forward.1 = (bf16[1024,1536]{1,0:T(8,128)(2,1)}, bf16[1024,1536]{1,0:T(8,128)(2,1)}, bf16[1024,1152]{1,0:T(8,128)(2,1)}, bf16[1024,1152]{1,0:T(8,128)(2,1)...) custom-call(s32[1]{0:T(128)} %bitcast.core, ...), custom_call_target="tpu_custom_call" | custom-call | flops 18119393280 | bytes 28311552 | tf_op jit(solution)/shard_map/feed_forward/pallas_call | solution.py:538
  231.7 8.9 %convolution_convert_fusion.1 = bf16[1536,1152]{1,0:T(8,128)(2,1)} fusion(bf16[1024,1536]{1,0:T(8,128)(2,1)} %get-tuple-element.206, bf16[1024,1152]{1,0:T(8,128)(2,1)} %get-tuple-element.207), kind=kOutput, calls=%fused_computation.1 | convolution fusion | flops 3625648128 | bytes 9043968 | tf_op jit(solution)/shard_map/dot_general | solution.py:28
  240.6 5.8 %convolution_convert_fusion = bf16[1536,1152]{1,0:T(8,128)(2,1)} fusion(bf16[1024,1536]{1,0:T(8,128)(2,1)S(1)} %copy-done.75, bf16[1024,1152]{1,0:T(8,128)(2,1)S(1)} %copy-done.76), kind=kOutput, calls=%fused_computation | convolution fusion | flops 3625648128 | bytes 9043968 | tf_op jit(solution)/shard_map/dot_general | solution.py:28
  249.2 6.6 %collective-permute-done.45 = bf16[1536,1152]{1,0:T(8,128)(2,1)} collective-permute-done((bf16[1536,1152]{1,0:T(8,128)(2,1)}, bf16[1536,1152]{1,0:T(8,128)(2,1)}, u32[]{:S(2)}, u32[]{:S(2)}) %collective-permute-start.45) | collective-permute-done | bytes 3538976 | tf_op jit(solution)/shard_map/ppermute | solution.py:55
  255.8 5.8 %add_convert_fusion = bf16[1536,1152]{1,0:T(8,128)(2,1)} fusion(bf16[1536,1152]{1,0:T(8,128)(2,1)} %collective-permute-done.45, bf16[1536,1152]{1,0:T(8,128)(2,1)} %convolution_convert_fusion.1), kind=kLoop, calls=%fused_computation.2 | loop fusion | flops 7077888 | bytes 10616832 | tf_op jit(solution)/shard_map/convert_element_type | solution.py:795
  261.8 5.5 %convolution_convert_fusion.7 = bf16[1152,768]{1,0:T(8,128)(2,1)} fusion(bf16[1024,1152]{1,0:T(8,128)(2,1)} %get-tuple-element.214, bf16[1024,1536]{1,0:T(8,128)(2,1)} %get-tuple-element.215, s32[]{:T(128)S(6)} %select_n.169), kind=kOutput, calls=%fused_computation.9 | convolution fusion | flops 1812824064 | bytes 5701636 | tf_op jit(solution)/shard_map/dot_general | solution.py:28
  277.4 5.9 %collective-permute-done.34.x_last = bf16[256,768]{1,0:T(8,128)(2,1)S(1)} collective-permute-done((bf16[256,768]{1,0:T(8,128)(2,1)S(1)}, bf16[256,768]{1,0:T(8,128)(2,1)S(1)}, u32[]{:S(2)}, u32[]{:S(2)}) %collective-permute-start.34) | collective-permute-done | bytes 393248 | tf_op jit(solution)/shard_map/ppermute | solution.py:50
  286.3 8.1 %norm_two_backward.1 = (f32[256,1536]{1,0:T(8,128)}, bf16[256,1536]{1,0:T(8,128)(2,1)}, bf16[256,1536]{1,0:T(8,128)(2,1)}, f32[1,1536]{1,0:T(1,128)}) custom-call(s32[1]{0:T(128)} %bitcast.core, bf16[2,256,768]{2,1,0:T(8,128)(2,1)} %get-tuple-element.203.x_keep, bf16[2,256,768]{2,1,0:T(8,128)(2,1)} %copy-done.19, bf16[256,768]{1,0:T(8,128)(2,1)} %copy-done.43, ...), custom_call_target="tpu_custom_call" | custom-call | flops 1207959552 | bytes 12582912 | tf_op jit(solution)/shard_map/norm_two_backward/pallas_call | solution.py:584
  294.3 19.9 %attend_backward.1 = (bf16[256,1536]{1,0:T(8,128)(2,1)}, bf16[2,1024,128]{2,1,0:T(8,128)(2,1)}, bf16[2,1024,128]{2,1,0:T(8,128)(2,1)}, bf16[2,1024,128]{2,1,0:T(8,128)(2,1)}, bf16[2,1024,128]{2,1,0:T(8,128)(2,1)}) custom-call(s32[6]{0:T(128)} %pad_add_fusion.info, bf16[256,1536]{1,0:T(8,128)(2,1)} %fusion.q_ref, bf16[256,1536]{1,0:T(8,128)(2,1)} %get-tuple-element.220.g_ref, ...), custom_call_target="tpu_custom_call" | custom-call | flops 4529848320 | bytes 8388608 | tf_op jit(solution)/shard_map/attend_backward/pallas_call | solution.py:831
  350.4 4.4 split_rows.3
  354.8 5.2 %collective-permute-done.46 = bf16[2,256,256]{2,1,0:T(8,128)(2,1)S(1)} collective-permute-done((bf16[2,256,256]{2,1,0:T(8,128)(2,1)S(1)}, bf16[2,256,256]{2,1,0:T(8,128)(2,1)S(1)}, u32[]{:S(2)}, u32[]{:S(2)}) %collective-permute-start.46) | collective-permute-done | bytes 262176 | tf_op jit(solution)/shard_map/ppermute | solution.py:50
  365.7 4.3 split_rows.4
  372.8 5.6 %input_backward.1 = (bf16[256,1536]{1,0:T(8,128)(2,1)}, bf16[1536,256]{1,0:T(8,128)(2,1)}, bf16[1536,256]{1,0:T(8,128)(2,1)}) custom-call(s32[1]{0:T(128)} %bitcast.core, f32[256,1536]{1,0:T(8,128)} %convolution_add_fusion.partial, bf16[256,256]{1,0:T(8,128)(2,1)} %fusion.34.dkv, bf16[1536,128]{1,0:T(8,128)(2,1)} %slice.241.kv_own, ...), custom_call_target="tpu_custom_call" | custom-call | flops 402653184 | bytes 6291456 | tf_op jit(solution)/shard_map/input_backward/pallas_call | solution.py:636
  380.7 8.6 %collective-permute-done.49 = bf16[2,2,96,768]{3,2,1,0:T(8,128)(2,1)S(1)} collective-permute-done((bf16[2,2,96,768]{3,2,1,0:T(8,128)(2,1)}, bf16[2,2,96,768]{3,2,1,0:T(8,128)(2,1)S(1)}, u32[]{:S(2)}, u32[]{:S(2)}) %collective-permute-start.49) | collective-permute-done | bytes 589856 | tf_op jit(solution)/shard_map/ppermute | solution.py:50
  423.5 7.5 %collective-permute-done.66.p3 = bf16[96,1152]{1,0:T(8,128)(2,1)S(1)} collective-permute-done((bf16[96,1152]{1,0:T(8,128)(2,1)S(1)}, bf16[96,1152]{1,0:T(8,128)(2,1)S(1)}, u32[]{:S(2)}, u32[]{:S(2)}) %collective-permute-start.66) | collective-permute-done | bytes 221216 | tf_op jit(solution)/shard_map/ppermute | solution.py:50
  441.8 5.4 %reduce-scatter.8.cloned.1.call-done = bf16[96,1792]{1,0:T(8,128)(2,1)} async-done(((bf16[384,1792]{1,0:T(8,128)(2,1)}), bf16[96,1792]{1,0:T(8,128)(2,1)}) %reduce-scatter.8.cloned.1.call-update) | async-done | bytes 344080 | tf_op jit(solution)/shard_map/reduce_scatter | solution.py:70
  (414 shorter events, 195.3 us)
Async XLA Ops:
  7.3 51.7 %all-gather.4.cloned.1.call-start = ((), (), s32[]{:S(2)}) async-start(), calls=%async_computation.3 | async-start | bytes 1474560 | tf_op jit(solution)/shard_map/all_gather | solution.py:64
  10.1 150.1 %all-gather.8.cloned.1.call-start = ((), (), s32[]{:S(2)}) async-start(), calls=%async_computation.5 | async-start | bytes 2211840 | tf_op jit(solution)/shard_map/all_gather | solution.py:64
  10.1 21.8 %collective-permute-start.1 = (bf16[256,1536]{1,0:T(8,128)(2,1)}, bf16[256,1536]{1,0:T(8,128)(2,1)}, u32[]{:S(2)}, u32[]{:S(2)}) collective-permute-start(bf16[256,1536]{1,0:T(8,128)(2,1)} %bitcast.160), channel_id=1, source_target_pairs={{0,2},{1,3},{2,0},{3,1},{4,6},{5,7},{6,4},{7,5},{8,10},{9,11},{10,... | collective-permute-start | bytes 2359304 | tf_op jit(solution)/shard_map/ppermute | solution.py:50
  13.2 19.3 %collective-permute-start = (bf16[256,1536]{1,0:T(8,128)(2,1)}, bf16[256,1536]{1,0:T(8,128)(2,1)}, u32[]{:S(2)}, u32[]{:S(2)}) collective-permute-start(bf16[256,1536]{1,0:T(8,128)(2,1)} %bitcast.161), channel_id=1, source_target_pairs={{0,1},{1,0},{2,3},{3,2},{4,5},{5,4},{6,7},{7,6},{8,9},{9,8},{10,11... | collective-permute-start | bytes 2359304 | tf_op jit(solution)/shard_map/ppermute | solution.py:50
  15.5 162.6 %all-gather.6.cloned.1.call-start = ((), (), s32[]{:S(2)}) async-start(), calls=%async_computation.4 | async-start | bytes 4423680 | tf_op jit(solution)/shard_map/all_gather | solution.py:64
  61.2 31.3 %collective-permute-start.11 = (bf16[4,96,768]{2,1,0:T(8,128)(2,1)}, bf16[4,96,768]{2,1,0:T(8,128)(2,1)}, u32[]{:S(2)}, u32[]{:S(2)}) collective-permute-start(bf16[4,96,768]{2,1,0:T(8,128)(2,1)} %bitcast.11.own), channel_id=1, source_target_pairs={{0,2},{1,3},{2,0},{3,1},{4,6},{5,7},{6,4},{7,5},{8,10},{9,11},{10,... | collective-permute-start | bytes 1769480 | tf_op jit(solution)/shard_map/ppermute | solution.py:50
  61.8 30.7 %collective-permute-start.10 = (bf16[4,96,768]{2,1,0:T(8,128)(2,1)}, bf16[4,96,768]{2,1,0:T(8,128)(2,1)}, u32[]{:S(2)}, u32[]{:S(2)}) collective-permute-start(bf16[4,96,768]{2,1,0:T(8,128)(2,1)} %bitcast.11.own), channel_id=1, source_target_pairs={{0,1},{1,0},{2,3},{3,2},{4,5},{5,4},{6,7},{7,6},{8,9},{9,8},{10,11... | collective-permute-start | bytes 1769480 | tf_op jit(solution)/shard_map/ppermute | solution.py:50
  62.4 30.1 %collective-permute-start.13 = (bf16[4,96,768]{2,1,0:T(8,128)(2,1)S(1)}, bf16[4,96,768]{2,1,0:T(8,128)(2,1)}, u32[]{:S(2)}, u32[]{:S(2)}) collective-permute-start(bf16[4,96,768]{2,1,0:T(8,128)(2,1)S(1)} %bitcast.152), channel_id=1, source_target_pairs={{0,2},{1,3},{2,0},{3,1},{4,6},{5,7},{6,4},{7,5},{8,10},{9,11},{10,... | collective-permute-start | bytes 1769480 | tf_op jit(solution)/shard_map/ppermute | solution.py:50
  63.7 28.8 %collective-permute-start.12 = (bf16[4,96,768]{2,1,0:T(8,128)(2,1)S(1)}, bf16[4,96,768]{2,1,0:T(8,128)(2,1)}, u32[]{:S(2)}, u32[]{:S(2)}) collective-permute-start(bf16[4,96,768]{2,1,0:T(8,128)(2,1)S(1)} %bitcast.153), channel_id=1, source_target_pairs={{0,1},{1,0},{2,3},{3,2},{4,5},{5,4},{6,7},{7,6},{8,9},{9,8},{10,11... | collective-permute-start | bytes 1769480 | tf_op jit(solution)/shard_map/ppermute | solution.py:50
  69.6 274.1 %reduce-scatter.4.cloned.1.call-start = ((), (), s32[]{:S(2)}) async-start(), calls=%async_computation.6 | async-start | bytes 4423680 | tf_op jit(solution)/shard_map/reduce_scatter | solution.py:70
  92.5 23.3 %collective-permute-start.15 = (bf16[1024,256]{1,0:T(8,128)(2,1)S(1)}, bf16[1024,256]{1,0:T(8,128)(2,1)S(1)}, u32[]{:S(2)}, u32[]{:S(2)}) collective-permute-start(bf16[1024,256]{1,0:T(8,128)(2,1)S(1)} %all_gather.17.k0), channel_id=1, source_target_pairs={{0,2},{1,3},{2,0},{3,1},{4,6},{5,7},{6,4},{7,5},{8,10},{9,11},{10,... | collective-permute-start | bytes 1572872 | tf_op jit(solution)/shard_map/ppermute | solution.py:50
  93.3 22.5 %collective-permute-start.14 = (bf16[1024,256]{1,0:T(8,128)(2,1)S(1)}, bf16[1024,256]{1,0:T(8,128)(2,1)S(1)}, u32[]{:S(2)}, u32[]{:S(2)}) collective-permute-start(bf16[1024,256]{1,0:T(8,128)(2,1)S(1)} %all_gather.17.k0), channel_id=1, source_target_pairs={{0,1},{1,0},{2,3},{3,2},{4,5},{5,4},{6,7},{7,6},{8,9},{9,8},{10,11... | collective-permute-start | bytes 1572872 | tf_op jit(solution)/shard_map/ppermute | solution.py:50
  94.8 19.6 %collective-permute-start.17 = (bf16[2,96,768]{2,1,0:T(8,128)(2,1)S(1)}, bf16[2,96,768]{2,1,0:T(8,128)(2,1)S(1)}, u32[]{:S(2)}, u32[]{:S(2)}) collective-permute-start(bf16[2,96,768]{2,1,0:T(8,128)(2,1)S(1)} %slice.246), channel_id=1, source_target_pairs={{0,1},{1,0},{2,3},{3,2},{4,5},{5,4},{6,7},{7,6},{8,9},{9,8},{10,11... | collective-permute-start | bytes 884744 | tf_op jit(solution)/shard_map/ppermute | solution.py:50
  100.7 20.1 %collective-permute-start.21 = (bf16[2,96,768]{2,1,0:T(8,128)(2,1)S(1)}, bf16[2,96,768]{2,1,0:T(8,128)(2,1)S(1)}, u32[]{:S(2)}, u32[]{:S(2)}) collective-permute-start(bf16[2,96,768]{2,1,0:T(8,128)(2,1)S(1)} %slice.250), channel_id=1, source_target_pairs={{0,1},{1,0},{2,3},{3,2},{4,5},{5,4},{6,7},{7,6},{8,9},{9,8},{10,11... | collective-permute-start | bytes 884744 | tf_op jit(solution)/shard_map/ppermute | solution.py:50
  128.0 24.0 %collective-permute-start.25 = (bf16[1536,768]{1,0:T(8,128)(2,1)}, bf16[1536,768]{1,0:T(8,128)(2,1)}, u32[]{:S(2)}, u32[]{:S(2)}) collective-permute-start(bf16[1536,768]{1,0:T(8,128)(2,1)} %bitcast.136), channel_id=1, source_target_pairs={{0,16},{16,0},{1,17},{17,1},{2,18},{18,2},{3,19},{19,3},{4,20},{20... | collective-permute-start | bytes 7077896 | tf_op jit(solution)/shard_map/ppermute | solution.py:55
  132.2 19.7 %collective-permute-start.24 = (bf16[128,1536]{1,0:T(8,128)(2,1)S(1)}, bf16[128,1536]{1,0:T(8,128)(2,1)S(1)}, u32[]{:S(2)}, u32[]{:S(2)}) collective-permute-start(bf16[128,1536]{1,0:T(8,128)(2,1)S(1)} %slice.252), channel_id=1, source_target_pairs={{0,1},{1,0},{2,3},{3,2},{4,5},{5,4},{6,7},{7,6},{8,9},{9,8},{10,11... | collective-permute-start | bytes 1179656 | tf_op jit(solution)/shard_map/ppermute | solution.py:50
  261.6 152.6 %reduce-scatter.6.cloned.1.call-start = ((), (), s32[]{:S(2)}) async-start(), calls=%async_computation.7 | async-start | bytes 2211840 | tf_op jit(solution)/shard_map/reduce_scatter | solution.py:70
  284.1 30.2 %collective-permute-start.37 = (bf16[2,256,768]{2,1,0:T(8,128)(2,1)S(1)}, bf16[2,256,768]{2,1,0:T(8,128)(2,1)S(1)}, u32[]{:S(2)}, u32[]{:S(2)}) collective-permute-start(bf16[2,256,768]{2,1,0:T(8,128)(2,1)S(1)} %bitcast.167), channel_id=1, source_target_pairs={{0,2},{1,3},{2,0},{3,1},{4,6},{5,7},{6,4},{7,5},{8,10},{9,11},{10,... | collective-permute-start | bytes 2359304 | tf_op jit(solution)/shard_map/ppermute | solution.py:50
  285.2 29.0 %collective-permute-start.36 = (bf16[2,256,768]{2,1,0:T(8,128)(2,1)S(1)}, bf16[2,256,768]{2,1,0:T(8,128)(2,1)S(1)}, u32[]{:S(2)}, u32[]{:S(2)}) collective-permute-start(bf16[2,256,768]{2,1,0:T(8,128)(2,1)S(1)} %bitcast.166), channel_id=1, source_target_pairs={{0,1},{1,0},{2,3},{3,2},{4,5},{5,4},{6,7},{7,6},{8,9},{9,8},{10,11... | collective-permute-start | bytes 2359304 | tf_op jit(solution)/shard_map/ppermute | solution.py:50
  319.2 43.0 %collective-permute-start.62 = (bf16[1152,768]{1,0:T(8,128)(2,1)}, bf16[1152,768]{1,0:T(8,128)(2,1)}, u32[]{:S(2)}, u32[]{:S(2)}) collective-permute-start(bf16[1152,768]{1,0:T(8,128)(2,1)} %convolution_convert_fusion.6), channel_id=1, source_target_pairs={{0,16},{16,0},{1,17},{17,1},{2,18},{18,2},{3,19},{19,3},{4,20},{20... | collective-permute-start | bytes 5308424 | tf_op jit(solution)/shard_map/ppermute | solution.py:55
  342.6 23.1 %collective-permute-start.48 = (bf16[1536,768]{1,0:T(8,128)(2,1)}, bf16[1536,768]{1,0:T(8,128)(2,1)}, u32[]{:S(2)}, u32[]{:S(2)}) collective-permute-start(bf16[1536,768]{1,0:T(8,128)(2,1)} %convolution_convert_fusion.2), channel_id=1, source_target_pairs={{0,16},{16,0},{1,17},{17,1},{2,18},{18,2},{3,19},{19,3},{4,20},{20... | collective-permute-start | bytes 7077896 | tf_op jit(solution)/shard_map/ppermute | solution.py:55
  365.4 81.8 %reduce-scatter.8.cloned.1.call-start = ((), (), s32[]{:S(2)}) async-start(), calls=%async_computation.8 | async-start | bytes 1720320 | tf_op jit(solution)/shard_map/reduce_scatter | solution.py:70
  370.1 19.3 %collective-permute-start.49 = (bf16[2,2,96,768]{3,2,1,0:T(8,128)(2,1)}, bf16[2,2,96,768]{3,2,1,0:T(8,128)(2,1)S(1)}, u32[]{:S(2)}, u32[]{:S(2)}) collective-permute-start(bf16[2,2,96,768]{3,2,1,0:T(8,128)(2,1)} %get-tuple-element.268), channel_id=1, source_target_pairs={{0,1},{1,0},{2,3},{3,2},{4,5},{5,4},{6,7},{7,6},{8,9},{9,8},{10,11... | collective-permute-start | bytes 1769480 | tf_op jit(solution)/shard_map/ppermute | solution.py:50
  371.1 19.3 %collective-permute-start.50 = (bf16[2,2,96,768]{3,2,1,0:T(8,128)(2,1)}, bf16[2,2,96,768]{3,2,1,0:T(8,128)(2,1)S(1)}, u32[]{:S(2)}, u32[]{:S(2)}) collective-permute-start(bf16[2,2,96,768]{3,2,1,0:T(8,128)(2,1)} %get-tuple-element.269), channel_id=1, source_target_pairs={{0,2},{1,3},{2,0},{3,1},{4,6},{5,7},{6,4},{7,5},{8,10},{9,11},{10,... | collective-permute-start | bytes 1769480 | tf_op jit(solution)/shard_map/ppermute | solution.py:50
  (128 other events, 1381.0 us)
Sparse Core Ops, SparseCore 0:
  10.2 34.3 all-gather.3
  46.2 48.0 all-gather.7
  96.5 68.8 all-gather.5
  261.7 67.4 reduce-scatter.3
  365.5 37.5 reduce-scatter.5
  415.5 31.6 reduce-scatter.7

commit v3 on v2

--- a/solution.py
+++ b/solution.py
@@ -72,25 +72,26 @@
     )
 
 
-def halve_column(value, line_place, during=()):
+def double_column(value):
+    held = value[None]
+    while held.shape[0] < lax.axis_size("shard") // plane:
+        got = across(held, held.shape[0] * plane)
+        held = jnp.concatenate([held, got], axis=0)
+    return held
+
+
+def halve_column(held, *during):
     during = list(during)
-    lead = lax.axis_size("shard") // plane
-    held = value.reshape(lead, -1, value.shape[1])
-    size = lead // 2
-    done = 0
-    while size >= 1:
-        pair = held.reshape(2, size, *held.shape[1:])
-        mine = (line_place // size) % 2
-        kept = lax.dynamic_index_in_dim(pair, mine, axis=0, keepdims=False)
-        got = across(
-            lax.dynamic_index_in_dim(pair, 1 - mine, axis=0, keepdims=False), size * plane
-        )
-        if done < len(during):
-            got, *during[done] = tie(got, *during[done])
-            done += 1
-        held = (kept.astype(f32) + got.astype(f32)).astype(bf16)
-        size //= 2
-    return held[0], during
+    ready = ()
+    while held.shape[0] > 1:
+        size = held.shape[0] // 2
+        got = across(held[size:], size * plane)
+        if during:
+            got, *ready = tie(got, *during.pop(0)(*ready))
+        held = (held[:size].astype(f32) + got.astype(f32)).astype(bf16)
+    for rest in during:
+        ready = rest(*ready)
+    return held[0], ready
 
 
 def start_plane(value):
@@ -108,21 +109,22 @@
     return finish_plane(value, *tie(*start_plane(value)))
 
 
-def place_kernel(place, own, first, second, far_top, far_bottom, out):
+def place_kernel(relative, place, own, first, second, far_top, far_bottom, out):
     half = far_top.shape[0]
     me = place[0]
-    out[:, pl.ds(me, 1)] = own[...][:, None]
-    out[:, pl.ds(me ^ 1, 1)] = first[...][:, None]
-    out[:, pl.ds(me ^ 2, 1)] = second[...][:, None]
-    out[:half, pl.ds(me ^ 3, 1)] = far_top[...][:, None]
-    out[half:, pl.ds(me ^ 3, 1)] = far_bottom[...][:, None]
-
-
-def place_plane(blocks, place):
+    line = place[1] // plane if relative else 0
+    for at in range(own.shape[0]):
+        far = far_top[at : at + 1] if at < half else far_bottom[at - half : at - half + 1]
+        blocks = (own[at : at + 1], first[at : at + 1], second[at : at + 1], far)
+        for mask, block in enumerate(blocks):
+            out[pl.ds(line ^ at, 1), pl.ds(me ^ mask, 1)] = block[:, None]
+
+
+def place_plane(blocks, place, relative=False):
     lead, rows, width = blocks[0].shape
     vmem = pl.BlockSpec(memory_space=pltpu.VMEM)
     return pl.pallas_call(
-        place_kernel,
+        functools.partial(place_kernel, relative),
         out_shape=jax.ShapeDtypeStruct((lead, plane, rows, width), blocks[0].dtype),
         in_specs=[pl.BlockSpec(memory_space=pltpu.SMEM)] + [vmem] * 5,
         out_specs=vmem,
@@ -161,22 +163,24 @@
     )(place, *pieces)
 
 
-def exchange_plane(x_send, x_keep, y_send, y_keep, during_first=(), during_second=()):
-    x_got = across(x_send.astype(bf16), 1)
-    y_got = across(y_send.astype(bf16), 2)
-    x_got, y_got, *during_first = tie(x_got, y_got, *during_first)
+def pass_plane(x_keep, x_got, y_keep, y_got):
     x_pass, y_pass = tie(
         (x_keep[1].astype(f32) + x_got[1].astype(f32)).astype(bf16),
         (y_keep[1].astype(f32) + y_got[0].astype(f32)).astype(bf16),
     )
-    x_last = across(x_pass, 2)
-    y_last = across(y_pass, 1)
+    return across(x_pass, 2), across(y_pass, 1)
+
+
+def exchange_plane(x_send, x_keep, y_send, y_keep, during_first=(), during_second=()):
+    x_got, y_got, *during_first = tie(across(x_send, 1), across(y_send, 2), *during_first)
+    x_last, y_last = pass_plane(x_keep, x_got, y_keep, y_got)
     x_last, y_last, *during_second = tie(x_last, y_last, *during_second)
     return x_got, x_last, y_got, y_last, during_first, during_second
 
 
-def split_kernel(place, own, got, x_send, x_keep, y_send, y_keep):
-    half = own.shape[0] // 2
+def split_kernel(place, *refs):
+    *pairs, x_send, x_keep, y_send, y_keep = refs
+    half = x_send.shape[1]
     for out, slot, mask, first in (
         (x_send, 0, 1, 0),
         (x_send, 1, 3, 0),
@@ -188,25 +192,29 @@
         (y_keep, 1, 1, half),
     ):
         at = (slice(first, first + half), pl.ds(place[0] ^ mask, 1))
-        out[slot] = (own[at].astype(f32) + got[at].astype(f32))[:, 0].astype(bf16)
-
-
-def split_rows(place, own, got, rows):
-    lead = own.shape[0] // (plane * rows)
-    shape = (lead, plane, rows, own.shape[1])
+        start = 0
+        for own, got in zip(pairs[::2], pairs[1::2]):
+            end = start + own.shape[3]
+            total = (own[at].astype(f32) + got[at].astype(f32))[:, 0].astype(bf16)
+            out[slot, :, :, start:end] = total
+            start = end
+
+
+def split_rows(place, rows, *pairs):
+    lead = pairs[0].shape[0] // (plane * rows)
+    width = sum(value.shape[1] for value in pairs) // 2
     vmem = pl.BlockSpec(memory_space=pltpu.VMEM)
-    sent = jax.ShapeDtypeStruct((2, lead // 2, rows, own.shape[1]), bf16)
+    sent = jax.ShapeDtypeStruct((2, lead // 2, rows, width), bf16)
+    size = width * pairs[0].shape[0]
     return pl.pallas_call(
         split_kernel,
         out_shape=(sent,) * 4,
-        in_specs=[pl.BlockSpec(memory_space=pltpu.SMEM), vmem, vmem],
+        in_specs=[pl.BlockSpec(memory_space=pltpu.SMEM)] + [vmem] * len(pairs),
         out_specs=(vmem,) * 4,
-        cost_estimate=pl.CostEstimate(
-            flops=own.size, transcendentals=0, bytes_accessed=6 * own.size
-        ),
+        cost_estimate=pl.CostEstimate(flops=size, transcendentals=0, bytes_accessed=6 * size),
         compiler_params=pltpu.CompilerParams(vmem_limit_bytes=56 * 2**20),
         name="split_rows",
-    )(place, own.reshape(shape), got.reshape(shape))
+    )(place, *(value.reshape(lead, plane, rows, value.shape[1]) for value in pairs))
 
 
 def joined(x_keep, x_got, x_last, y_keep, y_got, y_last, axis):
@@ -369,6 +377,7 @@
 
     lax.fori_loop(0, micro_count * pieces, slot, 0)
     slots = micro_count * pieces
+    line = info[1] // plane
     for mask, k_out, k_at, v_out, v_at in (
         (0, kx_keep, 0, vy_keep, 0),
         (1, kx_send, 0, vy_keep, 1),
@@ -379,7 +388,7 @@
 
         def copy(index, carry, member=member, k_out=k_out, k_at=k_at, v_out=v_out, v_at=v_at):
             row = pl.multiple_of(
-                pad + (index % pieces) * window + ((index // slots) * plane + member) * sub, 16
+                pad + (index % pieces) * window + (((index // slots) ^ line) * plane + member) * sub, 16
             )
             micro = (index // pieces) % micro_count
             to = pl.ds(pl.multiple_of(index * sub, 16), sub)
@@ -796,25 +805,25 @@
 
     wide_peer = product_tn(all_normed, grad_other_in).astype(bf16)
     wide_mine = product_tn(all_normed, grad_own_in).astype(bf16)
-    out_mine = product(hidden, down_own).astype(bf16)
-    out_peer = product(hidden, down_other).astype(bf16)
     x_send, x_keep, y_send, y_keep = sums
-    x_got, x_last, y_got, y_last, during_first, during_second = exchange_plane(
-        x_send,
-        x_keep,
-        y_send,
-        y_keep,
-        (wide_mine, wide_peer),
-        (
-            out_mine,
-            out_peer,
-            product_tn(hidden, up_own).astype(bf16),
-            product_tn(hidden, up_other).astype(bf16),
-        ),
-    )
-    out_mine, out_peer, *down_parts = during_second
-    wide_grad = scatter_column(chip_sum(*during_first))
-    down_grad = scatter_column(chip_sum(*down_parts))
+    x_got, y_got, wide_mine, wide_peer = tie(
+        across(x_send, 1), across(y_send, 2), wide_mine, wide_peer
+    )
+    x_pass, y_pass, wide_mine, wide_peer, hidden = tie(
+        (x_keep[1].astype(f32) + x_got[1].astype(f32)).astype(bf16),
+        (y_keep[1].astype(f32) + y_got[0].astype(f32)).astype(bf16),
+        wide_mine,
+        wide_peer,
+        hidden,
+    )
+    x_last, y_last, out_mine, out_peer, wide_sum = tie(
+        across(x_pass, 2),
+        across(y_pass, 1),
+        product(hidden, down_own).astype(bf16),
+        product(hidden, down_other).astype(bf16),
+        chip_sum(wide_mine, wide_peer),
+    )
+    wide_grad = scatter_column(wide_sum)
     grad_resid, grad_attn, grad_mixed, grad_gain_two = norm_two_backward(
         core_info,
         (x_keep, x_got, x_last, y_keep, y_got, y_last),
@@ -827,14 +836,21 @@
 
     one = out_mine.reshape(plane, token_count, -1)
     two = out_peer.reshape(plane, token_count, -1)
-    out_parts = (one[1:3], (one[0], one[3]), two[2:4], (two[0], two[1]))
     grad_queries, kx_send, kx_keep, vy_send, vy_keep = backward(
         info, queries, grad_mixed, logsum, *kv_blocks
     )
-    out_x, out_x_last, out_y, out_y_last, kernel_out, _ = exchange_plane(
-        *out_parts, (grad_queries, kx_send, kx_keep, vy_send, vy_keep, grad_attn)
-    )
-    grad_queries, kx_send, kx_keep, vy_send, vy_keep, grad_attn = kernel_out
+    out_x, out_y, grad_queries, kx_send, kx_keep, vy_send, vy_keep, grad_attn, hidden = tie(
+        across(one[1:3], 1),
+        across(two[2:4], 2),
+        grad_queries,
+        kx_send,
+        kx_keep,
+        vy_send,
+        vy_keep,
+        grad_attn,
+        hidden,
+    )
+    out_x_last, out_y_last = pass_plane((one[0], one[3]), out_x, (two[0], two[1]), out_y)
     out_sum = (
         one[0].astype(f32) + out_x[0].astype(f32) + out_x_last.astype(f32),
         two[0].astype(f32) + out_y[1].astype(f32) + out_y_last.astype(f32),
@@ -845,36 +861,42 @@
     da_own, da_other = halves(grad_attn)
     attn_mine = product_tn(attended, da_own).astype(bf16)
     attn_peer = peer(product_tn(attended, da_other).astype(bf16))
-    kx_got, kx_last, vy_got, vy_last, attn_parts, query_parts = exchange_plane(
-        kx_send,
-        kx_keep,
-        vy_send,
-        vy_keep,
-        (attn_mine, attn_peer),
-        (
-            product_tn(normed_one, dq_own).astype(bf16),
-            product_tn(normed_one, dq_other).astype(bf16),
-        ),
-    )
+    kx_got, vy_got, attn_mine, attn_peer, query_mine, query_peer = tie(
+        across(kx_send, 1),
+        across(vy_send, 2),
+        attn_mine,
+        attn_peer,
+        product_tn(normed_one, dq_own).astype(bf16),
+        peer(product_tn(normed_one, dq_other).astype(bf16)),
+    )
+    kx_last, vy_last = pass_plane(kx_keep, kx_got, vy_keep, vy_got)
+    kx_last, vy_last, hidden, attn_x, attn_x_keep, attn_y, attn_y_keep = tie(
+        kx_last,
+        vy_last,
+        hidden,
+        *split_rows(place, my_rows, query_mine, query_peer, attn_mine, attn_peer),
+    )
+    attn_x, attn_y = across(attn_x, 1), across(attn_y, 2)
     grad_kv, wide_grad = tie(
         joined(kx_keep, kx_got, kx_last, vy_keep, vy_got, vy_last, 1), wide_grad
     )
-    attn_split = split_rows(place, *attn_parts, my_rows)
-    query_split = split_rows(place, query_parts[0], peer(query_parts[1]), my_rows)
     partial = product_nt(dq_own, query_own) + product_nt(dq_other, query_other)
-    grad_keyvals, (attn_split, query_split) = halve_column(
-        grad_kv, my_index // plane, (attn_split, (*query_split, partial))
-    )
-    *query_split, partial = query_split
+
+    def first_step():
+        return (
+            product_tn(hidden, up_own).astype(bf16),
+            product_tn(hidden, up_other).astype(bf16),
+        )
+
+    def second_step(down_mine, down_peer):
+        return partial, down_mine, down_peer, attn_x, attn_y
+
+    grad_keyvals, (partial, down_mine, down_peer, attn_x, attn_y) = halve_column(
+        grad_kv.reshape(lead, token_count, -1), first_step, second_step
+    )
+    grad_keyvals, down_sum = tie(grad_keyvals, chip_sum(down_mine, down_peer))
+    down_grad = scatter_column(down_sum)
     wide_grad = wide_grad.reshape(plane, my_rows, part)
-
-    def plane_rows(x_send, x_keep, y_send, y_keep):
-        x_got, x_last, y_got, y_last, _, _ = exchange_plane(x_send, x_keep, y_send, y_keep)
-        total = joined(x_keep, x_got, x_last, y_keep, y_got, y_last, 0)
-        return total.reshape(lead * my_rows, -1)
-
-    attn_plane = plane_rows(*attn_split)
-    query_plane = plane_rows(*query_split)
     input_grad, last_own, last_other = input_backward(
         core_info,
         partial,
@@ -888,10 +910,21 @@
         grad_resid,
     )
     input_grad = input_grad.reshape(tokens.shape)
-    last_plane = plane_rows(*split_rows(place, last_own, peer(last_other), my_rows))
+    last_split = split_rows(place, my_rows, last_own, peer(last_other))
+    attn_x_last, attn_y_last = pass_plane(attn_x_keep, attn_x, attn_y_keep, attn_y)
+    attn_plane = joined(
+        attn_x_keep, attn_x, attn_x_last, attn_y_keep, attn_y, attn_y_last, 0
+    ).reshape(lead * my_rows, -1)
+    last_x, last_x_keep, last_y, last_y_keep = last_split
+    last_x, last_x_last, last_y, last_y_last, _, _ = exchange_plane(
+        last_x, last_x_keep, last_y, last_y_keep
+    )
+    last_plane = joined(
+        last_x_keep, last_x, last_x_last, last_y_keep, last_y, last_y_last, 0
+    ).reshape(lead * my_rows, -1)
     last_plane, down_grad = tie(last_plane, down_grad)
     last_share = scatter_column(
-        jnp.concatenate([query_plane, attn_plane, last_plane], axis=1)
+        jnp.concatenate([attn_plane, last_plane], axis=1)
     )
 
     wide_back = []

time: 467 us -> 456 us (0.976)
  matrix products: 47.9 us -> 41.6 us
    dot_general x8, matrix products: 32.5 us -> 25.3 us  [product_tn(): lax.dot_general(first_op, second_op, (((0,), (0,)), ((), ())), preferred_...]
    ppermute x56 -> x52, starting transfers between devices: 59.4 us -> 55.8 us  [across(): return lax.ppermute(value, 'shard', [(i, i ^ mask) for i in range(count)])]
    ppermute x56 -> x52, waiting for transfers between devices: 109 us -> 106 us  [across(): return lax.ppermute(value, 'shard', [(i, i ^ mask) for i in range(count)])]
    pallas_call x3 -> x2, Pallas kernels: 11.1 us -> 9.45 us  [split_rows(): pl.pallas_call(split_kernel, out_shape=(sent,) * 4, in_specs=[pl.BlockSpe...]
  transfers between devices with their start and end apart: 75 -> 71, of which waited for: 36 -> 36; matrix products, arithmetic and copies ran while one was open for 20% -> 20% of each run, Pallas kernels for 16% -> 16%
where the time goes in v3:
time: 456 us; the launch traced here: 448 us
  waiting for transfers between devices  118 us (26%)
  Pallas kernels  112 us (25%)
  starting transfers between devices  58.1 us (13%)
  matrix products  41.6 us (9%)
  blocking collectives  38.5 us (8%)
  local copies, waits for them, and re-layouts  33.2 us (7%)
  other arithmetic  31.3 us (7%)
  between operations  15.7 us (3%)
    ppermute x52, waiting for transfers between devices, across(): return lax.ppermute(value, 'shard', [(i, i ^ mask) for i in range(count)])  106 us
    ppermute x52, starting transfers between devices, across(): return lax.ppermute(value, 'shard', [(i, i ^ mask) for i in range(count)])  55.8 us
    all_gather x2, blocking collectives, gather_column(): lax.all_gather(value, 'shard', axis=0, tiled=True, axis_index_groups=colu...  38.5 us
    pallas_call x1, Pallas kernels, feed_forward(): pl.pallas_call(feed_kernel, out_shape=(shape((count, width), bf16),) * 2...  37.8 us
    dot_general x8, matrix products, product_tn(): lax.dot_general(first_op, second_op, (((0,), (0,)), ((), ())), preferred_...  25.3 us
    pallas_call x1, Pallas kernels, on_device(): backward(info, queries, grad_mixed, logsum, *kv_blocks)  20 us
    pallas_call x1, Pallas kernels, on_device(): attended, logsum = forward(info, queries, *kv_blocks)  12.8 us
    dot_general x6, matrix products, product(): return jnp.dot(first_op, second_op, preferred_element_type=f32)  10.7 us
  transfers between devices with their start and end apart: 71, of which 36 were waited for; matrix products, arithmetic and copies ran while one was open for 20% of the time, Pallas kernels for 16%

profile of v3, /device:TPU:0, one launch (start us, length us, event | category | flops | bytes accessed | tf_op | source)
XLA Modules:
  0.0 447.7 jit_solution(3676025784719091146)
XLA Ops:
  16.1 15.7 %all_gather.15 = bf16[384,256]{1,0:T(8,128)(2,1)} all-gather(bf16[96,256]{1,0:T(8,128)(2,1)S(1)} %copy.39), channel_id=1, replica_groups={{0,4,8,12},{1,5,9,13},{2,6,10,14},{3,7,11,15},{16,20,24,28},{17,21,25,2..., dimensions={0}, use_global_device_ids=true | all-gather | bytes 245760 | tf_op jit(solution)/shard_map/all_gather | solution.py:64
  49.3 5.7 %collective-permute-done.8 = bf16[1,96,1152]{2,1,0:T(8,128)(2,1)S(1)} collective-permute-done((bf16[1,96,1152]{2,1,0:T(8,128)(2,1)S(1)}, bf16[1,96,1152]{2,1,0:T(8,128)(2,1)S(1)}, u32[]{:S(2)}, u32[]{:S(2)}) %collective-permute-start.8) | collective-permute-done | bytes 221216 | tf_op jit(solution)/shard_map/ppermute | solution.py:50
  69.1 22.8 %all_gather.17.k0 = bf16[1024,256]{1,0:T(8,128)(2,1)S(1)} all-gather(bf16[256,256]{1,0:T(8,128)(2,1)S(1)} %fusion.27), channel_id=1, replica_groups={{0,4,8,12},{1,5,9,13},{2,6,10,14},{3,7,11,15},{16,20,24,28},{17,21,25,2..., dimensions={0}, use_global_device_ids=true | all-gather | bytes 655360 | tf_op jit(solution)/shard_map/all_gather | solution.py:64
  100.8 13.2 %collective-permute-done.17.far_bottom = bf16[2,96,768]{2,1,0:T(8,128)(2,1)S(1)} collective-permute-done((bf16[2,96,768]{2,1,0:T(8,128)(2,1)S(1)}, bf16[2,96,768]{2,1,0:T(8,128)(2,1)S(1)}, u32[]{:S(2)}, u32[]{:S(2)}) %collective-permute-start.17) | collective-permute-done | bytes 294944 | tf_op jit(solution)/shard_map/ppermute | solution.py:50
  138.4 12.8 %attend_forward.1 = (bf16[256,1536]{1,0:T(8,128)(2,1)}, f32[4,768,1]{2,1,0:T(8,128)}) custom-call(s32[6]{0:T(128)} %pad_add_fusion.info, bf16[256,1536]{1,0:T(8,128)(2,1)} %fusion.q_ref, bf16[1024,256]{1,0:T(8,128)(2,1)} %copy-done.30, bf16[1024,256]{1,0:T(8,128)(2,1)} %copy-done.51, bf16[1024,256]{1,0:T(8,128)(2,1)} %copy-done.50, ...), custom_call_target="tpu_custom_call" | custom-call | flops 1811939328 | bytes 4194304 | tf_op jit(solution)/shard_map/attend_forward/pallas_call | solution.py:779
  151.2 6.1 %outproj_norm.1 = (f32[256,1536]{1,0:T(8,128)}, bf16[256,1536]{1,0:T(8,128)(2,1)}) custom-call(s32[1]{0:T(128)} %bitcast.core, bf16[256,1536]{1,0:T(8,128)(2,1)} %get-tuple-element.177.att, bf16[1536,768]{1,0:T(8,128)(2,1)} %bitcast.121, bf16[1536,768]{1,0:T(8,128)(2,1)} %collective-permute-done.25.other, bf16[256,1536]{1,0:T(8,128)(2,1)} %bitcast.125, ...), custom_call_target="tpu_custom_call" | custom-call | flops 1207959552 | bytes 8650752 | tf_op jit(solution)/shard_map/outproj_norm/pallas_call | solution.py:460
  160.3 16.5 %collective-permute-done.27.h2 = bf16[256,1536]{1,0:T(8,128)(2,1)} collective-permute-done((bf16[256,1536]{1,0:T(8,128)(2,1)}, bf16[256,1536]{1,0:T(8,128)(2,1)}, u32[]{:S(2)}, u32[]{:S(2)}) %collective-permute-start.27) | collective-permute-done | bytes 786464 | tf_op jit(solution)/shard_map/ppermute | solution.py:50
  182.8 8.6 %collective-permute-done.29.h4 = bf16[128,1536]{1,0:T(8,128)(2,1)S(1)} collective-permute-done((bf16[128,1536]{1,0:T(8,128)(2,1)S(1)}, bf16[128,1536]{1,0:T(8,128)(2,1)S(1)}, u32[]{:S(2)}, u32[]{:S(2)}) %collective-permute-start.29) | collective-permute-done | bytes 393248 | tf_op jit(solution)/shard_map/ppermute | solution.py:50
  194.1 37.8 %feed_forward.1 = (bf16[1024,1536]{1,0:T(8,128)(2,1)}, bf16[1024,1536]{1,0:T(8,128)(2,1)}, bf16[1024,1152]{1,0:T(8,128)(2,1)}, bf16[1024,1152]{1,0:T(8,128)(2,1)...) custom-call(s32[1]{0:T(128)} %bitcast.core, ...), custom_call_target="tpu_custom_call" | custom-call | flops 18119393280 | bytes 28311552 | tf_op jit(solution)/shard_map/feed_forward/pallas_call | solution.py:547
  233.2 7.0 %convolution_convert_fusion.1 = bf16[1536,1152]{1,0:T(8,128)(2,1)S(1)} fusion(bf16[1024,1536]{1,0:T(8,128)(2,1)} %get-tuple-element.198, bf16[1024,1152]{1,0:T(8,128)(2,1)} %get-tuple-element.199), kind=kOutput, calls=%fused_computation.1 | convolution fusion | flops 3625648128 | bytes 9043968 | tf_op jit(solution)/shard_map/dot_general | solution.py:28
  240.3 4.6 %convolution_convert_fusion = bf16[1536,1152]{1,0:T(8,128)(2,1)S(1)} fusion(bf16[1024,1536]{1,0:T(8,128)(2,1)S(1)} %copy-done.72, bf16[1024,1152]{1,0:T(8,128)(2,1)S(1)} %copy-done.73), kind=kOutput, calls=%fused_computation | convolution fusion | flops 3625648128 | bytes 9043968 | tf_op jit(solution)/shard_map/dot_general | solution.py:28
  244.9 5.7 %collective-permute-done.32.x_got = bf16[2,256,768]{2,1,0:T(8,128)(2,1)S(1)} collective-permute-done((bf16[2,256,768]{2,1,0:T(8,128)(2,1)}, bf16[2,256,768]{2,1,0:T(8,128)(2,1)S(1)}, u32[]{:S(2)}, u32[]{:S(2)}) %collective-permute-start.32) | collective-permute-done | bytes 786464 | tf_op jit(solution)/shard_map/ppermute | solution.py:50
  271.1 8.7 %norm_two_backward.1 = (f32[256,1536]{1,0:T(8,128)}, bf16[256,1536]{1,0:T(8,128)(2,1)}, bf16[256,1536]{1,0:T(8,128)(2,1)}, f32[1,1536]{1,0:T(1,128)}) custom-call(s32[1]{0:T(128)} %bitcast.core, bf16[2,256,768]{2,1,0:T(8,128)(2,1)} %get-tuple-element.195.x_keep, bf16[2,256,768]{2,1,0:T(8,128)(2,1)} %copy-done.20, ...), custom_call_target="tpu_custom_call" | custom-call | flops 1207959552 | bytes 12582912 | tf_op jit(solution)/shard_map/norm_two_backward/pallas_call | solution.py:593
  279.8 20.0 %attend_backward.1 = (bf16[256,1536]{1,0:T(8,128)(2,1)}, bf16[2,1024,128]{2,1,0:T(8,128)(2,1)}, bf16[2,1024,128]{2,1,0:T(8,128)(2,1)}, bf16[2,1024,128]{2,1,0:T(8,128)(2,1)}, bf16[2,1024,128]{2,1,0:T(8,128)(2,1)}) custom-call(s32[6]{0:T(128)} %pad_add_fusion.info, bf16[256,1536]{1,0:T(8,128)(2,1)} %fusion.q_ref, bf16[256,1536]{1,0:T(8,128)(2,1)} %get-tuple-element.216.g_ref, ...), custom_call_target="tpu_custom_call" | custom-call | flops 4529848320 | bytes 8388608 | tf_op jit(solution)/shard_map/attend_backward/pallas_call | solution.py:839
  308.4 7.8 %collective-permute-done.41 = bf16[2,1024,128]{2,1,0:T(8,128)(2,1)S(1)} collective-permute-done((bf16[2,1024,128]{2,1,0:T(8,128)(2,1)S(1)}, bf16[2,1024,128]{2,1,0:T(8,128)(2,1)S(1)}, u32[]{:S(2)}, u32[]{:S(2)}) %collective-permute-start.41) | collective-permute-done | bytes 524320 | tf_op jit(solution)/shard_map/ppermute | solution.py:50
  319.2 3.6 fusion.20
  322.8 7.0 %split_rows.2 = (bf16[2,2,96,1536]{3,2,1,0:T(8,128)(2,1)}, bf16[2,2,96,1536]{3,2,1,0:T(8,128)(2,1)}, bf16[2,2,96,1536]{3,2,1,0:T(8,128)(2,1)}, bf16[2,2,96,1536]{3,2,1,0:T(8,128)(2,1)}) custom-call(s32[2]{0:T(128)} %pad_add_fusion.1.place, bf16[4,4,96,768]{3,2,1,0:T(8,128)(2,1)} %bitcast.124, bf16[4,4,96,768]{3,2,1,0:T(8,128)(2,1)} %bitcast.140, ...), custom_call_target="tpu_custom_call" | custom-call | flops 2359296 | bytes 14155776 | tf_op jit(solution)/shard_map/split_rows/pallas_call | solution.py:209
  337.5 4.3 convolution_convert_fusion.3
  341.8 6.7 %collective-permute-done.47 = bf16[2,256,256]{2,1,0:T(8,128)(2,1)S(1)} collective-permute-done((bf16[2,256,256]{2,1,0:T(8,128)(2,1)S(1)}, bf16[2,256,256]{2,1,0:T(8,128)(2,1)S(1)}, u32[]{:S(2)}, u32[]{:S(2)}) %collective-permute-start.47) | collective-permute-done | bytes 262176 | tf_op jit(solution)/shard_map/ppermute | solution.py:50
  350.7 6.1 %collective-permute-done.49 = bf16[2,2,96,1536]{3,2,1,0:T(8,128)(2,1)} collective-permute-done((bf16[2,2,96,1536]{3,2,1,0:T(8,128)(2,1)}, bf16[2,2,96,1536]{3,2,1,0:T(8,128)(2,1)}, u32[]{:S(2)}, u32[]{:S(2)}) %collective-permute-start.49) | collective-permute-done | bytes 1179680 | tf_op jit(solution)/shard_map/ppermute | solution.py:50
  370.4 5.5 %input_backward.1 = (bf16[256,1536]{1,0:T(8,128)(2,1)}, bf16[1536,256]{1,0:T(8,128)(2,1)}, bf16[1536,256]{1,0:T(8,128)(2,1)}) custom-call(s32[1]{0:T(128)} %bitcast.core, f32[256,1536]{1,0:T(8,128)} %convolution_add_fusion.partial, bf16[256,256]{1,0:T(8,128)(2,1)} %fusion.30.dkv, bf16[1536,128]{1,0:T(8,128)(2,1)} %slice.233.kv_own, ...), custom_call_target="tpu_custom_call" | custom-call | flops 402653184 | bytes 6291456 | tf_op jit(solution)/shard_map/input_backward/pallas_call | solution.py:645
  379.3 3.4 collective-permute-done.52
  409.0 4.3 collective-permute-done.62.p3
  430.4 5.6 %reduce-scatter.8.cloned.1.call-done = bf16[96,1792]{1,0:T(8,128)(2,1)} async-done(((bf16[384,1792]{1,0:T(8,128)(2,1)}), bf16[96,1792]{1,0:T(8,128)(2,1)}) %reduce-scatter.8.cloned.1.call-update) | async-done | bytes 344080 | tf_op jit(solution)/shard_map/reduce_scatter | solution.py:70
  (394 shorter events, 192.4 us)
Async XLA Ops:
  7.2 51.7 %all-gather.4.cloned.1.call-start = ((), (), s32[]{:S(2)}) async-start(), calls=%async_computation.3 | async-start | bytes 1474560 | tf_op jit(solution)/shard_map/all_gather | solution.py:64
  10.1 150.3 %all-gather.8.cloned.1.call-start = ((), (), s32[]{:S(2)}) async-start(), calls=%async_computation.5 | async-start | bytes 2211840 | tf_op jit(solution)/shard_map/all_gather | solution.py:64
  10.1 21.8 %collective-permute-start.1 = (bf16[256,1536]{1,0:T(8,128)(2,1)}, bf16[256,1536]{1,0:T(8,128)(2,1)}, u32[]{:S(2)}, u32[]{:S(2)}) collective-permute-start(bf16[256,1536]{1,0:T(8,128)(2,1)} %bitcast.144), channel_id=1, source_target_pairs={{0,2},{1,3},{2,0},{3,1},{4,6},{5,7},{6,4},{7,5},{8,10},{9,11},{10,... | collective-permute-start | bytes 2359304 | tf_op jit(solution)/shard_map/ppermute | solution.py:50
  15.5 162.3 %all-gather.6.cloned.1.call-start = ((), (), s32[]{:S(2)}) async-start(), calls=%async_computation.4 | async-start | bytes 4423680 | tf_op jit(solution)/shard_map/all_gather | solution.py:64
  61.1 30.9 %collective-permute-start.11 = (bf16[4,96,768]{2,1,0:T(8,128)(2,1)}, bf16[4,96,768]{2,1,0:T(8,128)(2,1)}, u32[]{:S(2)}, u32[]{:S(2)}) collective-permute-start(bf16[4,96,768]{2,1,0:T(8,128)(2,1)} %bitcast.11.own), channel_id=1, source_target_pairs={{0,2},{1,3},{2,0},{3,1},{4,6},{5,7},{6,4},{7,5},{8,10},{9,11},{10,... | collective-permute-start | bytes 1769480 | tf_op jit(solution)/shard_map/ppermute | solution.py:50
  61.7 30.3 %collective-permute-start.10 = (bf16[4,96,768]{2,1,0:T(8,128)(2,1)}, bf16[4,96,768]{2,1,0:T(8,128)(2,1)}, u32[]{:S(2)}, u32[]{:S(2)}) collective-permute-start(bf16[4,96,768]{2,1,0:T(8,128)(2,1)} %bitcast.11.own), channel_id=1, source_target_pairs={{0,1},{1,0},{2,3},{3,2},{4,5},{5,4},{6,7},{7,6},{8,9},{9,8},{10,11... | collective-permute-start | bytes 1769480 | tf_op jit(solution)/shard_map/ppermute | solution.py:50
  62.3 29.7 %collective-permute-start.13 = (bf16[4,96,768]{2,1,0:T(8,128)(2,1)S(1)}, bf16[4,96,768]{2,1,0:T(8,128)(2,1)}, u32[]{:S(2)}, u32[]{:S(2)}) collective-permute-start(bf16[4,96,768]{2,1,0:T(8,128)(2,1)S(1)} %bitcast.137), channel_id=1, source_target_pairs={{0,2},{1,3},{2,0},{3,1},{4,6},{5,7},{6,4},{7,5},{8,10},{9,11},{10,... | collective-permute-start | bytes 1769480 | tf_op jit(solution)/shard_map/ppermute | solution.py:50
  63.6 28.3 %collective-permute-start.12 = (bf16[4,96,768]{2,1,0:T(8,128)(2,1)S(1)}, bf16[4,96,768]{2,1,0:T(8,128)(2,1)}, u32[]{:S(2)}, u32[]{:S(2)}) collective-permute-start(bf16[4,96,768]{2,1,0:T(8,128)(2,1)S(1)} %bitcast.138), channel_id=1, source_target_pairs={{0,1},{1,0},{2,3},{3,2},{4,5},{5,4},{6,7},{7,6},{8,9},{9,8},{10,11... | collective-permute-start | bytes 1769480 | tf_op jit(solution)/shard_map/ppermute | solution.py:50
  69.1 266.6 %reduce-scatter.4.cloned.1.call-start = ((), (), s32[]{:S(2)}) async-start(), calls=%async_computation.6 | async-start | bytes 4423680 | tf_op jit(solution)/shard_map/reduce_scatter | solution.py:70
  92.0 23.3 %collective-permute-start.15 = (bf16[1024,256]{1,0:T(8,128)(2,1)S(1)}, bf16[1024,256]{1,0:T(8,128)(2,1)S(1)}, u32[]{:S(2)}, u32[]{:S(2)}) collective-permute-start(bf16[1024,256]{1,0:T(8,128)(2,1)S(1)} %all_gather.17.k0), channel_id=1, source_target_pairs={{0,2},{1,3},{2,0},{3,1},{4,6},{5,7},{6,4},{7,5},{8,10},{9,11},{10,... | collective-permute-start | bytes 1572872 | tf_op jit(solution)/shard_map/ppermute | solution.py:50
  92.8 22.5 %collective-permute-start.14 = (bf16[1024,256]{1,0:T(8,128)(2,1)S(1)}, bf16[1024,256]{1,0:T(8,128)(2,1)S(1)}, u32[]{:S(2)}, u32[]{:S(2)}) collective-permute-start(bf16[1024,256]{1,0:T(8,128)(2,1)S(1)} %all_gather.17.k0), channel_id=1, source_target_pairs={{0,1},{1,0},{2,3},{3,2},{4,5},{5,4},{6,7},{7,6},{8,9},{9,8},{10,11... | collective-permute-start | bytes 1572872 | tf_op jit(solution)/shard_map/ppermute | solution.py:50
  94.3 19.6 %collective-permute-start.17 = (bf16[2,96,768]{2,1,0:T(8,128)(2,1)S(1)}, bf16[2,96,768]{2,1,0:T(8,128)(2,1)S(1)}, u32[]{:S(2)}, u32[]{:S(2)}) collective-permute-start(bf16[2,96,768]{2,1,0:T(8,128)(2,1)S(1)} %slice.238), channel_id=1, source_target_pairs={{0,1},{1,0},{2,3},{3,2},{4,5},{5,4},{6,7},{7,6},{8,9},{9,8},{10,11... | collective-permute-start | bytes 884744 | tf_op jit(solution)/shard_map/ppermute | solution.py:50
  100.2 20.1 %collective-permute-start.21 = (bf16[2,96,768]{2,1,0:T(8,128)(2,1)S(1)}, bf16[2,96,768]{2,1,0:T(8,128)(2,1)S(1)}, u32[]{:S(2)}, u32[]{:S(2)}) collective-permute-start(bf16[2,96,768]{2,1,0:T(8,128)(2,1)S(1)} %slice.242), channel_id=1, source_target_pairs={{0,1},{1,0},{2,3},{3,2},{4,5},{5,4},{6,7},{7,6},{8,9},{9,8},{10,11... | collective-permute-start | bytes 884744 | tf_op jit(solution)/shard_map/ppermute | solution.py:50
  128.1 23.1 %collective-permute-start.25 = (bf16[1536,768]{1,0:T(8,128)(2,1)}, bf16[1536,768]{1,0:T(8,128)(2,1)}, u32[]{:S(2)}, u32[]{:S(2)}) collective-permute-start(bf16[1536,768]{1,0:T(8,128)(2,1)} %bitcast.120), channel_id=1, source_target_pairs={{0,16},{16,0},{1,17},{17,1},{2,18},{18,2},{3,19},{19,3},{4,20},{20... | collective-permute-start | bytes 7077896 | tf_op jit(solution)/shard_map/ppermute | solution.py:55
  157.4 19.4 %collective-permute-start.27 = (bf16[256,1536]{1,0:T(8,128)(2,1)}, bf16[256,1536]{1,0:T(8,128)(2,1)}, u32[]{:S(2)}, u32[]{:S(2)}) collective-permute-start(bf16[256,1536]{1,0:T(8,128)(2,1)} %get-tuple-element.184.h0), channel_id=1, source_target_pairs={{0,2},{1,3},{2,0},{3,1},{4,6},{5,7},{6,4},{7,5},{8,10},{9,11},{10,... | collective-permute-start | bytes 2359304 | tf_op jit(solution)/shard_map/ppermute | solution.py:50
  158.4 19.4 %collective-permute-start.26 = (bf16[256,1536]{1,0:T(8,128)(2,1)}, bf16[256,1536]{1,0:T(8,128)(2,1)}, u32[]{:S(2)}, u32[]{:S(2)}) collective-permute-start(bf16[256,1536]{1,0:T(8,128)(2,1)} %get-tuple-element.184.h0), channel_id=1, source_target_pairs={{0,1},{1,0},{2,3},{3,2},{4,5},{5,4},{6,7},{7,6},{8,9},{9,8},{10,11... | collective-permute-start | bytes 2359304 | tf_op jit(solution)/shard_map/ppermute | solution.py:50
  265.2 136.5 %reduce-scatter.6.cloned.1.call-start = ((), (), s32[]{:S(2)}) async-start(), calls=%async_computation.7 | async-start | bytes 2211840 | tf_op jit(solution)/shard_map/reduce_scatter | solution.py:70
  268.6 31.2 %collective-permute-start.38 = (bf16[2,256,768]{2,1,0:T(8,128)(2,1)}, bf16[2,256,768]{2,1,0:T(8,128)(2,1)}, u32[]{:S(2)}, u32[]{:S(2)}) collective-permute-start(bf16[2,256,768]{2,1,0:T(8,128)(2,1)} %bitcast.19), channel_id=1, source_target_pairs={{0,2},{1,3},{2,0},{3,1},{4,6},{5,7},{6,4},{7,5},{8,10},{9,11},{10,... | collective-permute-start | bytes 2359304 | tf_op jit(solution)/shard_map/ppermute | solution.py:50
  269.8 29.9 %collective-permute-start.37 = (bf16[2,256,768]{2,1,0:T(8,128)(2,1)}, bf16[2,256,768]{2,1,0:T(8,128)(2,1)}, u32[]{:S(2)}, u32[]{:S(2)}) collective-permute-start(bf16[2,256,768]{2,1,0:T(8,128)(2,1)} %bitcast.18), channel_id=1, source_target_pairs={{0,1},{1,0},{2,3},{3,2},{4,5},{5,4},{6,7},{7,6},{8,9},{9,8},{10,11... | collective-permute-start | bytes 2359304 | tf_op jit(solution)/shard_map/ppermute | solution.py:50
  329.9 26.9 %collective-permute-start.49 = (bf16[2,2,96,1536]{3,2,1,0:T(8,128)(2,1)}, bf16[2,2,96,1536]{3,2,1,0:T(8,128)(2,1)}, u32[]{:S(2)}, u32[]{:S(2)}) collective-permute-start(bf16[2,2,96,1536]{3,2,1,0:T(8,128)(2,1)} %get-tuple-element.256), channel_id=1, source_target_pairs={{0,1},{1,0},{2,3},{3,2},{4,5},{5,4},{6,7},{7,6},{8,9},{9,8},{10,11... | collective-permute-start | bytes 3538952 | tf_op jit(solution)/shard_map/ppermute | solution.py:50
  330.8 26.9 %collective-permute-start.50 = (bf16[2,2,96,1536]{3,2,1,0:T(8,128)(2,1)}, bf16[2,2,96,1536]{3,2,1,0:T(8,128)(2,1)}, u32[]{:S(2)}, u32[]{:S(2)}) collective-permute-start(bf16[2,2,96,1536]{3,2,1,0:T(8,128)(2,1)} %get-tuple-element.257), channel_id=1, source_target_pairs={{0,2},{1,3},{2,0},{3,1},{4,6},{5,7},{6,4},{7,5},{8,10},{9,11},{10,... | collective-permute-start | bytes 3538952 | tf_op jit(solution)/shard_map/ppermute | solution.py:50
  363.1 72.9 %reduce-scatter.8.cloned.1.call-start = ((), (), s32[]{:S(2)}) async-start(), calls=%async_computation.8 | async-start | bytes 1720320 | tf_op jit(solution)/shard_map/reduce_scatter | solution.py:70
  369.4 19.9 %collective-permute-start.53 = (bf16[2,96,1536]{2,1,0:T(8,128)(2,1)S(1)}, bf16[2,96,1536]{2,1,0:T(8,128)(2,1)S(1)}, u32[]{:S(2)}, u32[]{:S(2)}) collective-permute-start(bf16[2,96,1536]{2,1,0:T(8,128)(2,1)S(1)} %fusion.12), channel_id=1, source_target_pairs={{0,1},{1,0},{2,3},{3,2},{4,5},{5,4},{6,7},{7,6},{8,9},{9,8},{10,11... | collective-permute-start | bytes 1769480 | tf_op jit(solution)/shard_map/ppermute | solution.py:50
  378.4 43.0 %collective-permute-start.39 = (bf16[256,768]{1,0:T(8,128)(2,1)}, bf16[256,768]{1,0:T(8,128)(2,1)}, u32[]{:S(2)}, u32[]{:S(2)}) collective-permute-start(bf16[256,768]{1,0:T(8,128)(2,1)} %get-tuple-element.226), channel_id=1, source_target_pairs={{0,2},{1,3},{2,0},{3,1},{4,6},{5,7},{6,4},{7,5},{8,10},{9,11},{10,... | collective-permute-start | bytes 1179656 | tf_op jit(solution)/shard_map/ppermute | solution.py:50
  (121 other events, 1213.0 us)
Sparse Core Ops, SparseCore 0:
  10.2 34.3 all-gather.3
  46.2 48.0 all-gather.7
  96.4 68.8 all-gather.5
  265.3 67.0 reduce-scatter.3
  363.2 38.4 reduce-scatter.5
  404.6 31.3 reduce-scatter.7

commit v4 on v3

--- a/solution.py
+++ b/solution.py
@@ -850,13 +850,6 @@
         grad_attn,
         hidden,
     )
-    out_x_last, out_y_last = pass_plane((one[0], one[3]), out_x, (two[0], two[1]), out_y)
-    out_sum = (
-        one[0].astype(f32) + out_x[0].astype(f32) + out_x_last.astype(f32),
-        two[0].astype(f32) + out_y[1].astype(f32) + out_y_last.astype(f32),
-    )
-    block_output = (residual + in_order(*out_sum)).astype(bf16).reshape(tokens.shape)
-
     dq_own, dq_other = halves(grad_queries)
     da_own, da_other = halves(grad_attn)
     attn_mine = product_tn(attended, da_own).astype(bf16)
@@ -885,16 +878,16 @@
     def first_step():
         return (
             product_tn(hidden, up_own).astype(bf16),
-            product_tn(hidden, up_other).astype(bf16),
+            peer(product_tn(hidden, up_other).astype(bf16)),
         )
 
     def second_step(down_mine, down_peer):
-        return partial, down_mine, down_peer, attn_x, attn_y
-
-    grad_keyvals, (partial, down_mine, down_peer, attn_x, attn_y) = halve_column(
+        down_sum = (down_mine.astype(f32) + down_peer.astype(f32)).astype(bf16)
+        return partial, down_sum, attn_x, attn_y
+
+    grad_keyvals, (partial, down_sum, attn_x, attn_y) = halve_column(
         grad_kv.reshape(lead, token_count, -1), first_step, second_step
     )
-    grad_keyvals, down_sum = tie(grad_keyvals, chip_sum(down_mine, down_peer))
     down_grad = scatter_column(down_sum)
     wide_grad = wide_grad.reshape(plane, my_rows, part)
     input_grad, last_own, last_other = input_backward(
@@ -922,10 +915,17 @@
     last_plane = joined(
         last_x_keep, last_x, last_x_last, last_y_keep, last_y, last_y_last, 0
     ).reshape(lead * my_rows, -1)
-    last_plane, down_grad = tie(last_plane, down_grad)
+    last_plane, down_grad, out_x, out_y = tie(last_plane, down_grad, out_x, out_y)
     last_share = scatter_column(
         jnp.concatenate([attn_plane, last_plane], axis=1)
     )
+
+    out_x_last, out_y_last = pass_plane((one[0], one[3]), out_x, (two[0], two[1]), out_y)
+    out_sum = (
+        one[0].astype(f32) + out_x[0].astype(f32) + out_x_last.astype(f32),
+        two[0].astype(f32) + out_y[1].astype(f32) + out_y_last.astype(f32),
+    )
+    block_output = (residual + in_order(*out_sum)).astype(bf16).reshape(tokens.shape)
 
     wide_back = []
     for mask in range(plane):

time: 456 us -> 471 us (1.033)
  waiting for transfers between devices: 118 us -> 130 us
    reduce_scatter x3, waiting for transfers between devices: 6.61 us -> 17.6 us  [scatter_column(): lax.psum_scatter(value, 'shard', scatter_dimension=0, tiled=True, axis_in...]
  transfers between devices with their start and end apart: 71 -> 71, of which waited for: 36 -> 30; matrix products, arithmetic and copies ran while one was open for 20% -> 21% of each run, Pallas kernels for 16% -> 16%
where the time goes in v4:
time: 471 us; the launch traced here: 462 us
  waiting for transfers between devices  130 us (28%)
  Pallas kernels  112 us (24%)
  starting transfers between devices  58.1 us (12%)
  matrix products  41 us (9%)
  blocking collectives  38.5 us (8%)
  other arithmetic  35.3 us (7%)
  local copies, waits for them, and re-layouts  31.3 us (7%)
  between operations  15.7 us (3%)
    ppermute x52, waiting for transfers between devices, across(): return lax.ppermute(value, 'shard', [(i, i ^ mask) for i in range(count)])  110 us
    ppermute x52, starting transfers between devices, across(): return lax.ppermute(value, 'shard', [(i, i ^ mask) for i in range(count)])  55.9 us
    all_gather x2, blocking collectives, gather_column(): lax.all_gather(value, 'shard', axis=0, tiled=True, axis_index_groups=colu...  38.5 us
    pallas_call x1, Pallas kernels, feed_forward(): pl.pallas_call(feed_kernel, out_shape=(shape((count, width), bf16),) * 2...  38 us
    dot_general x8, matrix products, product_tn(): lax.dot_general(first_op, second_op, (((0,), (0,)), ((), ())), preferred_...  25.9 us
    pallas_call x1, Pallas kernels, on_device(): backward(info, queries, grad_mixed, logsum, *kv_blocks)  20 us
    reduce_scatter x3, waiting for transfers between devices, scatter_column(): lax.psum_scatter(value, 'shard', scatter_dimension=0, tiled=True, axis_in...  17.6 us
    pallas_call x1, Pallas kernels, on_device(): attended, logsum = forward(info, queries, *kv_blocks)  12.8 us
  transfers between devices with their start and end apart: 71, of which 30 were waited for; matrix products, arithmetic and copies ran while one was open for 21% of the time, Pallas kernels for 16%

profile of v4, /device:TPU:0, one launch (start us, length us, event | category | flops | bytes accessed | tf_op | source)
XLA Modules:
  0.0 461.8 jit_solution(15302227193892463437)
XLA Ops:
  16.1 15.7 %all_gather.15 = bf16[384,256]{1,0:T(8,128)(2,1)} all-gather(bf16[96,256]{1,0:T(8,128)(2,1)S(1)} %copy.39), channel_id=1, replica_groups={{0,4,8,12},{1,5,9,13},{2,6,10,14},{3,7,11,15},{16,20,24,28},{17,21,25,2..., dimensions={0}, use_global_device_ids=true | all-gather | bytes 245760 | tf_op jit(solution)/shard_map/all_gather | solution.py:64
  49.3 5.8 %collective-permute-done.8 = bf16[1,96,1152]{2,1,0:T(8,128)(2,1)S(1)} collective-permute-done((bf16[1,96,1152]{2,1,0:T(8,128)(2,1)S(1)}, bf16[1,96,1152]{2,1,0:T(8,128)(2,1)S(1)}, u32[]{:S(2)}, u32[]{:S(2)}) %collective-permute-start.8) | collective-permute-done | bytes 221216 | tf_op jit(solution)/shard_map/ppermute | solution.py:50
  69.2 22.8 %all_gather.17.k0 = bf16[1024,256]{1,0:T(8,128)(2,1)S(1)} all-gather(bf16[256,256]{1,0:T(8,128)(2,1)S(1)} %fusion.27), channel_id=1, replica_groups={{0,4,8,12},{1,5,9,13},{2,6,10,14},{3,7,11,15},{16,20,24,28},{17,21,25,2..., dimensions={0}, use_global_device_ids=true | all-gather | bytes 655360 | tf_op jit(solution)/shard_map/all_gather | solution.py:64
  100.9 13.1 %collective-permute-done.17.far_bottom = bf16[2,96,768]{2,1,0:T(8,128)(2,1)S(1)} collective-permute-done((bf16[2,96,768]{2,1,0:T(8,128)(2,1)S(1)}, bf16[2,96,768]{2,1,0:T(8,128)(2,1)S(1)}, u32[]{:S(2)}, u32[]{:S(2)}) %collective-permute-start.17) | collective-permute-done | bytes 294944 | tf_op jit(solution)/shard_map/ppermute | solution.py:50
  138.4 12.8 %attend_forward.1 = (bf16[256,1536]{1,0:T(8,128)(2,1)}, f32[4,768,1]{2,1,0:T(8,128)}) custom-call(s32[6]{0:T(128)} %pad_add_fusion.info, bf16[256,1536]{1,0:T(8,128)(2,1)} %fusion.q_ref, bf16[1024,256]{1,0:T(8,128)(2,1)} %copy-done.27, bf16[1024,256]{1,0:T(8,128)(2,1)} %copy-done.51, bf16[1024,256]{1,0:T(8,128)(2,1)} %copy-done.50, ...), custom_call_target="tpu_custom_call" | custom-call | flops 1811939328 | bytes 4194304 | tf_op jit(solution)/shard_map/attend_forward/pallas_call | solution.py:779
  151.3 6.1 %outproj_norm.1 = (f32[256,1536]{1,0:T(8,128)}, bf16[256,1536]{1,0:T(8,128)(2,1)}) custom-call(s32[1]{0:T(128)} %bitcast.core, bf16[256,1536]{1,0:T(8,128)(2,1)} %get-tuple-element.176.att, bf16[1536,768]{1,0:T(8,128)(2,1)} %bitcast.121, bf16[1536,768]{1,0:T(8,128)(2,1)} %collective-permute-done.25.other, bf16[256,1536]{1,0:T(8,128)(2,1)} %bitcast.125, ...), custom_call_target="tpu_custom_call" | custom-call | flops 1207959552 | bytes 8650752 | tf_op jit(solution)/shard_map/outproj_norm/pallas_call | solution.py:460
  160.2 16.6 %collective-permute-done.27.h2 = bf16[256,1536]{1,0:T(8,128)(2,1)} collective-permute-done((bf16[256,1536]{1,0:T(8,128)(2,1)}, bf16[256,1536]{1,0:T(8,128)(2,1)}, u32[]{:S(2)}, u32[]{:S(2)}) %collective-permute-start.27) | collective-permute-done | bytes 786464 | tf_op jit(solution)/shard_map/ppermute | solution.py:50
  182.8 8.4 %collective-permute-done.29.h4 = bf16[128,1536]{1,0:T(8,128)(2,1)S(1)} collective-permute-done((bf16[128,1536]{1,0:T(8,128)(2,1)S(1)}, bf16[128,1536]{1,0:T(8,128)(2,1)S(1)}, u32[]{:S(2)}, u32[]{:S(2)}) %collective-permute-start.29) | collective-permute-done | bytes 393248 | tf_op jit(solution)/shard_map/ppermute | solution.py:50
  194.0 38.0 %feed_forward.1 = (bf16[1024,1536]{1,0:T(8,128)(2,1)}, bf16[1024,1536]{1,0:T(8,128)(2,1)}, bf16[1024,1152]{1,0:T(8,128)(2,1)}, bf16[1024,1152]{1,0:T(8,128)(2,1)...) custom-call(s32[1]{0:T(128)} %bitcast.core, ...), custom_call_target="tpu_custom_call" | custom-call | flops 18119393280 | bytes 28311552 | tf_op jit(solution)/shard_map/feed_forward/pallas_call | solution.py:547
  233.3 7.0 %convolution_convert_fusion.1 = bf16[1536,1152]{1,0:T(8,128)(2,1)S(1)} fusion(bf16[1024,1536]{1,0:T(8,128)(2,1)} %get-tuple-element.197, bf16[1024,1152]{1,0:T(8,128)(2,1)} %get-tuple-element.198), kind=kOutput, calls=%fused_computation.1 | convolution fusion | flops 3625648128 | bytes 9043968 | tf_op jit(solution)/shard_map/dot_general | solution.py:28
  240.4 4.6 convolution_convert_fusion
  245.0 5.6 %collective-permute-done.32.x_got = bf16[2,256,768]{2,1,0:T(8,128)(2,1)S(1)} collective-permute-done((bf16[2,256,768]{2,1,0:T(8,128)(2,1)}, bf16[2,256,768]{2,1,0:T(8,128)(2,1)S(1)}, u32[]{:S(2)}, u32[]{:S(2)}) %collective-permute-start.32) | collective-permute-done | bytes 786464 | tf_op jit(solution)/shard_map/ppermute | solution.py:50
  271.1 8.7 %norm_two_backward.1 = (f32[256,1536]{1,0:T(8,128)}, bf16[256,1536]{1,0:T(8,128)(2,1)}, bf16[256,1536]{1,0:T(8,128)(2,1)}, f32[1,1536]{1,0:T(1,128)}) custom-call(s32[1]{0:T(128)} %bitcast.core, bf16[2,256,768]{2,1,0:T(8,128)(2,1)} %get-tuple-element.194.x_keep, bf16[2,256,768]{2,1,0:T(8,128)(2,1)} %copy-done.18, ...), custom_call_target="tpu_custom_call" | custom-call | flops 1207959552 | bytes 12582912 | tf_op jit(solution)/shard_map/norm_two_backward/pallas_call | solution.py:593
  279.8 20.0 %attend_backward.1 = (bf16[256,1536]{1,0:T(8,128)(2,1)}, bf16[2,1024,128]{2,1,0:T(8,128)(2,1)}, bf16[2,1024,128]{2,1,0:T(8,128)(2,1)}, bf16[2,1024,128]{2,1,0:T(8,128)(2,1)}, bf16[2,1024,128]{2,1,0:T(8,128)(2,1)}) custom-call(s32[6]{0:T(128)} %pad_add_fusion.info, bf16[256,1536]{1,0:T(8,128)(2,1)} %fusion.q_ref, bf16[256,1536]{1,0:T(8,128)(2,1)} %get-tuple-element.215.g_ref, ...), custom_call_target="tpu_custom_call" | custom-call | flops 4529848320 | bytes 8388608 | tf_op jit(solution)/shard_map/attend_backward/pallas_call | solution.py:839
  308.6 7.7 %collective-permute-done.39 = bf16[2,1024,128]{2,1,0:T(8,128)(2,1)S(1)} collective-permute-done((bf16[2,1024,128]{2,1,0:T(8,128)(2,1)S(1)}, bf16[2,1024,128]{2,1,0:T(8,128)(2,1)S(1)}, u32[]{:S(2)}, u32[]{:S(2)}) %collective-permute-start.39) | collective-permute-done | bytes 524320 | tf_op jit(solution)/shard_map/ppermute | solution.py:50
  320.9 7.2 %split_rows.2 = (bf16[2,2,96,1536]{3,2,1,0:T(8,128)(2,1)}, bf16[2,2,96,1536]{3,2,1,0:T(8,128)(2,1)}, bf16[2,2,96,1536]{3,2,1,0:T(8,128)(2,1)}, bf16[2,2,96,1536]{3,2,1,0:T(8,128)(2,1)}) custom-call(s32[2]{0:T(128)} %pad_add_fusion.1.place, bf16[4,4,96,768]{3,2,1,0:T(8,128)(2,1)} %bitcast.124, bf16[4,4,96,768]{3,2,1,0:T(8,128)(2,1)} %bitcast.140, ...), custom_call_target="tpu_custom_call" | custom-call | flops 2359296 | bytes 14155776 | tf_op jit(solution)/shard_map/split_rows/pallas_call | solution.py:209
  328.1 4.7 %convolution_convert_fusion.2 = bf16[1152,768]{1,0:T(8,128)(2,1)} fusion(bf16[1024,1152]{1,0:T(8,128)(2,1)S(1)} %copy-done.69, bf16[1024,1536]{1,0:T(8,128)(2,1)} %get-tuple-element.247, s32[]{:T(128)S(6)} %select_n.147), kind=kOutput, calls=%fused_computation.4 | convolution fusion | flops 1812824064 | bytes 5701636 | tf_op jit(solution)/shard_map/dot_general | solution.py:28
  345.7 9.4 %collective-permute-done.45 = bf16[2,256,256]{2,1,0:T(8,128)(2,1)S(1)} collective-permute-done((bf16[2,256,256]{2,1,0:T(8,128)(2,1)S(1)}, bf16[2,256,256]{2,1,0:T(8,128)(2,1)S(1)}, u32[]{:S(2)}, u32[]{:S(2)}) %collective-permute-start.45) | collective-permute-done | bytes 262176 | tf_op jit(solution)/shard_map/ppermute | solution.py:50
  358.6 7.4 %collective-permute-done.48 = bf16[2,2,96,1536]{3,2,1,0:T(8,128)(2,1)} collective-permute-done((bf16[2,2,96,1536]{3,2,1,0:T(8,128)(2,1)}, bf16[2,2,96,1536]{3,2,1,0:T(8,128)(2,1)}, u32[]{:S(2)}, u32[]{:S(2)}) %collective-permute-start.48) | collective-permute-done | bytes 1179680 | tf_op jit(solution)/shard_map/ppermute | solution.py:50
  374.9 5.6 %input_backward.1 = (bf16[256,1536]{1,0:T(8,128)(2,1)}, bf16[1536,256]{1,0:T(8,128)(2,1)}, bf16[1536,256]{1,0:T(8,128)(2,1)}) custom-call(s32[1]{0:T(128)} %bitcast.core, f32[256,1536]{1,0:T(8,128)} %convolution_add_fusion.partial, bf16[256,256]{1,0:T(8,128)(2,1)} %fusion.30.dkv, bf16[1536,128]{1,0:T(8,128)(2,1)} %slice.233.kv_own, ...), custom_call_target="tpu_custom_call" | custom-call | flops 402653184 | bytes 6291456 | tf_op jit(solution)/shard_map/input_backward/pallas_call | solution.py:645
  383.6 11.2 %collective-permute-done.61.p2 = bf16[96,1152]{1,0:T(8,128)(2,1)S(1)} collective-permute-done((bf16[96,1152]{1,0:T(8,128)(2,1)S(1)}, bf16[96,1152]{1,0:T(8,128)(2,1)S(1)}, u32[]{:S(2)}, u32[]{:S(2)}) %collective-permute-start.61) | collective-permute-done | bytes 221216 | tf_op jit(solution)/shard_map/ppermute | solution.py:50
  405.9 3.7 collective-permute-done.51
  424.6 4.2 collective-permute-done.55
  432.5 17.6 %reduce-scatter.8.cloned.1.call-done = bf16[96,1792]{1,0:T(8,128)(2,1)} async-done(((bf16[384,1792]{1,0:T(8,128)(2,1)}), bf16[96,1792]{1,0:T(8,128)(2,1)}) %reduce-scatter.8.cloned.1.call-update) | async-done | bytes 344080 | tf_op jit(solution)/shard_map/reduce_scatter | solution.py:70
  (392 shorter events, 182.3 us)
Async XLA Ops:
  7.2 51.7 %all-gather.4.cloned.1.call-start = ((), (), s32[]{:S(2)}) async-start(), calls=%async_computation.3 | async-start | bytes 1474560 | tf_op jit(solution)/shard_map/all_gather | solution.py:64
  10.1 150.1 %all-gather.8.cloned.1.call-start = ((), (), s32[]{:S(2)}) async-start(), calls=%async_computation.5 | async-start | bytes 2211840 | tf_op jit(solution)/shard_map/all_gather | solution.py:64
  10.1 21.8 %collective-permute-start.1 = (bf16[256,1536]{1,0:T(8,128)(2,1)}, bf16[256,1536]{1,0:T(8,128)(2,1)}, u32[]{:S(2)}, u32[]{:S(2)}) collective-permute-start(bf16[256,1536]{1,0:T(8,128)(2,1)} %bitcast.144), channel_id=1, source_target_pairs={{0,2},{1,3},{2,0},{3,1},{4,6},{5,7},{6,4},{7,5},{8,10},{9,11},{10,... | collective-permute-start | bytes 2359304 | tf_op jit(solution)/shard_map/ppermute | solution.py:50
  15.5 162.1 %all-gather.6.cloned.1.call-start = ((), (), s32[]{:S(2)}) async-start(), calls=%async_computation.4 | async-start | bytes 4423680 | tf_op jit(solution)/shard_map/all_gather | solution.py:64
  61.1 30.9 %collective-permute-start.11 = (bf16[4,96,768]{2,1,0:T(8,128)(2,1)}, bf16[4,96,768]{2,1,0:T(8,128)(2,1)}, u32[]{:S(2)}, u32[]{:S(2)}) collective-permute-start(bf16[4,96,768]{2,1,0:T(8,128)(2,1)} %bitcast.11.own), channel_id=1, source_target_pairs={{0,2},{1,3},{2,0},{3,1},{4,6},{5,7},{6,4},{7,5},{8,10},{9,11},{10,... | collective-permute-start | bytes 1769480 | tf_op jit(solution)/shard_map/ppermute | solution.py:50
  61.7 30.3 %collective-permute-start.10 = (bf16[4,96,768]{2,1,0:T(8,128)(2,1)}, bf16[4,96,768]{2,1,0:T(8,128)(2,1)}, u32[]{:S(2)}, u32[]{:S(2)}) collective-permute-start(bf16[4,96,768]{2,1,0:T(8,128)(2,1)} %bitcast.11.own), channel_id=1, source_target_pairs={{0,1},{1,0},{2,3},{3,2},{4,5},{5,4},{6,7},{7,6},{8,9},{9,8},{10,11... | collective-permute-start | bytes 1769480 | tf_op jit(solution)/shard_map/ppermute | solution.py:50
  62.3 29.7 %collective-permute-start.13 = (bf16[4,96,768]{2,1,0:T(8,128)(2,1)S(1)}, bf16[4,96,768]{2,1,0:T(8,128)(2,1)}, u32[]{:S(2)}, u32[]{:S(2)}) collective-permute-start(bf16[4,96,768]{2,1,0:T(8,128)(2,1)S(1)} %bitcast.137), channel_id=1, source_target_pairs={{0,2},{1,3},{2,0},{3,1},{4,6},{5,7},{6,4},{7,5},{8,10},{9,11},{10,... | collective-permute-start | bytes 1769480 | tf_op jit(solution)/shard_map/ppermute | solution.py:50
  63.7 28.4 %collective-permute-start.12 = (bf16[4,96,768]{2,1,0:T(8,128)(2,1)S(1)}, bf16[4,96,768]{2,1,0:T(8,128)(2,1)}, u32[]{:S(2)}, u32[]{:S(2)}) collective-permute-start(bf16[4,96,768]{2,1,0:T(8,128)(2,1)S(1)} %bitcast.138), channel_id=1, source_target_pairs={{0,1},{1,0},{2,3},{3,2},{4,5},{5,4},{6,7},{7,6},{8,9},{9,8},{10,11... | collective-permute-start | bytes 1769480 | tf_op jit(solution)/shard_map/ppermute | solution.py:50
  69.1 271.3 %reduce-scatter.4.cloned.1.call-start = ((), (), s32[]{:S(2)}) async-start(), calls=%async_computation.6 | async-start | bytes 4423680 | tf_op jit(solution)/shard_map/reduce_scatter | solution.py:70
  92.1 23.3 %collective-permute-start.15 = (bf16[1024,256]{1,0:T(8,128)(2,1)S(1)}, bf16[1024,256]{1,0:T(8,128)(2,1)S(1)}, u32[]{:S(2)}, u32[]{:S(2)}) collective-permute-start(bf16[1024,256]{1,0:T(8,128)(2,1)S(1)} %all_gather.17.k0), channel_id=1, source_target_pairs={{0,2},{1,3},{2,0},{3,1},{4,6},{5,7},{6,4},{7,5},{8,10},{9,11},{10,... | collective-permute-start | bytes 1572872 | tf_op jit(solution)/shard_map/ppermute | solution.py:50
  92.8 22.6 %collective-permute-start.14 = (bf16[1024,256]{1,0:T(8,128)(2,1)S(1)}, bf16[1024,256]{1,0:T(8,128)(2,1)S(1)}, u32[]{:S(2)}, u32[]{:S(2)}) collective-permute-start(bf16[1024,256]{1,0:T(8,128)(2,1)S(1)} %all_gather.17.k0), channel_id=1, source_target_pairs={{0,1},{1,0},{2,3},{3,2},{4,5},{5,4},{6,7},{7,6},{8,9},{9,8},{10,11... | collective-permute-start | bytes 1572872 | tf_op jit(solution)/shard_map/ppermute | solution.py:50
  94.4 19.6 %collective-permute-start.17 = (bf16[2,96,768]{2,1,0:T(8,128)(2,1)S(1)}, bf16[2,96,768]{2,1,0:T(8,128)(2,1)S(1)}, u32[]{:S(2)}, u32[]{:S(2)}) collective-permute-start(bf16[2,96,768]{2,1,0:T(8,128)(2,1)S(1)} %slice.238), channel_id=1, source_target_pairs={{0,1},{1,0},{2,3},{3,2},{4,5},{5,4},{6,7},{7,6},{8,9},{9,8},{10,11... | collective-permute-start | bytes 884744 | tf_op jit(solution)/shard_map/ppermute | solution.py:50
  100.2 20.1 %collective-permute-start.21 = (bf16[2,96,768]{2,1,0:T(8,128)(2,1)S(1)}, bf16[2,96,768]{2,1,0:T(8,128)(2,1)S(1)}, u32[]{:S(2)}, u32[]{:S(2)}) collective-permute-start(bf16[2,96,768]{2,1,0:T(8,128)(2,1)S(1)} %slice.242), channel_id=1, source_target_pairs={{0,1},{1,0},{2,3},{3,2},{4,5},{5,4},{6,7},{7,6},{8,9},{9,8},{10,11... | collective-permute-start | bytes 884744 | tf_op jit(solution)/shard_map/ppermute | solution.py:50
  128.0 23.3 %collective-permute-start.25 = (bf16[1536,768]{1,0:T(8,128)(2,1)}, bf16[1536,768]{1,0:T(8,128)(2,1)}, u32[]{:S(2)}, u32[]{:S(2)}) collective-permute-start(bf16[1536,768]{1,0:T(8,128)(2,1)} %bitcast.120), channel_id=1, source_target_pairs={{0,16},{16,0},{1,17},{17,1},{2,18},{18,2},{3,19},{19,3},{4,20},{20... | collective-permute-start | bytes 7077896 | tf_op jit(solution)/shard_map/ppermute | solution.py:55
  157.4 19.4 %collective-permute-start.27 = (bf16[256,1536]{1,0:T(8,128)(2,1)}, bf16[256,1536]{1,0:T(8,128)(2,1)}, u32[]{:S(2)}, u32[]{:S(2)}) collective-permute-start(bf16[256,1536]{1,0:T(8,128)(2,1)} %get-tuple-element.183.h0), channel_id=1, source_target_pairs={{0,2},{1,3},{2,0},{3,1},{4,6},{5,7},{6,4},{7,5},{8,10},{9,11},{10,... | collective-permute-start | bytes 2359304 | tf_op jit(solution)/shard_map/ppermute | solution.py:50
  265.3 151.2 %reduce-scatter.6.cloned.1.call-start = ((), (), s32[]{:S(2)}) async-start(), calls=%async_computation.7 | async-start | bytes 2211840 | tf_op jit(solution)/shard_map/reduce_scatter | solution.py:70
  268.7 31.1 %collective-permute-start.38 = (bf16[2,256,768]{2,1,0:T(8,128)(2,1)}, bf16[2,256,768]{2,1,0:T(8,128)(2,1)}, u32[]{:S(2)}, u32[]{:S(2)}) collective-permute-start(bf16[2,256,768]{2,1,0:T(8,128)(2,1)} %bitcast.19), channel_id=1, source_target_pairs={{0,2},{1,3},{2,0},{3,1},{4,6},{5,7},{6,4},{7,5},{8,10},{9,11},{10,... | collective-permute-start | bytes 2359304 | tf_op jit(solution)/shard_map/ppermute | solution.py:50
  269.8 30.0 %collective-permute-start.37 = (bf16[2,256,768]{2,1,0:T(8,128)(2,1)}, bf16[2,256,768]{2,1,0:T(8,128)(2,1)}, u32[]{:S(2)}, u32[]{:S(2)}) collective-permute-start(bf16[2,256,768]{2,1,0:T(8,128)(2,1)} %bitcast.18), channel_id=1, source_target_pairs={{0,1},{1,0},{2,3},{3,2},{4,5},{5,4},{6,7},{7,6},{8,9},{9,8},{10,11... | collective-permute-start | bytes 2359304 | tf_op jit(solution)/shard_map/ppermute | solution.py:50
  337.2 28.7 %collective-permute-start.48 = (bf16[2,2,96,1536]{3,2,1,0:T(8,128)(2,1)}, bf16[2,2,96,1536]{3,2,1,0:T(8,128)(2,1)}, u32[]{:S(2)}, u32[]{:S(2)}) collective-permute-start(bf16[2,2,96,1536]{3,2,1,0:T(8,128)(2,1)} %get-tuple-element.251), channel_id=1, source_target_pairs={{0,1},{1,0},{2,3},{3,2},{4,5},{5,4},{6,7},{7,6},{8,9},{9,8},{10,11... | collective-permute-start | bytes 3538952 | tf_op jit(solution)/shard_map/ppermute | solution.py:50
  338.0 28.4 %collective-permute-start.49 = (bf16[2,2,96,1536]{3,2,1,0:T(8,128)(2,1)}, bf16[2,2,96,1536]{3,2,1,0:T(8,128)(2,1)}, u32[]{:S(2)}, u32[]{:S(2)}) collective-permute-start(bf16[2,2,96,1536]{3,2,1,0:T(8,128)(2,1)} %get-tuple-element.252), channel_id=1, source_target_pairs={{0,2},{1,3},{2,0},{3,1},{4,6},{5,7},{6,4},{7,5},{8,10},{9,11},{10,... | collective-permute-start | bytes 3538952 | tf_op jit(solution)/shard_map/ppermute | solution.py:50
  367.1 83.0 %reduce-scatter.8.cloned.1.call-start = ((), (), s32[]{:S(2)}) async-start(), calls=%async_computation.8 | async-start | bytes 1720320 | tf_op jit(solution)/shard_map/reduce_scatter | solution.py:70
  370.7 27.5 %collective-permute-start.57 = (bf16[2,96,1536]{2,1,0:T(8,128)(2,1)S(1)}, bf16[2,96,1536]{2,1,0:T(8,128)(2,1)}, u32[]{:S(2)}, u32[]{:S(2)}) collective-permute-start(bf16[2,96,1536]{2,1,0:T(8,128)(2,1)S(1)} %fusion.11), channel_id=1, source_target_pairs={{0,2},{1,3},{2,0},{3,1},{4,6},{5,7},{6,4},{7,5},{8,10},{9,11},{10,... | collective-permute-start | bytes 1769480 | tf_op jit(solution)/shard_map/ppermute | solution.py:50
  382.4 22.1 %collective-permute-start.58 = (bf16[2,96,1536]{2,1,0:T(8,128)(2,1)}, bf16[2,96,1536]{2,1,0:T(8,128)(2,1)}, u32[]{:S(2)}, u32[]{:S(2)}) collective-permute-start(bf16[2,96,1536]{2,1,0:T(8,128)(2,1)} %fusion.12), channel_id=1, source_target_pairs={{0,1},{1,0},{2,3},{3,2},{4,5},{5,4},{6,7},{7,6},{8,9},{9,8},{10,11... | collective-permute-start | bytes 1769480 | tf_op jit(solution)/shard_map/ppermute | solution.py:50
  398.2 23.0 %collective-permute-start.63 = (bf16[96,4608]{1,0:T(8,128)(2,1)}, bf16[96,4608]{1,0:T(8,128)(2,1)}, u32[]{:S(2)}, u32[]{:S(2)}) collective-permute-start(bf16[96,4608]{1,0:T(8,128)(2,1)} %unshuffle.1), channel_id=1, source_target_pairs={{0,16},{16,0},{1,17},{17,1},{2,18},{18,2},{3,19},{19,3},{4,20},{20... | collective-permute-start | bytes 2654216 | tf_op jit(solution)/shard_map/ppermute | solution.py:55
  (120 other events, 1257.1 us)
Sparse Core Ops, SparseCore 0:
  10.2 34.3 all-gather.3
  46.2 48.0 all-gather.7
  96.4 68.8 all-gather.5
  265.5 67.0 reduce-scatter.3
  366.6 38.9 reduce-scatter.5
  417.9 32.1 reduce-scatter.7

commit v5 on v4

--- a/solution.py
+++ b/solution.py
@@ -878,16 +878,16 @@
     def first_step():
         return (
             product_tn(hidden, up_own).astype(bf16),
-            peer(product_tn(hidden, up_other).astype(bf16)),
+            product_tn(hidden, up_other).astype(bf16),
         )
 
     def second_step(down_mine, down_peer):
-        down_sum = (down_mine.astype(f32) + down_peer.astype(f32)).astype(bf16)
-        return partial, down_sum, attn_x, attn_y
-
-    grad_keyvals, (partial, down_sum, attn_x, attn_y) = halve_column(
+        return partial, down_mine, down_peer, attn_x, attn_y
+
+    grad_keyvals, (partial, down_mine, down_peer, attn_x, attn_y) = halve_column(
         grad_kv.reshape(lead, token_count, -1), first_step, second_step
     )
+    grad_keyvals, down_sum = tie(grad_keyvals, chip_sum(down_mine, down_peer))
     down_grad = scatter_column(down_sum)
     wide_grad = wide_grad.reshape(plane, my_rows, part)
     input_grad, last_own, last_other = input_backward(

time: 471 us -> 469 us (level)
  transfers between devices with their start and end apart: 71 -> 71, of which waited for: 30 -> 31; matrix products, arithmetic and copies ran while one was open for 21% -> 20% of each run, Pallas kernels for 16% -> 16%
where the time goes in v5:
time: 469 us; the launch traced here: 460 us
  waiting for transfers between devices  129 us (28%)
  Pallas kernels  111 us (24%)
  starting transfers between devices  58.8 us (13%)
  matrix products  41.7 us (9%)
  blocking collectives  38.5 us (8%)
  other arithmetic  33.7 us (7%)
  local copies, waits for them, and re-layouts  31.6 us (7%)
  between operations  15.5 us (3%)
    ppermute x52, waiting for transfers between devices, across(): return lax.ppermute(value, 'shard', [(i, i ^ mask) for i in range(count)])  106 us
    ppermute x52, starting transfers between devices, across(): return lax.ppermute(value, 'shard', [(i, i ^ mask) for i in range(count)])  56.4 us
    all_gather x2, blocking collectives, gather_column(): lax.all_gather(value, 'shard', axis=0, tiled=True, axis_index_groups=colu...  38.5 us
    pallas_call x1, Pallas kernels, feed_forward(): pl.pallas_call(feed_kernel, out_shape=(shape((count, width), bf16),) * 2...  37.7 us
    dot_general x8, matrix products, product_tn(): lax.dot_general(first_op, second_op, (((0,), (0,)), ((), ())), preferred_...  25.4 us
    pallas_call x1, Pallas kernels, on_device(): backward(info, queries, grad_mixed, logsum, *kv_blocks)  19.9 us
    reduce_scatter x3, waiting for transfers between devices, scatter_column(): lax.psum_scatter(value, 'shard', scatter_dimension=0, tiled=True, axis_in...  18 us
    pallas_call x1, Pallas kernels, on_device(): attended, logsum = forward(info, queries, *kv_blocks)  12.7 us
  transfers between devices with their start and end apart: 71, of which 31 were waited for; matrix products, arithmetic and copies ran while one was open for 20% of the time, Pallas kernels for 16%

profile of v5, /device:TPU:0, one launch (start us, length us, event | category | flops | bytes accessed | tf_op | source)
XLA Modules:
  0.0 460.2 jit_solution(17087869107154007041)
XLA Ops:
  16.1 15.7 %all_gather.15 = bf16[384,256]{1,0:T(8,128)(2,1)} all-gather(bf16[96,256]{1,0:T(8,128)(2,1)S(1)} %copy.39), channel_id=1, replica_groups={{0,4,8,12},{1,5,9,13},{2,6,10,14},{3,7,11,15},{16,20,24,28},{17,21,25,2..., dimensions={0}, use_global_device_ids=true | all-gather | bytes 245760 | tf_op jit(solution)/shard_map/all_gather | solution.py:64
  49.3 5.8 %collective-permute-done.8 = bf16[1,96,1152]{2,1,0:T(8,128)(2,1)S(1)} collective-permute-done((bf16[1,96,1152]{2,1,0:T(8,128)(2,1)S(1)}, bf16[1,96,1152]{2,1,0:T(8,128)(2,1)S(1)}, u32[]{:S(2)}, u32[]{:S(2)}) %collective-permute-start.8) | collective-permute-done | bytes 221216 | tf_op jit(solution)/shard_map/ppermute | solution.py:50
  69.2 22.8 %all_gather.17.k0 = bf16[1024,256]{1,0:T(8,128)(2,1)S(1)} all-gather(bf16[256,256]{1,0:T(8,128)(2,1)S(1)} %fusion.27), channel_id=1, replica_groups={{0,4,8,12},{1,5,9,13},{2,6,10,14},{3,7,11,15},{16,20,24,28},{17,21,25,2..., dimensions={0}, use_global_device_ids=true | all-gather | bytes 655360 | tf_op jit(solution)/shard_map/all_gather | solution.py:64
  100.9 13.1 %collective-permute-done.17.far_bottom = bf16[2,96,768]{2,1,0:T(8,128)(2,1)S(1)} collective-permute-done((bf16[2,96,768]{2,1,0:T(8,128)(2,1)S(1)}, bf16[2,96,768]{2,1,0:T(8,128)(2,1)S(1)}, u32[]{:S(2)}, u32[]{:S(2)}) %collective-permute-start.17) | collective-permute-done | bytes 294944 | tf_op jit(solution)/shard_map/ppermute | solution.py:50
  138.4 12.7 %attend_forward.1 = (bf16[256,1536]{1,0:T(8,128)(2,1)}, f32[4,768,1]{2,1,0:T(8,128)}) custom-call(s32[6]{0:T(128)} %pad_add_fusion.info, bf16[256,1536]{1,0:T(8,128)(2,1)} %fusion.q_ref, bf16[1024,256]{1,0:T(8,128)(2,1)} %copy-done.29, bf16[1024,256]{1,0:T(8,128)(2,1)} %copy-done.49, bf16[1024,256]{1,0:T(8,128)(2,1)} %copy-done.48, ...), custom_call_target="tpu_custom_call" | custom-call | flops 1811939328 | bytes 4194304 | tf_op jit(solution)/shard_map/attend_forward/pallas_call | solution.py:779
  151.2 6.1 %outproj_norm.1 = (f32[256,1536]{1,0:T(8,128)}, bf16[256,1536]{1,0:T(8,128)(2,1)}) custom-call(s32[1]{0:T(128)} %bitcast.core, bf16[256,1536]{1,0:T(8,128)(2,1)} %get-tuple-element.179.att, bf16[1536,768]{1,0:T(8,128)(2,1)} %bitcast.121, bf16[1536,768]{1,0:T(8,128)(2,1)} %collective-permute-done.25.other, bf16[256,1536]{1,0:T(8,128)(2,1)} %bitcast.125, ...), custom_call_target="tpu_custom_call" | custom-call | flops 1207959552 | bytes 8650752 | tf_op jit(solution)/shard_map/outproj_norm/pallas_call | solution.py:460
  160.2 16.6 %collective-permute-done.27.h2 = bf16[256,1536]{1,0:T(8,128)(2,1)} collective-permute-done((bf16[256,1536]{1,0:T(8,128)(2,1)}, bf16[256,1536]{1,0:T(8,128)(2,1)}, u32[]{:S(2)}, u32[]{:S(2)}) %collective-permute-start.27) | collective-permute-done | bytes 786464 | tf_op jit(solution)/shard_map/ppermute | solution.py:50
  182.8 8.4 %collective-permute-done.29.h4 = bf16[128,1536]{1,0:T(8,128)(2,1)S(1)} collective-permute-done((bf16[128,1536]{1,0:T(8,128)(2,1)S(1)}, bf16[128,1536]{1,0:T(8,128)(2,1)S(1)}, u32[]{:S(2)}, u32[]{:S(2)}) %collective-permute-start.29) | collective-permute-done | bytes 393248 | tf_op jit(solution)/shard_map/ppermute | solution.py:50
  194.0 37.7 %feed_forward.1 = (bf16[1024,1536]{1,0:T(8,128)(2,1)}, bf16[1024,1536]{1,0:T(8,128)(2,1)}, bf16[1024,1152]{1,0:T(8,128)(2,1)}, bf16[1024,1152]{1,0:T(8,128)(2,1)...) custom-call(s32[1]{0:T(128)} %bitcast.core, ...), custom_call_target="tpu_custom_call" | custom-call | flops 18119393280 | bytes 28311552 | tf_op jit(solution)/shard_map/feed_forward/pallas_call | solution.py:547
  233.0 7.0 %convolution_convert_fusion.1 = bf16[1536,1152]{1,0:T(8,128)(2,1)S(1)} fusion(bf16[1024,1536]{1,0:T(8,128)(2,1)} %get-tuple-element.200, bf16[1024,1152]{1,0:T(8,128)(2,1)} %get-tuple-element.201), kind=kOutput, calls=%fused_computation.1 | convolution fusion | flops 3625648128 | bytes 9043968 | tf_op jit(solution)/shard_map/dot_general | solution.py:28
  240.1 4.6 convolution_convert_fusion
  244.7 5.6 %collective-permute-done.32.x_got = bf16[2,256,768]{2,1,0:T(8,128)(2,1)S(1)} collective-permute-done((bf16[2,256,768]{2,1,0:T(8,128)(2,1)}, bf16[2,256,768]{2,1,0:T(8,128)(2,1)S(1)}, u32[]{:S(2)}, u32[]{:S(2)}) %collective-permute-start.32) | collective-permute-done | bytes 786464 | tf_op jit(solution)/shard_map/ppermute | solution.py:50
  271.0 8.6 %norm_two_backward.1 = (f32[256,1536]{1,0:T(8,128)}, bf16[256,1536]{1,0:T(8,128)(2,1)}, bf16[256,1536]{1,0:T(8,128)(2,1)}, f32[1,1536]{1,0:T(1,128)}) custom-call(s32[1]{0:T(128)} %bitcast.core, bf16[2,256,768]{2,1,0:T(8,128)(2,1)} %get-tuple-element.197.x_keep, bf16[2,256,768]{2,1,0:T(8,128)(2,1)} %copy-done.20, ...), custom_call_target="tpu_custom_call" | custom-call | flops 1207959552 | bytes 12582912 | tf_op jit(solution)/shard_map/norm_two_backward/pallas_call | solution.py:593
  279.7 19.9 %attend_backward.1 = (bf16[256,1536]{1,0:T(8,128)(2,1)}, bf16[2,1024,128]{2,1,0:T(8,128)(2,1)}, bf16[2,1024,128]{2,1,0:T(8,128)(2,1)}, bf16[2,1024,128]{2,1,0:T(8,128)(2,1)}, bf16[2,1024,128]{2,1,0:T(8,128)(2,1)}) custom-call(s32[6]{0:T(128)} %pad_add_fusion.info, bf16[256,1536]{1,0:T(8,128)(2,1)} %fusion.q_ref, bf16[256,1536]{1,0:T(8,128)(2,1)} %get-tuple-element.218.g_ref, ...), custom_call_target="tpu_custom_call" | custom-call | flops 4529848320 | bytes 8388608 | tf_op jit(solution)/shard_map/attend_backward/pallas_call | solution.py:839
  308.5 7.6 %collective-permute-done.39 = bf16[2,1024,128]{2,1,0:T(8,128)(2,1)S(1)} collective-permute-done((bf16[2,1024,128]{2,1,0:T(8,128)(2,1)S(1)}, bf16[2,1024,128]{2,1,0:T(8,128)(2,1)S(1)}, u32[]{:S(2)}, u32[]{:S(2)}) %collective-permute-start.39) | collective-permute-done | bytes 524320 | tf_op jit(solution)/shard_map/ppermute | solution.py:50
  322.8 7.1 %split_rows.2 = (bf16[2,2,96,1536]{3,2,1,0:T(8,128)(2,1)}, bf16[2,2,96,1536]{3,2,1,0:T(8,128)(2,1)}, bf16[2,2,96,1536]{3,2,1,0:T(8,128)(2,1)}, bf16[2,2,96,1536]{3,2,1,0:T(8,128)(2,1)}) custom-call(s32[2]{0:T(128)} %pad_add_fusion.1.place, bf16[4,4,96,768]{3,2,1,0:T(8,128)(2,1)} %bitcast.124, bf16[4,4,96,768]{3,2,1,0:T(8,128)(2,1)} %bitcast.140, ...), custom_call_target="tpu_custom_call" | custom-call | flops 2359296 | bytes 14155776 | tf_op jit(solution)/shard_map/split_rows/pallas_call | solution.py:209
  337.6 4.3 convolution_convert_fusion.3
  341.9 6.6 %collective-permute-done.45 = bf16[2,256,256]{2,1,0:T(8,128)(2,1)S(1)} collective-permute-done((bf16[2,256,256]{2,1,0:T(8,128)(2,1)S(1)}, bf16[2,256,256]{2,1,0:T(8,128)(2,1)S(1)}, u32[]{:S(2)}, u32[]{:S(2)}) %collective-permute-start.45) | collective-permute-done | bytes 262176 | tf_op jit(solution)/shard_map/ppermute | solution.py:50
  350.7 6.0 %collective-permute-done.47 = bf16[2,2,96,1536]{3,2,1,0:T(8,128)(2,1)} collective-permute-done((bf16[2,2,96,1536]{3,2,1,0:T(8,128)(2,1)}, bf16[2,2,96,1536]{3,2,1,0:T(8,128)(2,1)}, u32[]{:S(2)}, u32[]{:S(2)}) %collective-permute-start.47) | collective-permute-done | bytes 1179680 | tf_op jit(solution)/shard_map/ppermute | solution.py:50
  373.1 5.6 %input_backward.1 = (bf16[256,1536]{1,0:T(8,128)(2,1)}, bf16[1536,256]{1,0:T(8,128)(2,1)}, bf16[1536,256]{1,0:T(8,128)(2,1)}) custom-call(s32[1]{0:T(128)} %bitcast.core, f32[256,1536]{1,0:T(8,128)} %convolution_add_fusion.partial, bf16[256,256]{1,0:T(8,128)(2,1)} %fusion.30.dkv, bf16[1536,128]{1,0:T(8,128)(2,1)} %slice.233.kv_own, ...), custom_call_target="tpu_custom_call" | custom-call | flops 402653184 | bytes 6291456 | tf_op jit(solution)/shard_map/input_backward/pallas_call | solution.py:645
  381.7 11.7 %collective-permute-done.61.p2 = bf16[96,1152]{1,0:T(8,128)(2,1)S(1)} collective-permute-done((bf16[96,1152]{1,0:T(8,128)(2,1)S(1)}, bf16[96,1152]{1,0:T(8,128)(2,1)S(1)}, u32[]{:S(2)}, u32[]{:S(2)}) %collective-permute-start.61) | collective-permute-done | bytes 221216 | tf_op jit(solution)/shard_map/ppermute | solution.py:50
  404.1 4.1 collective-permute-done.51
  423.2 3.8 collective-permute-done.55
  430.8 18.0 %reduce-scatter.8.cloned.1.call-done = bf16[96,1792]{1,0:T(8,128)(2,1)} async-done(((bf16[384,1792]{1,0:T(8,128)(2,1)}), bf16[96,1792]{1,0:T(8,128)(2,1)}) %reduce-scatter.8.cloned.1.call-update) | async-done | bytes 344080 | tf_op jit(solution)/shard_map/reduce_scatter | solution.py:70
  (390 shorter events, 185.4 us)
Async XLA Ops:
  7.2 51.7 %all-gather.4.cloned.1.call-start = ((), (), s32[]{:S(2)}) async-start(), calls=%async_computation.3 | async-start | bytes 1474560 | tf_op jit(solution)/shard_map/all_gather | solution.py:64
  10.1 150.1 %all-gather.8.cloned.1.call-start = ((), (), s32[]{:S(2)}) async-start(), calls=%async_computation.5 | async-start | bytes 2211840 | tf_op jit(solution)/shard_map/all_gather | solution.py:64
  10.1 21.8 %collective-permute-start.1 = (bf16[256,1536]{1,0:T(8,128)(2,1)}, bf16[256,1536]{1,0:T(8,128)(2,1)}, u32[]{:S(2)}, u32[]{:S(2)}) collective-permute-start(bf16[256,1536]{1,0:T(8,128)(2,1)} %bitcast.144), channel_id=1, source_target_pairs={{0,2},{1,3},{2,0},{3,1},{4,6},{5,7},{6,4},{7,5},{8,10},{9,11},{10,... | collective-permute-start | bytes 2359304 | tf_op jit(solution)/shard_map/ppermute | solution.py:50
  15.5 162.1 %all-gather.6.cloned.1.call-start = ((), (), s32[]{:S(2)}) async-start(), calls=%async_computation.4 | async-start | bytes 4423680 | tf_op jit(solution)/shard_map/all_gather | solution.py:64
  61.1 30.9 %collective-permute-start.11 = (bf16[4,96,768]{2,1,0:T(8,128)(2,1)}, bf16[4,96,768]{2,1,0:T(8,128)(2,1)}, u32[]{:S(2)}, u32[]{:S(2)}) collective-permute-start(bf16[4,96,768]{2,1,0:T(8,128)(2,1)} %bitcast.11.own), channel_id=1, source_target_pairs={{0,2},{1,3},{2,0},{3,1},{4,6},{5,7},{6,4},{7,5},{8,10},{9,11},{10,... | collective-permute-start | bytes 1769480 | tf_op jit(solution)/shard_map/ppermute | solution.py:50
  61.7 30.3 %collective-permute-start.10 = (bf16[4,96,768]{2,1,0:T(8,128)(2,1)}, bf16[4,96,768]{2,1,0:T(8,128)(2,1)}, u32[]{:S(2)}, u32[]{:S(2)}) collective-permute-start(bf16[4,96,768]{2,1,0:T(8,128)(2,1)} %bitcast.11.own), channel_id=1, source_target_pairs={{0,1},{1,0},{2,3},{3,2},{4,5},{5,4},{6,7},{7,6},{8,9},{9,8},{10,11... | collective-permute-start | bytes 1769480 | tf_op jit(solution)/shard_map/ppermute | solution.py:50
  62.3 29.7 %collective-permute-start.13 = (bf16[4,96,768]{2,1,0:T(8,128)(2,1)S(1)}, bf16[4,96,768]{2,1,0:T(8,128)(2,1)}, u32[]{:S(2)}, u32[]{:S(2)}) collective-permute-start(bf16[4,96,768]{2,1,0:T(8,128)(2,1)S(1)} %bitcast.137), channel_id=1, source_target_pairs={{0,2},{1,3},{2,0},{3,1},{4,6},{5,7},{6,4},{7,5},{8,10},{9,11},{10,... | collective-permute-start | bytes 1769480 | tf_op jit(solution)/shard_map/ppermute | solution.py:50
  63.7 28.4 %collective-permute-start.12 = (bf16[4,96,768]{2,1,0:T(8,128)(2,1)S(1)}, bf16[4,96,768]{2,1,0:T(8,128)(2,1)}, u32[]{:S(2)}, u32[]{:S(2)}) collective-permute-start(bf16[4,96,768]{2,1,0:T(8,128)(2,1)S(1)} %bitcast.138), channel_id=1, source_target_pairs={{0,1},{1,0},{2,3},{3,2},{4,5},{5,4},{6,7},{7,6},{8,9},{9,8},{10,11... | collective-permute-start | bytes 1769480 | tf_op jit(solution)/shard_map/ppermute | solution.py:50
  69.2 266.4 %reduce-scatter.4.cloned.1.call-start = ((), (), s32[]{:S(2)}) async-start(), calls=%async_computation.6 | async-start | bytes 4423680 | tf_op jit(solution)/shard_map/reduce_scatter | solution.py:70
  92.1 23.3 %collective-permute-start.15 = (bf16[1024,256]{1,0:T(8,128)(2,1)S(1)}, bf16[1024,256]{1,0:T(8,128)(2,1)S(1)}, u32[]{:S(2)}, u32[]{:S(2)}) collective-permute-start(bf16[1024,256]{1,0:T(8,128)(2,1)S(1)} %all_gather.17.k0), channel_id=1, source_target_pairs={{0,2},{1,3},{2,0},{3,1},{4,6},{5,7},{6,4},{7,5},{8,10},{9,11},{10,... | collective-permute-start | bytes 1572872 | tf_op jit(solution)/shard_map/ppermute | solution.py:50
  92.8 22.5 %collective-permute-start.14 = (bf16[1024,256]{1,0:T(8,128)(2,1)S(1)}, bf16[1024,256]{1,0:T(8,128)(2,1)S(1)}, u32[]{:S(2)}, u32[]{:S(2)}) collective-permute-start(bf16[1024,256]{1,0:T(8,128)(2,1)S(1)} %all_gather.17.k0), channel_id=1, source_target_pairs={{0,1},{1,0},{2,3},{3,2},{4,5},{5,4},{6,7},{7,6},{8,9},{9,8},{10,11... | collective-permute-start | bytes 1572872 | tf_op jit(solution)/shard_map/ppermute | solution.py:50
  94.4 19.6 %collective-permute-start.17 = (bf16[2,96,768]{2,1,0:T(8,128)(2,1)S(1)}, bf16[2,96,768]{2,1,0:T(8,128)(2,1)S(1)}, u32[]{:S(2)}, u32[]{:S(2)}) collective-permute-start(bf16[2,96,768]{2,1,0:T(8,128)(2,1)S(1)} %slice.238), channel_id=1, source_target_pairs={{0,1},{1,0},{2,3},{3,2},{4,5},{5,4},{6,7},{7,6},{8,9},{9,8},{10,11... | collective-permute-start | bytes 884744 | tf_op jit(solution)/shard_map/ppermute | solution.py:50
  100.2 20.1 %collective-permute-start.21 = (bf16[2,96,768]{2,1,0:T(8,128)(2,1)S(1)}, bf16[2,96,768]{2,1,0:T(8,128)(2,1)S(1)}, u32[]{:S(2)}, u32[]{:S(2)}) collective-permute-start(bf16[2,96,768]{2,1,0:T(8,128)(2,1)S(1)} %slice.242), channel_id=1, source_target_pairs={{0,1},{1,0},{2,3},{3,2},{4,5},{5,4},{6,7},{7,6},{8,9},{9,8},{10,11... | collective-permute-start | bytes 884744 | tf_op jit(solution)/shard_map/ppermute | solution.py:50
  128.0 23.2 %collective-permute-start.25 = (bf16[1536,768]{1,0:T(8,128)(2,1)}, bf16[1536,768]{1,0:T(8,128)(2,1)}, u32[]{:S(2)}, u32[]{:S(2)}) collective-permute-start(bf16[1536,768]{1,0:T(8,128)(2,1)} %bitcast.120), channel_id=1, source_target_pairs={{0,16},{16,0},{1,17},{17,1},{2,18},{18,2},{3,19},{19,3},{4,20},{20... | collective-permute-start | bytes 7077896 | tf_op jit(solution)/shard_map/ppermute | solution.py:55
  265.1 149.7 %reduce-scatter.6.cloned.1.call-start = ((), (), s32[]{:S(2)}) async-start(), calls=%async_computation.7 | async-start | bytes 2211840 | tf_op jit(solution)/shard_map/reduce_scatter | solution.py:70
  268.6 30.9 %collective-permute-start.38 = (bf16[2,256,768]{2,1,0:T(8,128)(2,1)}, bf16[2,256,768]{2,1,0:T(8,128)(2,1)}, u32[]{:S(2)}, u32[]{:S(2)}) collective-permute-start(bf16[2,256,768]{2,1,0:T(8,128)(2,1)} %bitcast.19), channel_id=1, source_target_pairs={{0,2},{1,3},{2,0},{3,1},{4,6},{5,7},{6,4},{7,5},{8,10},{9,11},{10,... | collective-permute-start | bytes 2359304 | tf_op jit(solution)/shard_map/ppermute | solution.py:50
  269.7 29.8 %collective-permute-start.37 = (bf16[2,256,768]{2,1,0:T(8,128)(2,1)}, bf16[2,256,768]{2,1,0:T(8,128)(2,1)}, u32[]{:S(2)}, u32[]{:S(2)}) collective-permute-start(bf16[2,256,768]{2,1,0:T(8,128)(2,1)} %bitcast.18), channel_id=1, source_target_pairs={{0,1},{1,0},{2,3},{3,2},{4,5},{5,4},{6,7},{7,6},{8,9},{9,8},{10,11... | collective-permute-start | bytes 2359304 | tf_op jit(solution)/shard_map/ppermute | solution.py:50
  329.9 26.9 %collective-permute-start.47 = (bf16[2,2,96,1536]{3,2,1,0:T(8,128)(2,1)}, bf16[2,2,96,1536]{3,2,1,0:T(8,128)(2,1)}, u32[]{:S(2)}, u32[]{:S(2)}) collective-permute-start(bf16[2,2,96,1536]{3,2,1,0:T(8,128)(2,1)} %get-tuple-element.254), channel_id=1, source_target_pairs={{0,1},{1,0},{2,3},{3,2},{4,5},{5,4},{6,7},{7,6},{8,9},{9,8},{10,11... | collective-permute-start | bytes 3538952 | tf_op jit(solution)/shard_map/ppermute | solution.py:50
  330.8 26.7 %collective-permute-start.48 = (bf16[2,2,96,1536]{3,2,1,0:T(8,128)(2,1)}, bf16[2,2,96,1536]{3,2,1,0:T(8,128)(2,1)}, u32[]{:S(2)}, u32[]{:S(2)}) collective-permute-start(bf16[2,2,96,1536]{3,2,1,0:T(8,128)(2,1)} %get-tuple-element.255), channel_id=1, source_target_pairs={{0,2},{1,3},{2,0},{3,1},{4,6},{5,7},{6,4},{7,5},{8,10},{9,11},{10,... | collective-permute-start | bytes 3538952 | tf_op jit(solution)/shard_map/ppermute | solution.py:50
  362.9 85.8 %reduce-scatter.8.cloned.1.call-start = ((), (), s32[]{:S(2)}) async-start(), calls=%async_computation.8 | async-start | bytes 1720320 | tf_op jit(solution)/shard_map/reduce_scatter | solution.py:70
  368.3 28.4 %collective-permute-start.57 = (bf16[2,96,1536]{2,1,0:T(8,128)(2,1)}, bf16[2,96,1536]{2,1,0:T(8,128)(2,1)}, u32[]{:S(2)}, u32[]{:S(2)}) collective-permute-start(bf16[2,96,1536]{2,1,0:T(8,128)(2,1)} %fusion.11), channel_id=1, source_target_pairs={{0,2},{1,3},{2,0},{3,1},{4,6},{5,7},{6,4},{7,5},{8,10},{9,11},{10,... | collective-permute-start | bytes 1769480 | tf_op jit(solution)/shard_map/ppermute | solution.py:50
  378.7 19.6 %collective-permute-start.50 = (bf16[1536,256]{1,0:T(8,128)(2,1)}, bf16[1536,256]{1,0:T(8,128)(2,1)}, u32[]{:S(2)}, u32[]{:S(2)}) collective-permute-start(bf16[1536,256]{1,0:T(8,128)(2,1)} %get-tuple-element.264), channel_id=1, source_target_pairs={{0,16},{16,0},{1,17},{17,1},{2,18},{18,2},{3,19},{19,3},{4,20},{20... | collective-permute-start | bytes 2359304 | tf_op jit(solution)/shard_map/ppermute | solution.py:55
  380.8 21.8 %collective-permute-start.58 = (bf16[2,96,1536]{2,1,0:T(8,128)(2,1)}, bf16[2,96,1536]{2,1,0:T(8,128)(2,1)}, u32[]{:S(2)}, u32[]{:S(2)}) collective-permute-start(bf16[2,96,1536]{2,1,0:T(8,128)(2,1)} %fusion.12), channel_id=1, source_target_pairs={{0,1},{1,0},{2,3},{3,2},{4,5},{5,4},{6,7},{7,6},{8,9},{9,8},{10,11... | collective-permute-start | bytes 1769480 | tf_op jit(solution)/shard_map/ppermute | solution.py:50
  396.8 23.0 %collective-permute-start.63 = (bf16[96,4608]{1,0:T(8,128)(2,1)}, bf16[96,4608]{1,0:T(8,128)(2,1)}, u32[]{:S(2)}, u32[]{:S(2)}) collective-permute-start(bf16[96,4608]{1,0:T(8,128)(2,1)} %unshuffle.1), channel_id=1, source_target_pairs={{0,16},{16,0},{1,17},{17,1},{2,18},{18,2},{3,19},{19,3},{4,20},{20... | collective-permute-start | bytes 2654216 | tf_op jit(solution)/shard_map/ppermute | solution.py:55
  (119 other events, 1255.7 us)
Sparse Core Ops, SparseCore 0:
  10.2 34.3 all-gather.3
  46.2 48.0 all-gather.7
  96.4 68.8 all-gather.5
  265.2 67.0 reduce-scatter.3
  363.0 38.5 reduce-scatter.5
  416.1 32.5 reduce-scatter.7
